TPU v7x, 32 devices: a whole 2x2x4 slice. The times are simulated.
32 devices in a mesh: ta: 2 (over x), tp: 16 (over z, y, core).
Axes of the slice: x: 2, y: 2, z: 4, core: 2. Of those that a mesh axis runs over, the one named last changes fastest.
Arguments:
- green: float32 [2, 2, 16, 16, 512], P(None, None, 'tp', None, 'ta'), may hold values from -5 to 5
- hamiltonian: float32 [32, 32], replicated, may hold values from -1 to 1
- interaction: float32 [32, 32], replicated, may hold values from 0.4 to 1.2
Outputs:
- green_next: float32 [2, 2, 16, 16, 512], P(None, None, 'tp', None, 'ta')
All inputs are finite; a program needn't handle non-finite values.
Results may differ from a plain program's by a relative error of at most 0.0091.
Values may be sent and summed in bfloat16 or wider, within the bound.
No kernel may reach another device: no remote copies, remote signals or barrier semaphores. Data moves between devices by JAX's collectives and lax.ppermute only.
A program may use at most 64 MiB of HBM per device.

v0:
```python
import math

import jax
import jax.numpy as jnp
from jax import lax
from jax.experimental import pallas as pl
from jax.experimental.pallas import tpu as pltpu
from jax.sharding import PartitionSpec as P

NO = 32
ITERS = 2


highest = lax.Precision.HIGHEST


def shifted(block, axis, distance):
    devices = range(lax.axis_size(axis))
    route = [(i - distance, i) for i in devices if i - distance in devices]
    return lax.ppermute(block, axis, route)


def half_dot(left_side, right_side):
    return jnp.dot(left_side, right_side, preferred_element_type=jnp.float32)


def accumulate(left_side, right_side):
    product_real = half_dot(left_side[0], right_side[0]) - half_dot(left_side[1], right_side[1])
    product_imag = half_dot(left_side[0], right_side[1]) + half_dot(left_side[1], right_side[0])
    return (product_real, product_imag)


def self_energy(values, mirror_part, weights):
    real_square = values[0] * values[0] - values[1] * values[1]
    imag_square = 2.0 * values[0] * values[1]
    sigma_real = weights * (real_square * mirror_part[0] - imag_square * mirror_part[1])
    sigma_imag = weights * (real_square * mirror_part[1] + imag_square * mirror_part[0])
    return jnp.stack([sigma_real, sigma_imag])


def windowed(green, hamiltonian, interaction):
    tp_count = lax.axis_size("tp")
    ta_place = lax.axis_index("ta")
    tp_place = lax.axis_index("tp")
    groups = green.shape[1]
    stripe = green.shape[3]
    block_rows = green.shape[4]
    columns = groups * stripe
    factor = 1.0 / math.sqrt(2 * block_rows)
    current = green[:, :, 0].reshape(2, columns, block_rows)
    squared = interaction * interaction
    column_global = (
        jnp.arange(groups, dtype=jnp.int32)[:, None] * tp_count + tp_place
    ) * stripe + jnp.arange(stripe, dtype=jnp.int32)[None, :]
    column_orbital = (column_global % NO).reshape(columns)
    onehot = (column_orbital[:, None] == jnp.arange(NO, dtype=jnp.int32)[None, :]).astype(
        jnp.float32
    )
    lookup_table = jnp.dot(onehot, squared.T, precision=highest)
    coupling = jnp.tile(lookup_table, (1, block_rows // NO))
    row_time = jnp.arange(block_rows, dtype=jnp.int32) // NO
    column_time = (tp_place * stripe + jnp.arange(stripe, dtype=jnp.int32)) // NO
    is_later = column_time[:, None] > row_time[None, :]
    block_width = math.gcd(block_rows, 128)
    blocked = jnp.kron(jnp.eye(block_width // NO, dtype=jnp.float32), hamiltonian.T)
    zero_half = jnp.zeros((), jnp.bfloat16)
    for _ in range(ITERS):
        rounded = current.astype(jnp.bfloat16)
        outgoing = rounded.reshape(2, groups, stripe, tp_count, stripe)
        previous = shifted(rounded, "ta", 1)
        earliest = shifted(rounded, "ta", 2)
        hamilton_term = jnp.dot(
            current.reshape(-1, block_width), blocked, precision=highest
        ).reshape(2, columns, block_rows)
        selected = []
        nearby = jnp.stack(
            [
                lax.dynamic_index_in_dim(
                    outgoing, jnp.minimum(ta_place + step_ahead, groups - 1), 1, keepdims=False
                )
                for step_ahead in range(3)
            ],
            1,
        )
        spread = lax.all_to_all(nearby, "tp", split_axis=3, concat_axis=3, tiled=True)
        from_one = shifted(spread[:, 1], "ta", 1)
        from_two = shifted(spread[:, 2], "ta", 2)
        received = (from_two, from_one, spread[:, 0])
        by_current = current.reshape(2, groups, stripe, block_rows)
        for window_index in range(3):
            group_pick = jnp.maximum(ta_place - 2 + window_index, 0)
            own_part = lax.dynamic_index_in_dim(by_current, group_pick, 1, keepdims=False)
            flipped = (
                jnp.transpose(received[window_index], (0, 3, 2, 1))
                .reshape(2, stripe, block_rows)
                .astype(jnp.float32)
            )
            selected.append(self_energy(own_part, flipped, coupling[:stripe]))
        oldest = jnp.where(is_later[None], selected[0], 0.0)
        middle = selected[1]
        newest = jnp.where(is_later[None], 0.0, selected[2])
        sending = jnp.stack([oldest + newest, middle], 1).astype(jnp.bfloat16)[:, :, None]
        portion = lax.all_gather(sending, "tp", axis=2, tiled=True)
        row_count = portion.shape[2] * stripe
        arriving_time = jnp.arange(row_count, dtype=jnp.int32) // NO
        later_here = (arriving_time[:, None] > row_time[None, :])[None]
        merged = portion[:, 0].reshape(2, row_count, block_rows)
        recent = portion[:, 1].reshape(2, row_count, block_rows)
        right_side = jnp.concatenate(
            [
                jnp.where(later_here, merged, zero_half),
                recent,
                jnp.where(later_here, zero_half, merged),
            ],
            1,
        )
        memory = accumulate(
            jnp.concatenate([source for source in (earliest, previous, rounded)], 2), right_side
        )
        next_real = current[0] + 0.5 * (hamilton_term[1] + factor * memory[1])
        next_imag = current[1] - 0.5 * (hamilton_term[0] + factor * memory[0])
        current = jnp.stack([next_real, next_imag])
    return current.reshape(2, groups, 1, stripe, block_rows)


def exchange_masks(tp_count):
    bits = [1 << bit for bit in reversed(range(1, tp_count.bit_length() - 1))]
    middle, low, ta_bit = bits[1:-1], bits[-1:], [tp_count]
    even, odd = ta_bit + middle + low, low + middle + ta_bit
    return bits[0], (even, odd), ta_bit + low + middle


def offsets_of(masks):
    offsets = [0]
    for mask in masks:
        offsets = offsets + [known ^ mask for known in offsets]
    return offsets


def bf16_dot(left_side, right_side):
    return lax.dot_general(
        left_side, right_side, (((1,), (0,)), ((), ())), preferred_element_type=jnp.float32
    )


def halves(values):
    high = values.astype(jnp.bfloat16)
    return high, (values - high.astype(jnp.float32)).astype(jnp.bfloat16)


def window_of(values, mirror, weights, first_time):
    rows, width = values[0].shape
    real_square = values[0] * values[0] - values[1] * values[1]
    imag_square = 2.0 * values[0] * values[1]
    real = real_square * mirror[0] - imag_square * mirror[1]
    imag = real_square * mirror[1] + imag_square * mirror[0]
    source_time = lax.broadcasted_iota(jnp.int32, (rows, width), 0) // NO
    target_time = lax.broadcasted_iota(jnp.int32, (rows, width), 1) // NO + first_time
    inside = source_time <= target_time

    def weighted(part):
        part = (part.reshape(rows // NO, NO, width) * weights[None]).reshape(rows, width)
        return jnp.where(inside, part, 0.0).astype(jnp.bfloat16)

    return weighted(real), weighted(imag)


def mirrored(rounded):
    return [jnp.transpose(part.astype(jnp.float32)) for part in rounded]


def products(left_side, right_side):
    real = bf16_dot(left_side[0], right_side[0]) - bf16_dot(left_side[1], right_side[1])
    imag = bf16_dot(left_side[0], right_side[1]) + bf16_dot(left_side[1], right_side[0])
    return real, imag


def tables_of(hamiltonian, interaction, block_rows):
    def repeated(tile):
        return jnp.concatenate([tile] * (block_rows // NO), axis=1)

    weights = repeated(jnp.transpose(interaction[...] * interaction[...]))
    table = jnp.concatenate([repeated(jnp.transpose(hamiltonian[...]))] * (block_rows // NO))
    same_time = (
        lax.broadcasted_iota(jnp.int32, table.shape, 0) // NO
        == lax.broadcasted_iota(jnp.int32, table.shape, 1) // NO
    )
    return weights, halves(jnp.where(same_time, table, 0.0))


def turned_by(table, high, low=None):
    result = bf16_dot(high, table[0]) + bf16_dot(high, table[1])
    return result if low is None else result + bf16_dot(low, table[0])


def started(values, turned):
    return values[0] + 0.5 * turned[1], values[1] - 0.5 * turned[0]


def rows_of(pieces):
    return pieces.reshape(pieces.shape[0] * pieces.shape[1], pieces.shape[2])


def whole(source, block):
    tp_count, stripe, block_rows = source.shape[1] // 2, source.shape[2], source.shape[3]
    return [
        source[part, block * tp_count : (block + 1) * tp_count].reshape(
            tp_count * stripe, block_rows
        )
        for part in range(2)
    ]


def put(device, targets, results, index, stripe):
    for target, result in zip(targets, results):
        for part in range(2):
            target[part, device] = result[part][index * stripe : (index + 1) * stripe]


def take_first(sources, late, me, offsets, stripe, table, targets):
    count = len(offsets[0]) // 2
    for flip in range(2):
        values = [rows_of(sources[flip][:, part]) for part in range(2)]
        split = [halves(part) for part in values]
        base = started(values, [turned_by(table, high, low) for high, low in split])
        highs = [high for high, _ in split]
        for index in range(count):
            place = late * count + index
            mask = jnp.where(me % 2 == flip, offsets[0][place], offsets[1][place])
            put(me ^ (flip ^ mask), targets, (values, highs, base), index, stripe)


def take_second(sources, late, me, offsets, tp_count, stripe, table, targets):
    count = len(offsets) // 2
    for flip in range(2):
        for plane in range(2):
            highs = [rows_of(sources[flip][:, plane, part]) for part in range(2)]
            values = [high.astype(jnp.float32) for high in highs]
            if plane == 0:
                lows = [rows_of(sources[flip][:, 2, part]) for part in range(2)]
                values = [values[part] + lows[part].astype(jnp.float32) for part in range(2)]
                turned = [turned_by(table, highs[part], lows[part]) for part in range(2)]
            else:
                turned = [turned_by(table, high) for high in highs]
            base = started(values, turned)
            for index in range(count):
                device = me ^ (flip ^ offsets[late * count + index] ^ (plane * tp_count))
                put(device, targets, (values, highs, base), index, stripe)


def own_place(tp_count):
    return lax.axis_index("ta") * tp_count + lax.axis_index("tp")


def kept_shapes(tp_count, stripe, block_rows):
    pieces = (2, 2 * tp_count, stripe, block_rows)
    return [jax.ShapeDtypeStruct(pieces, each) for each in (jnp.float32, jnp.bfloat16, jnp.float32)]


def in_vmem(count):
    return [pl.BlockSpec(memory_space=pltpu.VMEM)] * count


def early_stage(masks, tp_count, stripe, block_rows, factor):
    offsets = [offsets_of(each) for each in masks]

    def kernel(*refs):
        hamiltonian, interaction, weights_out, table_out = refs[2:4] + refs[7:]
        me = own_place(tp_count)
        weights, table = tables_of(hamiltonian, interaction, block_rows)
        weights_out[...] = weights
        table_out[0] = table[0]
        table_out[1] = table[1]
        take_first(refs[:2], 0, me, offsets, stripe, table, refs[4:7])

    shapes = kept_shapes(tp_count, stripe, block_rows)
    tables = [
        jax.ShapeDtypeStruct((NO, block_rows), jnp.float32),
        jax.ShapeDtypeStruct((2, block_rows, block_rows), jnp.bfloat16),
    ]
    return pl.pallas_call(
        kernel,
        out_shape=shapes + tables,
        in_specs=in_vmem(4),
        out_specs=in_vmem(5),
        compiler_params=pltpu.CompilerParams(vmem_limit_bytes=16 << 20),
        name="early_stage",
    )


def first_stage(masks, tp_count, stripe, block_rows, factor):
    offsets = [offsets_of(each) for each in masks]
    scale = 0.5 * factor

    def kernel(*refs):
        weights, table = refs[2], (refs[3][0], refs[3][1])
        targets, window = refs[7:10], refs[10]
        take_first(refs[:2], 1, own_place(tp_count), offsets, stripe, table, targets)
        values, highs, bases = targets
        high = whole(highs, 0)
        made = window_of(whole(values, 0), mirrored(high), weights[...], 0)
        memory = products(high, made)
        window[0] = made[0]
        window[1] = made[1]
        half = (tp_count, stripe, block_rows)
        bases[0, :tp_count] = bases[0, :tp_count] + scale * memory[1].reshape(half)
        bases[1, :tp_count] = bases[1, :tp_count] - scale * memory[0].reshape(half)

    square = jax.ShapeDtypeStruct((2, block_rows, block_rows), jnp.bfloat16)
    return pl.pallas_call(
        kernel,
        out_shape=kept_shapes(tp_count, stripe, block_rows) + [square],
        in_specs=in_vmem(7),
        out_specs=in_vmem(4),
        input_output_aliases={4: 0, 5: 1, 6: 2},
        compiler_params=pltpu.CompilerParams(vmem_limit_bytes=16 << 20),
        name="first_stage",
    )


def second_stage(masks, tp_count, stripe, block_rows, factor):
    offsets = offsets_of(masks)
    order_size = 2 * block_rows
    scale = 0.5 * factor

    def kernel(*refs):
        weights, table = refs[4][...], (refs[5][0], refs[5][1])
        values, lows, bases, window = refs[6:10]
        out, targets, nexts, low_next = refs[10], refs[11:14], refs[14], refs[15]
        ta_place = lax.axis_index("ta")
        tp_place = lax.axis_index("tp")
        me = own_place(tp_count)
        for late in range(2):
            sources = refs[late:4:2]
            take_second(sources, late, me, offsets, tp_count, stripe, table, targets)
        second_values, second_highs, second_bases = targets
        high = [whole(second_highs, block) for block in range(2)]

        def stored(block, group, real, imag):
            for part, result in ((0, real), (1, imag)):
                nexts[part, block, group] = result
                low_next[part, group, :, block * block_rows : (block + 1) * block_rows] = (
                    result.astype(jnp.bfloat16)
                )

        stored(0, 0, *whole(bases, 0))
        memory = products(high[0], (window[0], window[1]))
        base = whole(second_bases, 0)
        stored(0, 1, base[0] + scale * memory[1], base[1] - scale * memory[0])
        later = [
            window_of(whole(values, 1), mirrored(high[0]), weights, block_rows // NO),
            window_of(whole(second_values, 1), mirrored(high[1]), weights, 0),
        ]
        rows = [whole(lows, block) for block in range(2)]
        early_memory = [products(rows[0], later[0]), products(high[0], later[0])]
        late_memory = [products(rows[1], later[1]), products(high[1], later[1])]
        for group in range(2):
            start = whole(bases if group == 0 else second_bases, 1)
            real = early_memory[group][0] + late_memory[group][0]
            imag = early_memory[group][1] + late_memory[group][1]
            stored(1, group, start[0] + scale * imag, start[1] - scale * real)

        current = [nexts[part, ta_place].reshape(order_size, block_rows) for part in range(2)]
        mirror = mirrored([low_next[part, ta_place] for part in range(2)])
        last = window_of(current, mirror, weights, ta_place * (block_rows // NO))
        row = pl.multiple_of(tp_place * stripe, stripe)
        own = [
            nexts[part, ta_place, :, pl.ds(row, stripe), :].reshape(2 * stripe, block_rows)
            for part in range(2)
        ]
        own_rounded = [
            low_next[part, :, pl.ds(row, stripe), :].reshape(2 * stripe, order_size)
            for part in range(2)
        ]
        memory = products(own_rounded, last)
        real, imag = started(own, [turned_by(table, *halves(part)) for part in own])
        shape = (2, stripe, block_rows)
        out[0] = (real + scale * memory[1]).reshape(shape)
        out[1] = (imag - scale * memory[0]).reshape(shape)

    return pl.pallas_call(
        kernel,
        out_shape=jax.ShapeDtypeStruct((2, 2, stripe, block_rows), jnp.float32),
        in_specs=in_vmem(10),
        out_specs=in_vmem(1)[0],
        scratch_shapes=[
            pltpu.VMEM(each.shape, each.dtype)
            for each in kept_shapes(tp_count, stripe, block_rows)
        ]
        + [
            pltpu.VMEM((2, 2, 2, block_rows, block_rows), jnp.float32),
            pltpu.VMEM((2, 2, block_rows, order_size), jnp.bfloat16),
        ],
        compiler_params=pltpu.CompilerParams(vmem_limit_bytes=24 << 20),
        name="second_stage",
    )


def replicated(green, hamiltonian, interaction):
    tp_count = lax.axis_size("tp")
    count = 2 * tp_count
    stripe = green.shape[3]
    block_rows = green.shape[4]
    factor = 1.0 / math.sqrt(2 * block_rows)
    mask, first_masks, second_masks = exchange_masks(tp_count)

    def exchanged(block, mask):
        masks = (mask, mask) if isinstance(mask, int) else mask
        return lax.ppermute(block, ("ta", "tp"), [(i, i ^ masks[i % 2]) for i in range(count)])

    arriving = exchanged(green.reshape(-1, block_rows), mask).reshape(green.shape)
    first = jnp.stack([green[:, 0, 0], arriving[:, 0, 0]])
    second = jnp.stack([green[:, 1, 0], arriving[:, 1, 0]])
    high = lax.reduce_precision(second, 8, 7)
    second = jnp.stack([high, second - high], 1).astype(jnp.bfloat16)
    first_parts = second_parts = ()
    for first_mask, second_mask in zip(zip(*first_masks), second_masks):
        first_parts = [first, exchanged(first, first_mask)]
        first = jnp.concatenate(first_parts)
        if second_mask == tp_count:
            other_high = exchanged(second[:, 0], second_mask)[:, None]
            second = jnp.concatenate([second[:, :1], other_high, second[:, 1:]], 1)
        else:
            second_parts = [second, exchanged(second, second_mask)]
            second = jnp.concatenate(second_parts)
    first_parts += [exchanged(first_parts[0], 1)]
    first_parts += [exchanged(first_parts[1], 1)]
    second_parts += [exchanged(part, 1) for part in second_parts]
    first_masks = [[mask] + each for each in first_masks]
    second_masks = [mask] + [later for later in second_masks if later != tp_count]
    sizes = (tp_count, stripe, block_rows, factor)
    *kept, weights, table = early_stage(first_masks, *sizes)(
        *first_parts[::2], hamiltonian, interaction
    )
    known = first_stage(first_masks, *sizes)(*first_parts[1::2], weights, table, *kept)
    result = second_stage(second_masks, *sizes)(*second_parts, weights, table, *known)
    return result[:, :, None]


def solution(mesh):
    in_specs = (P(None, None, "tp", None, "ta"), P(), P())
    out_specs = P(None, None, "tp", None, "ta")
    ta_count = mesh.shape["ta"]
    tp_count = mesh.shape["tp"]

    def shards(green, hamiltonian, interaction):
        whole_bytes = green.size * green.dtype.itemsize * ta_count * tp_count
        covered = ta_count == 2 and green.shape[1] == 2 and tp_count >= 16
        if covered and tp_count & (tp_count - 1) == 0 and whole_bytes <= 1 << 22:
            return replicated(green, hamiltonian, interaction)
        return windowed(green, hamiltonian, interaction)

    return jax.shard_map(shards, mesh=mesh, in_specs=in_specs, out_specs=out_specs, check_vma=False)
```

profile of v0, /device:TPU:0, one launch (start us, length us, event | category | flops | bytes accessed | tf_op | source)
XLA Modules:
  0.0 29.9 jit_solution(16662589829824369541)
XLA Ops:
  0.0 4.1 %collective-permute-start = (f32[64,256]{1,0:T(8,128)}, f32[64,256]{1,0:T(8,128)S(1)}, u32[]{:S(2)}, u32[]{:S(2)}) collective-permute-start(f32[64,256]{1,0:T(8,128)} %bitcast.28), channel_id=1, source_target_pairs={{0,8},{1,9},{2,10},{3,11},{4,12},{5,13},{6,14},{7,15},{8,0},{9,1},... | collective-permute-start | bytes 196616 | tf_op jit(solution)/shard_map/ppermute | solution.py:409
  4.1 0.8 %slice_bitcast_fusion.2 = (f32[1,2,16,256]{3,2,1,0:T(8,128)S(1)}, f32[1,1,2,16,256]{4,3,2,1,0:T(8,128)S(1)}) fusion(f32[2,2,1,16,256]{4,3,2,1,0:T(8,128)} %param.3), kind=kLoop, calls=%fused_computation.11 | loop fusion | bytes 131072 | tf_op jit(solution)/shard_map/stack;squeeze | solution.py:412
  4.9 3.1 %collective-permute-done = f32[64,256]{1,0:T(8,128)S(1)} collective-permute-done((f32[64,256]{1,0:T(8,128)}, f32[64,256]{1,0:T(8,128)S(1)}, u32[]{:S(2)}, u32[]{:S(2)}) %collective-permute-start) | collective-permute-done | bytes 65568 | tf_op jit(solution)/shard_map/ppermute | solution.py:409
  7.9 1.8 %collective-permute-start.6 = (f32[2,2,16,256]{3,2,1,0:T(8,128)S(1)}, f32[2,2,16,256]{3,2,1,0:T(8,128)S(1)}, u32[]{:S(2)}, u32[]{:S(2)}) collective-permute-start(f32[2,2,16,256]{3,2,1,0:T(8,128)S(1)} %pad_maximum_fusion.5), channel_id=1, source_target_pairs={{0,16},{1,3},{2,18},{3,1},{4,20},{5,7},{6,22},{7,5},{8,24},{9,11},... | collective-permute-start | bytes 196616 | tf_op jit(solution)/shard_map/ppermute | solution.py:409
  9.7 0.4 %collective-permute-start.1 = (bf16[2,2,16,256]{3,2,1,0:T(8,128)(2,1)S(1)}, bf16[2,2,16,256]{3,2,1,0:T(8,128)(2,1)S(1)}, u32[]{:S(2)}, u32[]{:S(2)}) collective-permute-start(bf16[2,2,16,256]{3,2,1,0:T(8,128)(2,1)S(1)} %bitcast.25), channel_id=1, source_target_pairs={{0,16},{1,17},{2,18},{3,19},{4,20},{5,21},{6,22},{7,23},{8,24},{9,... | collective-permute-start | bytes 98312 | tf_op jit(solution)/shard_map/ppermute | solution.py:409
  10.1 2.2 %collective-permute-done.6 = f32[2,2,16,256]{3,2,1,0:T(8,128)S(1)} collective-permute-done((f32[2,2,16,256]{3,2,1,0:T(8,128)S(1)}, f32[2,2,16,256]{3,2,1,0:T(8,128)S(1)}, u32[]{:S(2)}, u32[]{:S(2)}) %collective-permute-start.6) | collective-permute-done | bytes 65568 | tf_op jit(solution)/shard_map/ppermute | solution.py:409
  12.3 1.0 %collective-permute-start.7 = (f32[4,2,16,256]{3,2,1,0:T(8,128)S(1)}, f32[4,2,16,256]{3,2,1,0:T(8,128)S(1)}, u32[]{:S(2)}, u32[]{:S(2)}) collective-permute-start(f32[4,2,16,256]{3,2,1,0:T(8,128)S(1)} %pad_maximum_fusion.2), channel_id=1, source_target_pairs={{0,4},{1,5},{2,6},{3,7},{4,0},{5,1},{6,2},{7,3},{8,12},{9,13},{10,... | collective-permute-start | bytes 393224 | tf_op jit(solution)/shard_map/ppermute | solution.py:409
  13.3 0.4 %collective-permute-done.1 = bf16[2,2,16,256]{3,2,1,0:T(8,128)(2,1)S(1)} collective-permute-done((bf16[2,2,16,256]{3,2,1,0:T(8,128)(2,1)S(1)}, bf16[2,2,16,256]{3,2,1,0:T(8,128)(2,1)S(1)}, u32[]{:S(2)}, u32[]{:S(2)}) %collective-permute-start.1) | collective-permute-done | bytes 32800 | tf_op jit(solution)/shard_map/ppermute | solution.py:409
  13.7 1.6 %collective-permute-start.2 = (bf16[2,3,2,16,256]{4,3,2,1,0:T(8,128)(2,1)S(1)}, bf16[2,3,2,16,256]{4,3,2,1,0:T(8,128)(2,1)S(1)}, u32[]{:S(2)}, u32[]{:S(2)}) collective-permute-start(bf16[2,3,2,16,256]{4,3,2,1,0:T(8,128)(2,1)S(1)} %pad_maximum_fusion.3), channel_id=1, source_target_pairs={{0,2},{1,3},{2,0},{3,1},{4,6},{5,7},{6,4},{7,5},{8,10},{9,11},{10,... | collective-permute-start | bytes 294920 | tf_op jit(solution)/shard_map/ppermute | solution.py:409
  15.3 2.0 %collective-permute-done.7 = f32[4,2,16,256]{3,2,1,0:T(8,128)S(1)} collective-permute-done((f32[4,2,16,256]{3,2,1,0:T(8,128)S(1)}, f32[4,2,16,256]{3,2,1,0:T(8,128)S(1)}, u32[]{:S(2)}, u32[]{:S(2)}) %collective-permute-start.7) | collective-permute-done | bytes 131104 | tf_op jit(solution)/shard_map/ppermute | solution.py:409
  17.3 0.0 copy-start
  17.4 0.0 copy-start.1
  17.4 1.8 %collective-permute-start.9 = (f32[8,2,16,256]{3,2,1,0:T(8,128)S(1)}, f32[8,2,16,256]{3,2,1,0:T(8,128)S(1)}, u32[]{:S(2)}, u32[]{:S(2)}) collective-permute-start(f32[8,2,16,256]{3,2,1,0:T(8,128)S(1)} %pad_maximum_fusion.refs_0_), channel_id=1, source_target_pairs={{0,2},{1,17},{2,0},{3,19},{4,6},{5,21},{6,4},{7,23},{8,10},{9,25},... | collective-permute-start | bytes 786440 | tf_op jit(solution)/shard_map/ppermute | solution.py:409
  19.2 0.0 collective-permute-done.2
  19.2 0.5 %collective-permute-start.3 = (bf16[4,3,2,16,256]{4,3,2,1,0:T(8,128)(2,1)S(1)}, bf16[4,3,2,16,256]{4,3,2,1,0:T(8,128)(2,1)S(1)}, u32[]{:S(2)}, u32[]{:S(2)}) collective-permute-start(bf16[4,3,2,16,256]{4,3,2,1,0:T(8,128)(2,1)S(1)} %pad_maximum_fusion.1.refs_0_), channel_id=1, source_target_pairs={{0,4},{1,5},{2,6},{3,7},{4,0},{5,1},{6,2},{7,3},{8,12},{9,13},{10,... | collective-permute-start | bytes 589832 | tf_op jit(solution)/shard_map/ppermute | solution.py:409
  19.7 0.0 collective-permute-start.8
  19.7 4.1 %collective-permute-done.9.refs_0_ = f32[8,2,16,256]{3,2,1,0:T(8,128)S(1)} collective-permute-done((f32[8,2,16,256]{3,2,1,0:T(8,128)S(1)}, f32[8,2,16,256]{3,2,1,0:T(8,128)S(1)}, u32[]{:S(2)}, u32[]{:S(2)}) %collective-permute-start.9) | collective-permute-done | bytes 262176 | tf_op jit(solution)/shard_map/ppermute | solution.py:409
  23.8 0.0 collective-permute-start.10
  23.8 0.5 %collective-permute-start.4 = (bf16[4,3,2,16,256]{4,3,2,1,0:T(8,128)(2,1)S(1)}, bf16[4,3,2,16,256]{4,3,2,1,0:T(8,128)(2,1)S(1)}, u32[]{:S(2)}, u32[]{:S(2)}) collective-permute-start(bf16[4,3,2,16,256]{4,3,2,1,0:T(8,128)(2,1)S(1)} %pad_maximum_fusion.1.refs_0_), channel_id=1, source_target_pairs={{0,1},{1,0},{2,3},{3,2},{4,5},{5,4},{6,7},{7,6},{8,9},{9,8},{10,11... | collective-permute-start | bytes 589832 | tf_op jit(solution)/shard_map/ppermute | solution.py:409
  24.3 0.6 %collective-permute-done.3.refs_1_ = bf16[4,3,2,16,256]{4,3,2,1,0:T(8,128)(2,1)S(1)} collective-permute-done((bf16[4,3,2,16,256]{4,3,2,1,0:T(8,128)(2,1)S(1)}, bf16[4,3,2,16,256]{4,3,2,1,0:T(8,128)(2,1)S(1)}, u32[]{:S(2)}, u32[]{:S(2)}) %collective-permute-start.3) | collective-permute-done | bytes 196640 | tf_op jit(solution)/shard_map/ppermute | solution.py:409
  24.9 0.0 collective-permute-start.5
  24.9 0.0 collective-permute-done.8.refs_1_
  24.9 0.0 copy-done
  25.0 0.0 copy-done.1
  25.0 0.6 %early_stage.1 = (f32[2,32,16,256]{3,2,1,0:T(8,128)S(1)}, bf16[2,32,16,256]{3,2,1,0:T(8,128)(2,1)S(1)}, f32[2,32,16,256]{3,2,1,0:T(8,128)S(1)}, f32[32,256]{1,0:T(8,128)S(1)}, bf16[2,256,256]{2,1,0:T(8,128)(2,1)S(1)}) custom-call(f32[8,2,16,256]{3,2,1,0:T(8,128)S(1)} %pad_maximum_fusion.refs_0_, f32[8,2,16,256]{3,2,1,0:T(8,128)S(1)} %collective-permute-done.8.refs_1_, ...), custom_call_target="tpu_custom_call" | custom-call | tf_op jit(solution)/shard_map/early_stage/pallas_call | solution.py:432
  25.5 0.0 collective-permute-done.10.refs_1_
  25.6 0.7 %first_stage.1 = (f32[2,32,16,256]{3,2,1,0:T(8,128)S(1)}, bf16[2,32,16,256]{3,2,1,0:T(8,128)(2,1)S(1)}, f32[2,32,16,256]{3,2,1,0:T(8,128)S(1)}, bf16[2,256,256]{2,1,0:T(8,128)(2,1)S(1)}) custom-call(f32[8,2,16,256]{3,2,1,0:T(8,128)S(1)} %collective-permute-done.9.refs_0_, ...), custom_call_target="tpu_custom_call", output_to_operand_aliasing={{0}: (4, {}), {1}: (5, {}), {2}: (6, {})} | custom-call | tf_op jit(solution)/shard_map/first_stage/pallas_call | solution.py:435
  26.3 0.0 collective-permute-done.4.refs_2_
  26.3 0.1 collective-permute-done.5.refs_3_
  26.4 3.5 %second_stage.1 = f32[2,2,16,256]{3,2,1,0:T(8,128)} custom-call(bf16[4,3,2,16,256]{4,3,2,1,0:T(8,128)(2,1)S(1)} %pad_maximum_fusion.1.refs_0_, bf16[4,3,2,16,256]{4,3,2,1,0:T(8,128)(2,1)S(1)} %collective-permute-done.3.refs_1_, bf16[4,3,2,16,256]{4,3,2,1,0:T(8,128)(2,1)S(1)} %collective-permute-done.4.refs_2_, ...), custom_call_target="tpu_custom_call" | custom-call | tf_op jit(solution)/shard_map/second_stage/pallas_call | solution.py:436
  (7 shorter events, 0.1 us)
Async XLA Ops:
  0.0 7.9 %collective-permute-start = (f32[64,256]{1,0:T(8,128)}, f32[64,256]{1,0:T(8,128)S(1)}, u32[]{:S(2)}, u32[]{:S(2)}) collective-permute-start(f32[64,256]{1,0:T(8,128)} %bitcast.28), channel_id=1, source_target_pairs={{0,8},{1,9},{2,10},{3,11},{4,12},{5,13},{6,14},{7,15},{8,0},{9,1},... | collective-permute-start | bytes 196616 | tf_op jit(solution)/shard_map/ppermute | solution.py:409
  7.9 4.3 %collective-permute-start.6 = (f32[2,2,16,256]{3,2,1,0:T(8,128)S(1)}, f32[2,2,16,256]{3,2,1,0:T(8,128)S(1)}, u32[]{:S(2)}, u32[]{:S(2)}) collective-permute-start(f32[2,2,16,256]{3,2,1,0:T(8,128)S(1)} %pad_maximum_fusion.5), channel_id=1, source_target_pairs={{0,16},{1,3},{2,18},{3,1},{4,20},{5,7},{6,22},{7,5},{8,24},{9,11},... | collective-permute-start | bytes 196616 | tf_op jit(solution)/shard_map/ppermute | solution.py:409
  9.7 4.0 %collective-permute-start.1 = (bf16[2,2,16,256]{3,2,1,0:T(8,128)(2,1)S(1)}, bf16[2,2,16,256]{3,2,1,0:T(8,128)(2,1)S(1)}, u32[]{:S(2)}, u32[]{:S(2)}) collective-permute-start(bf16[2,2,16,256]{3,2,1,0:T(8,128)(2,1)S(1)} %bitcast.25), channel_id=1, source_target_pairs={{0,16},{1,17},{2,18},{3,19},{4,20},{5,21},{6,22},{7,23},{8,24},{9,... | collective-permute-start | bytes 98312 | tf_op jit(solution)/shard_map/ppermute | solution.py:409
  12.3 5.0 %collective-permute-start.7 = (f32[4,2,16,256]{3,2,1,0:T(8,128)S(1)}, f32[4,2,16,256]{3,2,1,0:T(8,128)S(1)}, u32[]{:S(2)}, u32[]{:S(2)}) collective-permute-start(f32[4,2,16,256]{3,2,1,0:T(8,128)S(1)} %pad_maximum_fusion.2), channel_id=1, source_target_pairs={{0,4},{1,5},{2,6},{3,7},{4,0},{5,1},{6,2},{7,3},{8,12},{9,13},{10,... | collective-permute-start | bytes 393224 | tf_op jit(solution)/shard_map/ppermute | solution.py:409
  13.7 5.5 %collective-permute-start.2 = (bf16[2,3,2,16,256]{4,3,2,1,0:T(8,128)(2,1)S(1)}, bf16[2,3,2,16,256]{4,3,2,1,0:T(8,128)(2,1)S(1)}, u32[]{:S(2)}, u32[]{:S(2)}) collective-permute-start(bf16[2,3,2,16,256]{4,3,2,1,0:T(8,128)(2,1)S(1)} %pad_maximum_fusion.3), channel_id=1, source_target_pairs={{0,2},{1,3},{2,0},{3,1},{4,6},{5,7},{6,4},{7,5},{8,10},{9,11},{10,... | collective-permute-start | bytes 294920 | tf_op jit(solution)/shard_map/ppermute | solution.py:409
  17.3 7.6 %copy-start = (f32[32,32]{1,0:T(8,128)S(1)}, f32[32,32]{1,0:T(8,128)}, u32[]{:S(2)}) copy-start(f32[32,32]{1,0:T(8,128)} %refs_2_.1) | copy-start | bytes 12292
  17.4 7.6 %copy-start.1 = (f32[32,32]{1,0:T(8,128)S(1)}, f32[32,32]{1,0:T(8,128)}, u32[]{:S(2)}) copy-start(f32[32,32]{1,0:T(8,128)} %refs_3_.1) | copy-start | bytes 12292
  17.4 6.4 %collective-permute-start.9 = (f32[8,2,16,256]{3,2,1,0:T(8,128)S(1)}, f32[8,2,16,256]{3,2,1,0:T(8,128)S(1)}, u32[]{:S(2)}, u32[]{:S(2)}) collective-permute-start(f32[8,2,16,256]{3,2,1,0:T(8,128)S(1)} %pad_maximum_fusion.refs_0_), channel_id=1, source_target_pairs={{0,2},{1,17},{2,0},{3,19},{4,6},{5,21},{6,4},{7,23},{8,10},{9,25},... | collective-permute-start | bytes 786440 | tf_op jit(solution)/shard_map/ppermute | solution.py:409
  19.2 5.7 %collective-permute-start.3 = (bf16[4,3,2,16,256]{4,3,2,1,0:T(8,128)(2,1)S(1)}, bf16[4,3,2,16,256]{4,3,2,1,0:T(8,128)(2,1)S(1)}, u32[]{:S(2)}, u32[]{:S(2)}) collective-permute-start(bf16[4,3,2,16,256]{4,3,2,1,0:T(8,128)(2,1)S(1)} %pad_maximum_fusion.1.refs_0_), channel_id=1, source_target_pairs={{0,4},{1,5},{2,6},{3,7},{4,0},{5,1},{6,2},{7,3},{8,12},{9,13},{10,... | collective-permute-start | bytes 589832 | tf_op jit(solution)/shard_map/ppermute | solution.py:409
  19.7 5.2 %collective-permute-start.8 = (f32[8,2,16,256]{3,2,1,0:T(8,128)S(1)}, f32[8,2,16,256]{3,2,1,0:T(8,128)S(1)}, u32[]{:S(2)}, u32[]{:S(2)}) collective-permute-start(f32[8,2,16,256]{3,2,1,0:T(8,128)S(1)} %pad_maximum_fusion.refs_0_), channel_id=1, source_target_pairs={{0,1},{1,0},{2,3},{3,2},{4,5},{5,4},{6,7},{7,6},{8,9},{9,8},{10,11... | collective-permute-start | bytes 786440 | tf_op jit(solution)/shard_map/ppermute | solution.py:409
  23.8 1.8 %collective-permute-start.10 = (f32[8,2,16,256]{3,2,1,0:T(8,128)S(1)}, f32[8,2,16,256]{3,2,1,0:T(8,128)S(1)}, u32[]{:S(2)}, u32[]{:S(2)}) collective-permute-start(f32[8,2,16,256]{3,2,1,0:T(8,128)S(1)} %collective-permute-done.9.refs_0_), channel_id=1, source_target_pairs={{0,1},{1,0},{2,3},{3,2},{4,5},{5,4},{6,7},{7,6},{8,9},{9,8},{10,11... | collective-permute-start | bytes 786440 | tf_op jit(solution)/shard_map/ppermute | solution.py:409
  23.8 2.5 %collective-permute-start.4 = (bf16[4,3,2,16,256]{4,3,2,1,0:T(8,128)(2,1)S(1)}, bf16[4,3,2,16,256]{4,3,2,1,0:T(8,128)(2,1)S(1)}, u32[]{:S(2)}, u32[]{:S(2)}) collective-permute-start(bf16[4,3,2,16,256]{4,3,2,1,0:T(8,128)(2,1)S(1)} %pad_maximum_fusion.1.refs_0_), channel_id=1, source_target_pairs={{0,1},{1,0},{2,3},{3,2},{4,5},{5,4},{6,7},{7,6},{8,9},{9,8},{10,11... | collective-permute-start | bytes 589832 | tf_op jit(solution)/shard_map/ppermute | solution.py:409
  24.9 1.4 %collective-permute-start.5 = (bf16[4,3,2,16,256]{4,3,2,1,0:T(8,128)(2,1)S(1)}, bf16[4,3,2,16,256]{4,3,2,1,0:T(8,128)(2,1)S(1)}, u32[]{:S(2)}, u32[]{:S(2)}) collective-permute-start(bf16[4,3,2,16,256]{4,3,2,1,0:T(8,128)(2,1)S(1)} %collective-permute-done.3.refs_1_), channel_id=1, source_target_pairs={{0,1},{1,0},{2,3},{3,2},{4,5},{5,4},{6,7},{7,6},{8,9},{9,8},{10,11... | collective-permute-start | bytes 589832 | tf_op jit(solution)/shard_map/ppermute | solution.py:409
where the time goes:
time: 30.1 us; the launch traced here: 29.9 us
  waiting for transfers between devices  12.5 us (42%)
  starting transfers between devices  11.6 us (39%)
  Pallas kernels  4.81 us (16%)
  local copies, waits for them, and re-layouts  0.82 us (3%)
    ppermute x11, waiting for transfers between devices, exchanged(): lax.ppermute(block, ('ta', 'tp'), [(i, i ^ masks[i % 2]) for i in range(c...  12.5 us
    ppermute x11, starting transfers between devices, exchanged(): lax.ppermute(block, ('ta', 'tp'), [(i, i ^ masks[i % 2]) for i in range(c...  11.6 us
    pallas_call x1, Pallas kernels, replicated(): second_stage(second_masks, *sizes)(*second_parts, weights, table, *known)  3.54 us
    another operation x2, local copies, waits for them, and re-layouts, replicated(): first = jnp.stack([green[:, 0, 0], arriving[:, 0, 0]])  0.8 us
    pallas_call x1, Pallas kernels, replicated(): first_stage(first_masks, *sizes)(*first_parts[1::2], weights, table, *kept)  0.69 us
  transfers between devices with their start and end apart: 11, of which 7 were waited for; matrix products, arithmetic and copies ran while one was open for 3% of the time, Pallas kernels for 4%

commit v1 on v0

--- a/solution.py
+++ b/solution.py
@@ -148,21 +148,25 @@
     return high, (values - high.astype(jnp.float32)).astype(jnp.bfloat16)
 
 
-def window_of(values, mirror, weights, first_time):
+def window_of(values, mirror, weights, first_time=None):
     rows, width = values[0].shape
     real_square = values[0] * values[0] - values[1] * values[1]
     imag_square = 2.0 * values[0] * values[1]
     real = real_square * mirror[0] - imag_square * mirror[1]
     imag = real_square * mirror[1] + imag_square * mirror[0]
-    source_time = lax.broadcasted_iota(jnp.int32, (rows, width), 0) // NO
-    target_time = lax.broadcasted_iota(jnp.int32, (rows, width), 1) // NO + first_time
-    inside = source_time <= target_time
+    inside = None
+    if first_time is not None:
+        source_time = lax.broadcasted_iota(jnp.int32, (rows, width), 0) // NO
+        target_time = lax.broadcasted_iota(jnp.int32, (rows, width), 1) // NO + first_time
+        inside = source_time <= target_time
 
     def weighted(part):
         part = (part.reshape(rows // NO, NO, width) * weights[None]).reshape(rows, width)
-        return jnp.where(inside, part, 0.0).astype(jnp.bfloat16)
-
-    return weighted(real), weighted(imag)
+        part = part if inside is None else jnp.where(inside, part, 0.0)
+        return part.astype(jnp.bfloat16)
+
+    real, imag = weighted(real), weighted(imag)
+    return [jnp.concatenate([real, -imag]), jnp.concatenate([imag, real])]
 
 
 def mirrored(rounded):
@@ -170,9 +174,8 @@
 
 
 def products(left_side, right_side):
-    real = bf16_dot(left_side[0], right_side[0]) - bf16_dot(left_side[1], right_side[1])
-    imag = bf16_dot(left_side[0], right_side[1]) + bf16_dot(left_side[1], right_side[0])
-    return real, imag
+    left_side = jnp.concatenate(left_side, axis=1)
+    return [bf16_dot(left_side, part) for part in right_side]
 
 
 def tables_of(hamiltonian, interaction, block_rows):
@@ -185,12 +188,12 @@
         lax.broadcasted_iota(jnp.int32, table.shape, 0) // NO
         == lax.broadcasted_iota(jnp.int32, table.shape, 1) // NO
     )
-    return weights, halves(jnp.where(same_time, table, 0.0))
-
-
-def turned_by(table, high, low=None):
-    result = bf16_dot(high, table[0]) + bf16_dot(high, table[1])
-    return result if low is None else result + bf16_dot(low, table[0])
+    high, low = halves(jnp.where(same_time, table, 0.0))
+    return weights, jnp.concatenate([high, high, low])
+
+
+def turned_by(table, high, low):
+    return bf16_dot(jnp.concatenate([low, high, high], axis=1), table)
 
 
 def started(values, turned):
@@ -230,24 +233,6 @@
             put(me ^ (flip ^ mask), targets, (values, highs, base), index, stripe)
 
 
-def take_second(sources, late, me, offsets, tp_count, stripe, table, targets):
-    count = len(offsets) // 2
-    for flip in range(2):
-        for plane in range(2):
-            highs = [rows_of(sources[flip][:, plane, part]) for part in range(2)]
-            values = [high.astype(jnp.float32) for high in highs]
-            if plane == 0:
-                lows = [rows_of(sources[flip][:, 2, part]) for part in range(2)]
-                values = [values[part] + lows[part].astype(jnp.float32) for part in range(2)]
-                turned = [turned_by(table, highs[part], lows[part]) for part in range(2)]
-            else:
-                turned = [turned_by(table, high) for high in highs]
-            base = started(values, turned)
-            for index in range(count):
-                device = me ^ (flip ^ offsets[late * count + index] ^ (plane * tp_count))
-                put(device, targets, (values, highs, base), index, stripe)
-
-
 def own_place(tp_count):
     return lax.axis_index("ta") * tp_count + lax.axis_index("tp")
 
@@ -269,14 +254,13 @@
         me = own_place(tp_count)
         weights, table = tables_of(hamiltonian, interaction, block_rows)
         weights_out[...] = weights
-        table_out[0] = table[0]
-        table_out[1] = table[1]
+        table_out[...] = table
         take_first(refs[:2], 0, me, offsets, stripe, table, refs[4:7])
 
     shapes = kept_shapes(tp_count, stripe, block_rows)
     tables = [
         jax.ShapeDtypeStruct((NO, block_rows), jnp.float32),
-        jax.ShapeDtypeStruct((2, block_rows, block_rows), jnp.bfloat16),
+        jax.ShapeDtypeStruct((3 * block_rows, block_rows), jnp.bfloat16),
     ]
     return pl.pallas_call(
         kernel,
@@ -293,7 +277,7 @@
     scale = 0.5 * factor
 
     def kernel(*refs):
-        weights, table = refs[2], (refs[3][0], refs[3][1])
+        weights, table = refs[2], refs[3][...]
         targets, window = refs[7:10], refs[10]
         take_first(refs[:2], 1, own_place(tp_count), offsets, stripe, table, targets)
         values, highs, bases = targets
@@ -306,7 +290,7 @@
         bases[0, :tp_count] = bases[0, :tp_count] + scale * memory[1].reshape(half)
         bases[1, :tp_count] = bases[1, :tp_count] - scale * memory[0].reshape(half)
 
-    square = jax.ShapeDtypeStruct((2, block_rows, block_rows), jnp.bfloat16)
+    square = jax.ShapeDtypeStruct((2, 2 * block_rows, block_rows), jnp.bfloat16)
     return pl.pallas_call(
         kernel,
         out_shape=kept_shapes(tp_count, stripe, block_rows) + [square],
@@ -320,21 +304,39 @@
 
 def second_stage(masks, tp_count, stripe, block_rows, factor):
     offsets = offsets_of(masks)
+    half_count = len(offsets) // 2
     order_size = 2 * block_rows
     scale = 0.5 * factor
 
     def kernel(*refs):
-        weights, table = refs[4][...], (refs[5][0], refs[5][1])
+        weights, table = refs[4][...], refs[5][...]
         values, lows, bases, window = refs[6:10]
-        out, targets, nexts, low_next = refs[10], refs[11:14], refs[14], refs[15]
+        out, highs, rests, nexts, low_next = refs[10:]
         ta_place = lax.axis_index("ta")
         tp_place = lax.axis_index("tp")
         me = own_place(tp_count)
-        for late in range(2):
-            sources = refs[late:4:2]
-            take_second(sources, late, me, offsets, tp_count, stripe, table, targets)
-        second_values, second_highs, second_bases = targets
-        high = [whole(second_highs, block) for block in range(2)]
+        blank = jnp.zeros((stripe, block_rows), jnp.bfloat16)
+        for flip in range(2):
+            for index, mask in enumerate(offsets):
+                late, slot = divmod(index, half_count)
+                device = me ^ (flip ^ mask)
+                other = device ^ tp_count
+                source = refs[2 * flip + late]
+                for part in range(2):
+                    highs[part, device] = source[slot, 0, part]
+                    highs[part, other] = source[slot, 1, part]
+                    rests[part, device] = source[slot, 2, part]
+                    rests[part, other] = blank
+        high = [whole(highs, block) for block in range(2)]
+        rest = [whole(rests, block) for block in range(2)]
+        full = [
+            [high[block][k].astype(jnp.float32) + rest[block][k].astype(jnp.float32) for k in range(2)]
+            for block in range(2)
+        ]
+        base = [
+            started(full[block], [turned_by(table, high[block][k], rest[block][k]) for k in range(2)])
+            for block in range(2)
+        ]
 
         def stored(block, group, real, imag):
             for part, result in ((0, real), (1, imag)):
@@ -344,21 +346,18 @@
                 )
 
         stored(0, 0, *whole(bases, 0))
-        memory = products(high[0], (window[0], window[1]))
-        base = whole(second_bases, 0)
-        stored(0, 1, base[0] + scale * memory[1], base[1] - scale * memory[0])
+        memory = products(high[0], [window[0], window[1]])
+        stored(0, 1, base[0][0] + scale * memory[1], base[0][1] - scale * memory[0])
         later = [
-            window_of(whole(values, 1), mirrored(high[0]), weights, block_rows // NO),
-            window_of(whole(second_values, 1), mirrored(high[1]), weights, 0),
+            window_of(whole(values, 1), mirrored(high[0]), weights),
+            window_of(full[1], mirrored(high[1]), weights, 0),
         ]
-        rows = [whole(lows, block) for block in range(2)]
-        early_memory = [products(rows[0], later[0]), products(high[0], later[0])]
-        late_memory = [products(rows[1], later[1]), products(high[1], later[1])]
+        later = [jnp.concatenate([later[0][k], later[1][k]]) for k in range(2)]
         for group in range(2):
-            start = whole(bases if group == 0 else second_bases, 1)
-            real = early_memory[group][0] + late_memory[group][0]
-            imag = early_memory[group][1] + late_memory[group][1]
-            stored(1, group, start[0] + scale * imag, start[1] - scale * real)
+            start = whole(bases, 1) if group == 0 else base[1]
+            rows = whole(lows, 0) + whole(lows, 1) if group == 0 else high[0] + high[1]
+            memory = products(rows, later)
+            stored(1, group, start[0] + scale * memory[1], start[1] - scale * memory[0])
 
         current = [nexts[part, ta_place].reshape(order_size, block_rows) for part in range(2)]
         mirror = mirrored([low_next[part, ta_place] for part in range(2)])
@@ -383,10 +382,7 @@
         out_shape=jax.ShapeDtypeStruct((2, 2, stripe, block_rows), jnp.float32),
         in_specs=in_vmem(10),
         out_specs=in_vmem(1)[0],
-        scratch_shapes=[
-            pltpu.VMEM(each.shape, each.dtype)
-            for each in kept_shapes(tp_count, stripe, block_rows)
-        ]
+        scratch_shapes=[pltpu.VMEM((2, 2 * tp_count, stripe, block_rows), jnp.bfloat16)] * 2
         + [
             pltpu.VMEM((2, 2, 2, block_rows, block_rows), jnp.float32),
             pltpu.VMEM((2, 2, block_rows, order_size), jnp.bfloat16),

time: 30.1 us -> 29.7 us (0.987)
  Pallas kernels: 4.81 us -> 4.39 us
    pallas_call x1, Pallas kernels: 3.54 us -> 3.11 us  [replicated(): second_stage(second_masks, *sizes)(*second_parts, weights, table, *known)]
where the time goes in v1:
time: 29.7 us; the launch traced here: 29.5 us
  waiting for transfers between devices  12.5 us (42%)
  starting transfers between devices  11.6 us (39%)
  Pallas kernels  4.39 us (15%)
  local copies, waits for them, and re-layouts  0.82 us (3%)
    ppermute x11, waiting for transfers between devices, exchanged(): lax.ppermute(block, ('ta', 'tp'), [(i, i ^ masks[i % 2]) for i in range(c...  12.5 us
    ppermute x11, starting transfers between devices, exchanged(): lax.ppermute(block, ('ta', 'tp'), [(i, i ^ masks[i % 2]) for i in range(c...  11.6 us
    pallas_call x1, Pallas kernels, replicated(): second_stage(second_masks, *sizes)(*second_parts, weights, table, *known)  3.11 us
    another operation x2, local copies, waits for them, and re-layouts, replicated(): first = jnp.stack([green[:, 0, 0], arriving[:, 0, 0]])  0.8 us
    pallas_call x1, Pallas kernels, replicated(): first_stage(first_masks, *sizes)(*first_parts[1::2], weights, table, *kept)  0.71 us
  transfers between devices with their start and end apart: 11, of which 7 were waited for; matrix products, arithmetic and copies ran while one was open for 3% of the time, Pallas kernels for 4%

profile of v1, /device:TPU:0, one launch (start us, length us, event | category | flops | bytes accessed | tf_op | source)
XLA Modules:
  0.0 29.5 jit_solution(13957397983820367911)
XLA Ops:
  0.0 4.1 %collective-permute-start = (f32[64,256]{1,0:T(8,128)}, f32[64,256]{1,0:T(8,128)S(1)}, u32[]{:S(2)}, u32[]{:S(2)}) collective-permute-start(f32[64,256]{1,0:T(8,128)} %bitcast.28), channel_id=1, source_target_pairs={{0,8},{1,9},{2,10},{3,11},{4,12},{5,13},{6,14},{7,15},{8,0},{9,1},... | collective-permute-start | bytes 196616 | tf_op jit(solution)/shard_map/ppermute | solution.py:405
  4.1 0.8 %slice_bitcast_fusion.2 = (f32[1,2,16,256]{3,2,1,0:T(8,128)S(1)}, f32[1,1,2,16,256]{4,3,2,1,0:T(8,128)S(1)}) fusion(f32[2,2,1,16,256]{4,3,2,1,0:T(8,128)} %param.3), kind=kLoop, calls=%fused_computation.11 | loop fusion | bytes 131072 | tf_op jit(solution)/shard_map/stack;squeeze | solution.py:408
  4.9 3.1 %collective-permute-done = f32[64,256]{1,0:T(8,128)S(1)} collective-permute-done((f32[64,256]{1,0:T(8,128)}, f32[64,256]{1,0:T(8,128)S(1)}, u32[]{:S(2)}, u32[]{:S(2)}) %collective-permute-start) | collective-permute-done | bytes 65568 | tf_op jit(solution)/shard_map/ppermute | solution.py:405
  7.9 1.8 %collective-permute-start.6 = (f32[2,2,16,256]{3,2,1,0:T(8,128)S(1)}, f32[2,2,16,256]{3,2,1,0:T(8,128)S(1)}, u32[]{:S(2)}, u32[]{:S(2)}) collective-permute-start(f32[2,2,16,256]{3,2,1,0:T(8,128)S(1)} %pad_maximum_fusion.5), channel_id=1, source_target_pairs={{0,16},{1,3},{2,18},{3,1},{4,20},{5,7},{6,22},{7,5},{8,24},{9,11},... | collective-permute-start | bytes 196616 | tf_op jit(solution)/shard_map/ppermute | solution.py:405
  9.7 0.4 %collective-permute-start.1 = (bf16[2,2,16,256]{3,2,1,0:T(8,128)(2,1)S(1)}, bf16[2,2,16,256]{3,2,1,0:T(8,128)(2,1)S(1)}, u32[]{:S(2)}, u32[]{:S(2)}) collective-permute-start(bf16[2,2,16,256]{3,2,1,0:T(8,128)(2,1)S(1)} %bitcast.25), channel_id=1, source_target_pairs={{0,16},{1,17},{2,18},{3,19},{4,20},{5,21},{6,22},{7,23},{8,24},{9,... | collective-permute-start | bytes 98312 | tf_op jit(solution)/shard_map/ppermute | solution.py:405
  10.1 2.2 %collective-permute-done.6 = f32[2,2,16,256]{3,2,1,0:T(8,128)S(1)} collective-permute-done((f32[2,2,16,256]{3,2,1,0:T(8,128)S(1)}, f32[2,2,16,256]{3,2,1,0:T(8,128)S(1)}, u32[]{:S(2)}, u32[]{:S(2)}) %collective-permute-start.6) | collective-permute-done | bytes 65568 | tf_op jit(solution)/shard_map/ppermute | solution.py:405
  12.3 1.0 %collective-permute-start.7 = (f32[4,2,16,256]{3,2,1,0:T(8,128)S(1)}, f32[4,2,16,256]{3,2,1,0:T(8,128)S(1)}, u32[]{:S(2)}, u32[]{:S(2)}) collective-permute-start(f32[4,2,16,256]{3,2,1,0:T(8,128)S(1)} %pad_maximum_fusion.2), channel_id=1, source_target_pairs={{0,4},{1,5},{2,6},{3,7},{4,0},{5,1},{6,2},{7,3},{8,12},{9,13},{10,... | collective-permute-start | bytes 393224 | tf_op jit(solution)/shard_map/ppermute | solution.py:405
  13.3 0.4 %collective-permute-done.1 = bf16[2,2,16,256]{3,2,1,0:T(8,128)(2,1)S(1)} collective-permute-done((bf16[2,2,16,256]{3,2,1,0:T(8,128)(2,1)S(1)}, bf16[2,2,16,256]{3,2,1,0:T(8,128)(2,1)S(1)}, u32[]{:S(2)}, u32[]{:S(2)}) %collective-permute-start.1) | collective-permute-done | bytes 32800 | tf_op jit(solution)/shard_map/ppermute | solution.py:405
  13.7 1.6 %collective-permute-start.2 = (bf16[2,3,2,16,256]{4,3,2,1,0:T(8,128)(2,1)S(1)}, bf16[2,3,2,16,256]{4,3,2,1,0:T(8,128)(2,1)S(1)}, u32[]{:S(2)}, u32[]{:S(2)}) collective-permute-start(bf16[2,3,2,16,256]{4,3,2,1,0:T(8,128)(2,1)S(1)} %pad_maximum_fusion.3), channel_id=1, source_target_pairs={{0,2},{1,3},{2,0},{3,1},{4,6},{5,7},{6,4},{7,5},{8,10},{9,11},{10,... | collective-permute-start | bytes 294920 | tf_op jit(solution)/shard_map/ppermute | solution.py:405
  15.3 2.0 %collective-permute-done.7 = f32[4,2,16,256]{3,2,1,0:T(8,128)S(1)} collective-permute-done((f32[4,2,16,256]{3,2,1,0:T(8,128)S(1)}, f32[4,2,16,256]{3,2,1,0:T(8,128)S(1)}, u32[]{:S(2)}, u32[]{:S(2)}) %collective-permute-start.7) | collective-permute-done | bytes 131104 | tf_op jit(solution)/shard_map/ppermute | solution.py:405
  17.3 0.0 copy-start
  17.4 0.0 copy-start.1
  17.4 1.8 %collective-permute-start.9 = (f32[8,2,16,256]{3,2,1,0:T(8,128)S(1)}, f32[8,2,16,256]{3,2,1,0:T(8,128)S(1)}, u32[]{:S(2)}, u32[]{:S(2)}) collective-permute-start(f32[8,2,16,256]{3,2,1,0:T(8,128)S(1)} %pad_maximum_fusion.refs_0_), channel_id=1, source_target_pairs={{0,2},{1,17},{2,0},{3,19},{4,6},{5,21},{6,4},{7,23},{8,10},{9,25},... | collective-permute-start | bytes 786440 | tf_op jit(solution)/shard_map/ppermute | solution.py:405
  19.2 0.0 collective-permute-done.2
  19.2 0.5 %collective-permute-start.3 = (bf16[4,3,2,16,256]{4,3,2,1,0:T(8,128)(2,1)S(1)}, bf16[4,3,2,16,256]{4,3,2,1,0:T(8,128)(2,1)S(1)}, u32[]{:S(2)}, u32[]{:S(2)}) collective-permute-start(bf16[4,3,2,16,256]{4,3,2,1,0:T(8,128)(2,1)S(1)} %pad_maximum_fusion.1.refs_0_), channel_id=1, source_target_pairs={{0,4},{1,5},{2,6},{3,7},{4,0},{5,1},{6,2},{7,3},{8,12},{9,13},{10,... | collective-permute-start | bytes 589832 | tf_op jit(solution)/shard_map/ppermute | solution.py:405
  19.7 0.0 collective-permute-start.8
  19.7 4.1 %collective-permute-done.9.refs_0_ = f32[8,2,16,256]{3,2,1,0:T(8,128)S(1)} collective-permute-done((f32[8,2,16,256]{3,2,1,0:T(8,128)S(1)}, f32[8,2,16,256]{3,2,1,0:T(8,128)S(1)}, u32[]{:S(2)}, u32[]{:S(2)}) %collective-permute-start.9) | collective-permute-done | bytes 262176 | tf_op jit(solution)/shard_map/ppermute | solution.py:405
  23.8 0.0 collective-permute-start.10
  23.8 0.5 %collective-permute-start.4 = (bf16[4,3,2,16,256]{4,3,2,1,0:T(8,128)(2,1)S(1)}, bf16[4,3,2,16,256]{4,3,2,1,0:T(8,128)(2,1)S(1)}, u32[]{:S(2)}, u32[]{:S(2)}) collective-permute-start(bf16[4,3,2,16,256]{4,3,2,1,0:T(8,128)(2,1)S(1)} %pad_maximum_fusion.1.refs_0_), channel_id=1, source_target_pairs={{0,1},{1,0},{2,3},{3,2},{4,5},{5,4},{6,7},{7,6},{8,9},{9,8},{10,11... | collective-permute-start | bytes 589832 | tf_op jit(solution)/shard_map/ppermute | solution.py:405
  24.3 0.6 %collective-permute-done.3.refs_1_ = bf16[4,3,2,16,256]{4,3,2,1,0:T(8,128)(2,1)S(1)} collective-permute-done((bf16[4,3,2,16,256]{4,3,2,1,0:T(8,128)(2,1)S(1)}, bf16[4,3,2,16,256]{4,3,2,1,0:T(8,128)(2,1)S(1)}, u32[]{:S(2)}, u32[]{:S(2)}) %collective-permute-start.3) | collective-permute-done | bytes 196640 | tf_op jit(solution)/shard_map/ppermute | solution.py:405
  24.9 0.0 collective-permute-start.5
  24.9 0.0 collective-permute-done.8.refs_1_
  24.9 0.0 copy-done
  25.0 0.0 copy-done.1
  25.0 0.6 %early_stage.1 = (f32[2,32,16,256]{3,2,1,0:T(8,128)S(1)}, bf16[2,32,16,256]{3,2,1,0:T(8,128)(2,1)S(1)}, f32[2,32,16,256]{3,2,1,0:T(8,128)S(1)}, f32[32,256]{1,0:T(8,128)S(1)}, bf16[768,256]{1,0:T(8,128)(2,1)S(1)}) custom-call(f32[8,2,16,256]{3,2,1,0:T(8,128)S(1)} %pad_maximum_fusion.refs_0_, f32[8,2,16,256]{3,2,1,0:T(8,128)S(1)} %collective-permute-done.8.refs_1_, ...), custom_call_target="tpu_custom_call" | custom-call | tf_op jit(solution)/shard_map/early_stage/pallas_call | solution.py:428
  25.5 0.0 collective-permute-done.10.refs_1_
  25.6 0.7 %first_stage.1 = (f32[2,32,16,256]{3,2,1,0:T(8,128)S(1)}, bf16[2,32,16,256]{3,2,1,0:T(8,128)(2,1)S(1)}, f32[2,32,16,256]{3,2,1,0:T(8,128)S(1)}, bf16[2,512,256]{2,1,0:T(8,128)(2,1)S(1)}) custom-call(f32[8,2,16,256]{3,2,1,0:T(8,128)S(1)} %collective-permute-done.9.refs_0_, ...), custom_call_target="tpu_custom_call", output_to_operand_aliasing={{0}: (4, {}), {1}: (5, {}), {2}: (6, {})} | custom-call | tf_op jit(solution)/shard_map/first_stage/pallas_call | solution.py:431
  26.3 0.0 collective-permute-done.4.refs_2_
  26.3 0.1 collective-permute-done.5.refs_3_
  26.4 3.1 %second_stage.1 = f32[2,2,16,256]{3,2,1,0:T(8,128)} custom-call(bf16[4,3,2,16,256]{4,3,2,1,0:T(8,128)(2,1)S(1)} %pad_maximum_fusion.1.refs_0_, bf16[4,3,2,16,256]{4,3,2,1,0:T(8,128)(2,1)S(1)} %collective-permute-done.3.refs_1_, bf16[4,3,2,16,256]{4,3,2,1,0:T(8,128)(2,1)S(1)} %collective-permute-done.4.refs_2_, ...), custom_call_target="tpu_custom_call" | custom-call | tf_op jit(solution)/shard_map/second_stage/pallas_call | solution.py:432
  (7 shorter events, 0.1 us)
Async XLA Ops:
  0.0 7.9 %collective-permute-start = (f32[64,256]{1,0:T(8,128)}, f32[64,256]{1,0:T(8,128)S(1)}, u32[]{:S(2)}, u32[]{:S(2)}) collective-permute-start(f32[64,256]{1,0:T(8,128)} %bitcast.28), channel_id=1, source_target_pairs={{0,8},{1,9},{2,10},{3,11},{4,12},{5,13},{6,14},{7,15},{8,0},{9,1},... | collective-permute-start | bytes 196616 | tf_op jit(solution)/shard_map/ppermute | solution.py:405
  7.9 4.3 %collective-permute-start.6 = (f32[2,2,16,256]{3,2,1,0:T(8,128)S(1)}, f32[2,2,16,256]{3,2,1,0:T(8,128)S(1)}, u32[]{:S(2)}, u32[]{:S(2)}) collective-permute-start(f32[2,2,16,256]{3,2,1,0:T(8,128)S(1)} %pad_maximum_fusion.5), channel_id=1, source_target_pairs={{0,16},{1,3},{2,18},{3,1},{4,20},{5,7},{6,22},{7,5},{8,24},{9,11},... | collective-permute-start | bytes 196616 | tf_op jit(solution)/shard_map/ppermute | solution.py:405
  9.7 4.0 %collective-permute-start.1 = (bf16[2,2,16,256]{3,2,1,0:T(8,128)(2,1)S(1)}, bf16[2,2,16,256]{3,2,1,0:T(8,128)(2,1)S(1)}, u32[]{:S(2)}, u32[]{:S(2)}) collective-permute-start(bf16[2,2,16,256]{3,2,1,0:T(8,128)(2,1)S(1)} %bitcast.25), channel_id=1, source_target_pairs={{0,16},{1,17},{2,18},{3,19},{4,20},{5,21},{6,22},{7,23},{8,24},{9,... | collective-permute-start | bytes 98312 | tf_op jit(solution)/shard_map/ppermute | solution.py:405
  12.3 5.0 %collective-permute-start.7 = (f32[4,2,16,256]{3,2,1,0:T(8,128)S(1)}, f32[4,2,16,256]{3,2,1,0:T(8,128)S(1)}, u32[]{:S(2)}, u32[]{:S(2)}) collective-permute-start(f32[4,2,16,256]{3,2,1,0:T(8,128)S(1)} %pad_maximum_fusion.2), channel_id=1, source_target_pairs={{0,4},{1,5},{2,6},{3,7},{4,0},{5,1},{6,2},{7,3},{8,12},{9,13},{10,... | collective-permute-start | bytes 393224 | tf_op jit(solution)/shard_map/ppermute | solution.py:405
  13.7 5.5 %collective-permute-start.2 = (bf16[2,3,2,16,256]{4,3,2,1,0:T(8,128)(2,1)S(1)}, bf16[2,3,2,16,256]{4,3,2,1,0:T(8,128)(2,1)S(1)}, u32[]{:S(2)}, u32[]{:S(2)}) collective-permute-start(bf16[2,3,2,16,256]{4,3,2,1,0:T(8,128)(2,1)S(1)} %pad_maximum_fusion.3), channel_id=1, source_target_pairs={{0,2},{1,3},{2,0},{3,1},{4,6},{5,7},{6,4},{7,5},{8,10},{9,11},{10,... | collective-permute-start | bytes 294920 | tf_op jit(solution)/shard_map/ppermute | solution.py:405
  17.3 7.6 %copy-start = (f32[32,32]{1,0:T(8,128)S(1)}, f32[32,32]{1,0:T(8,128)}, u32[]{:S(2)}) copy-start(f32[32,32]{1,0:T(8,128)} %refs_2_.1) | copy-start | bytes 12292
  17.4 7.6 %copy-start.1 = (f32[32,32]{1,0:T(8,128)S(1)}, f32[32,32]{1,0:T(8,128)}, u32[]{:S(2)}) copy-start(f32[32,32]{1,0:T(8,128)} %refs_3_.1) | copy-start | bytes 12292
  17.4 6.4 %collective-permute-start.9 = (f32[8,2,16,256]{3,2,1,0:T(8,128)S(1)}, f32[8,2,16,256]{3,2,1,0:T(8,128)S(1)}, u32[]{:S(2)}, u32[]{:S(2)}) collective-permute-start(f32[8,2,16,256]{3,2,1,0:T(8,128)S(1)} %pad_maximum_fusion.refs_0_), channel_id=1, source_target_pairs={{0,2},{1,17},{2,0},{3,19},{4,6},{5,21},{6,4},{7,23},{8,10},{9,25},... | collective-permute-start | bytes 786440 | tf_op jit(solution)/shard_map/ppermute | solution.py:405
  19.2 5.7 %collective-permute-start.3 = (bf16[4,3,2,16,256]{4,3,2,1,0:T(8,128)(2,1)S(1)}, bf16[4,3,2,16,256]{4,3,2,1,0:T(8,128)(2,1)S(1)}, u32[]{:S(2)}, u32[]{:S(2)}) collective-permute-start(bf16[4,3,2,16,256]{4,3,2,1,0:T(8,128)(2,1)S(1)} %pad_maximum_fusion.1.refs_0_), channel_id=1, source_target_pairs={{0,4},{1,5},{2,6},{3,7},{4,0},{5,1},{6,2},{7,3},{8,12},{9,13},{10,... | collective-permute-start | bytes 589832 | tf_op jit(solution)/shard_map/ppermute | solution.py:405
  19.7 5.2 %collective-permute-start.8 = (f32[8,2,16,256]{3,2,1,0:T(8,128)S(1)}, f32[8,2,16,256]{3,2,1,0:T(8,128)S(1)}, u32[]{:S(2)}, u32[]{:S(2)}) collective-permute-start(f32[8,2,16,256]{3,2,1,0:T(8,128)S(1)} %pad_maximum_fusion.refs_0_), channel_id=1, source_target_pairs={{0,1},{1,0},{2,3},{3,2},{4,5},{5,4},{6,7},{7,6},{8,9},{9,8},{10,11... | collective-permute-start | bytes 786440 | tf_op jit(solution)/shard_map/ppermute | solution.py:405
  23.8 1.8 %collective-permute-start.10 = (f32[8,2,16,256]{3,2,1,0:T(8,128)S(1)}, f32[8,2,16,256]{3,2,1,0:T(8,128)S(1)}, u32[]{:S(2)}, u32[]{:S(2)}) collective-permute-start(f32[8,2,16,256]{3,2,1,0:T(8,128)S(1)} %collective-permute-done.9.refs_0_), channel_id=1, source_target_pairs={{0,1},{1,0},{2,3},{3,2},{4,5},{5,4},{6,7},{7,6},{8,9},{9,8},{10,11... | collective-permute-start | bytes 786440 | tf_op jit(solution)/shard_map/ppermute | solution.py:405
  23.8 2.5 %collective-permute-start.4 = (bf16[4,3,2,16,256]{4,3,2,1,0:T(8,128)(2,1)S(1)}, bf16[4,3,2,16,256]{4,3,2,1,0:T(8,128)(2,1)S(1)}, u32[]{:S(2)}, u32[]{:S(2)}) collective-permute-start(bf16[4,3,2,16,256]{4,3,2,1,0:T(8,128)(2,1)S(1)} %pad_maximum_fusion.1.refs_0_), channel_id=1, source_target_pairs={{0,1},{1,0},{2,3},{3,2},{4,5},{5,4},{6,7},{7,6},{8,9},{9,8},{10,11... | collective-permute-start | bytes 589832 | tf_op jit(solution)/shard_map/ppermute | solution.py:405
  24.9 1.4 %collective-permute-start.5 = (bf16[4,3,2,16,256]{4,3,2,1,0:T(8,128)(2,1)S(1)}, bf16[4,3,2,16,256]{4,3,2,1,0:T(8,128)(2,1)S(1)}, u32[]{:S(2)}, u32[]{:S(2)}) collective-permute-start(bf16[4,3,2,16,256]{4,3,2,1,0:T(8,128)(2,1)S(1)} %collective-permute-done.3.refs_1_), channel_id=1, source_target_pairs={{0,1},{1,0},{2,3},{3,2},{4,5},{5,4},{6,7},{7,6},{8,9},{9,8},{10,11... | collective-permute-start | bytes 589832 | tf_op jit(solution)/shard_map/ppermute | solution.py:405

commit v2 on v1

--- a/solution.py
+++ b/solution.py
@@ -148,25 +148,23 @@
     return high, (values - high.astype(jnp.float32)).astype(jnp.bfloat16)
 
 
-def window_of(values, mirror, weights, first_time=None):
-    rows, width = values[0].shape
-    real_square = values[0] * values[0] - values[1] * values[1]
-    imag_square = 2.0 * values[0] * values[1]
-    real = real_square * mirror[0] - imag_square * mirror[1]
-    imag = real_square * mirror[1] + imag_square * mirror[0]
-    inside = None
-    if first_time is not None:
-        source_time = lax.broadcasted_iota(jnp.int32, (rows, width), 0) // NO
-        target_time = lax.broadcasted_iota(jnp.int32, (rows, width), 1) // NO + first_time
-        inside = source_time <= target_time
-
-    def weighted(part):
-        part = (part.reshape(rows // NO, NO, width) * weights[None]).reshape(rows, width)
-        part = part if inside is None else jnp.where(inside, part, 0.0)
-        return part.astype(jnp.bfloat16)
-
-    real, imag = weighted(real), weighted(imag)
+def squares_of(values, weights):
+    real = values[0] * values[0] - values[1] * values[1]
+    imag = 2.0 * values[0] * values[1]
+    return real * weights, imag * weights
+
+
+def window_of(squares, mirror):
+    real = squares[0] * mirror[0] - squares[1] * mirror[1]
+    imag = squares[0] * mirror[1] + squares[1] * mirror[0]
+    real, imag = real.astype(jnp.bfloat16), imag.astype(jnp.bfloat16)
     return [jnp.concatenate([real, -imag]), jnp.concatenate([imag, real])]
+
+
+def inside_only(weights, first_time):
+    source_time = lax.broadcasted_iota(jnp.int32, weights.shape, 0) // NO
+    target_time = lax.broadcasted_iota(jnp.int32, weights.shape, 1) // NO + first_time
+    return jnp.where(source_time <= target_time, weights, 0.0)
 
 
 def mirrored(rounded):
@@ -250,23 +248,29 @@
     offsets = [offsets_of(each) for each in masks]
 
     def kernel(*refs):
-        hamiltonian, interaction, weights_out, table_out = refs[2:4] + refs[7:]
+        hamiltonian, interaction, diagonal, last, table_out = refs[2:4] + refs[7:]
         me = own_place(tp_count)
         weights, table = tables_of(hamiltonian, interaction, block_rows)
-        weights_out[...] = weights
+        weights = jnp.concatenate([weights] * (block_rows // NO))
+        diagonal[0] = weights
+        diagonal[1] = inside_only(weights, 0)
+        last[...] = inside_only(
+            jnp.concatenate([weights] * 2), lax.axis_index("ta") * (block_rows // NO)
+        )
         table_out[...] = table
         take_first(refs[:2], 0, me, offsets, stripe, table, refs[4:7])
 
     shapes = kept_shapes(tp_count, stripe, block_rows)
     tables = [
-        jax.ShapeDtypeStruct((NO, block_rows), jnp.float32),
+        jax.ShapeDtypeStruct((2, block_rows, block_rows), jnp.float32),
+        jax.ShapeDtypeStruct((2 * block_rows, block_rows), jnp.float32),
         jax.ShapeDtypeStruct((3 * block_rows, block_rows), jnp.bfloat16),
     ]
     return pl.pallas_call(
         kernel,
         out_shape=shapes + tables,
         in_specs=in_vmem(4),
-        out_specs=in_vmem(5),
+        out_specs=in_vmem(6),
         compiler_params=pltpu.CompilerParams(vmem_limit_bytes=16 << 20),
         name="early_stage",
     )
@@ -278,11 +282,12 @@
 
     def kernel(*refs):
         weights, table = refs[2], refs[3][...]
-        targets, window = refs[7:10], refs[10]
+        targets, window, squares = refs[7:10], refs[10], refs[11]
         take_first(refs[:2], 1, own_place(tp_count), offsets, stripe, table, targets)
         values, highs, bases = targets
         high = whole(highs, 0)
-        made = window_of(whole(values, 0), mirrored(high), weights[...], 0)
+        made = window_of(squares_of(whole(values, 0), weights[1]), mirrored(high))
+        squares[0], squares[1] = squares_of(whole(values, 1), weights[0])
         memory = products(high, made)
         window[0] = made[0]
         window[1] = made[1]
@@ -293,9 +298,10 @@
     square = jax.ShapeDtypeStruct((2, 2 * block_rows, block_rows), jnp.bfloat16)
     return pl.pallas_call(
         kernel,
-        out_shape=kept_shapes(tp_count, stripe, block_rows) + [square],
+        out_shape=kept_shapes(tp_count, stripe, block_rows)
+        + [square, jax.ShapeDtypeStruct((2, block_rows, block_rows), jnp.float32)],
         in_specs=in_vmem(7),
-        out_specs=in_vmem(4),
+        out_specs=in_vmem(5),
         input_output_aliases={4: 0, 5: 1, 6: 2},
         compiler_params=pltpu.CompilerParams(vmem_limit_bytes=16 << 20),
         name="first_stage",
@@ -309,9 +315,9 @@
     scale = 0.5 * factor
 
     def kernel(*refs):
-        weights, table = refs[4][...], refs[5][...]
-        values, lows, bases, window = refs[6:10]
-        out, highs, rests, nexts, low_next = refs[10:]
+        diagonal, last_weights, table = refs[4], refs[5], refs[6][...]
+        lows, bases, window, squares = refs[7:11]
+        out, highs, rests, nexts, low_next = refs[11:]
         ta_place = lax.axis_index("ta")
         tp_place = lax.axis_index("tp")
         me = own_place(tp_count)
@@ -349,8 +355,8 @@
         memory = products(high[0], [window[0], window[1]])
         stored(0, 1, base[0][0] + scale * memory[1], base[0][1] - scale * memory[0])
         later = [
-            window_of(whole(values, 1), mirrored(high[0]), weights),
-            window_of(full[1], mirrored(high[1]), weights, 0),
+            window_of([squares[0], squares[1]], mirrored(high[0])),
+            window_of(squares_of(full[1], diagonal[1]), mirrored(high[1])),
         ]
         later = [jnp.concatenate([later[0][k], later[1][k]]) for k in range(2)]
         for group in range(2):
@@ -361,7 +367,7 @@
 
         current = [nexts[part, ta_place].reshape(order_size, block_rows) for part in range(2)]
         mirror = mirrored([low_next[part, ta_place] for part in range(2)])
-        last = window_of(current, mirror, weights, ta_place * (block_rows // NO))
+        last = window_of(squares_of(current, last_weights[...]), mirror)
         row = pl.multiple_of(tp_place * stripe, stripe)
         own = [
             nexts[part, ta_place, :, pl.ds(row, stripe), :].reshape(2 * stripe, block_rows)
@@ -380,7 +386,7 @@
     return pl.pallas_call(
         kernel,
         out_shape=jax.ShapeDtypeStruct((2, 2, stripe, block_rows), jnp.float32),
-        in_specs=in_vmem(10),
+        in_specs=in_vmem(11),
         out_specs=in_vmem(1)[0],
         scratch_shapes=[pltpu.VMEM((2, 2 * tp_count, stripe, block_rows), jnp.bfloat16)] * 2
         + [
@@ -425,11 +431,11 @@
     first_masks = [[mask] + each for each in first_masks]
     second_masks = [mask] + [later for later in second_masks if later != tp_count]
     sizes = (tp_count, stripe, block_rows, factor)
-    *kept, weights, table = early_stage(first_masks, *sizes)(
+    *kept, weights, last, table = early_stage(first_masks, *sizes)(
         *first_parts[::2], hamiltonian, interaction
     )
-    known = first_stage(first_masks, *sizes)(*first_parts[1::2], weights, table, *kept)
-    result = second_stage(second_masks, *sizes)(*second_parts, weights, table, *known)
+    _, *known = first_stage(first_masks, *sizes)(*first_parts[1::2], weights, table, *kept)
+    result = second_stage(second_masks, *sizes)(*second_parts, weights, last, table, *known)
     return result[:, :, None]
 
 

time: 29.7 us -> 29.6 us (level)
  transfers between devices with their start and end apart: 11 -> 11, of which waited for: 7 -> 6; matrix products, arithmetic and copies ran while one was open for 3% -> 3% of each run, Pallas kernels for 4% -> 5%
where the time goes in v2:
time: 29.6 us; the launch traced here: 29.4 us
  waiting for transfers between devices  12.4 us (42%)
  starting transfers between devices  11.6 us (39%)
  Pallas kernels  4.37 us (15%)
  local copies, waits for them, and re-layouts  0.82 us (3%)
    ppermute x11, waiting for transfers between devices, exchanged(): lax.ppermute(block, ('ta', 'tp'), [(i, i ^ masks[i % 2]) for i in range(c...  12.4 us
    ppermute x11, starting transfers between devices, exchanged(): lax.ppermute(block, ('ta', 'tp'), [(i, i ^ masks[i % 2]) for i in range(c...  11.6 us
    pallas_call x1, Pallas kernels, replicated(): second_stage(second_masks, *sizes)  2.97 us
    pallas_call x1, Pallas kernels, replicated(): first_stage(first_masks, *sizes)(*first_parts[1::2], weights, table, *kept)  0.81 us
    another operation x2, local copies, waits for them, and re-layouts, replicated(): first = jnp.stack([green[:, 0, 0], arriving[:, 0, 0]])  0.8 us
    pallas_call x1, Pallas kernels, replicated(): early_stage(first_masks, *sizes)  0.59 us
  transfers between devices with their start and end apart: 11, of which 6 were waited for; matrix products, arithmetic and copies ran while one was open for 3% of the time, Pallas kernels for 5%

profile of v2, /device:TPU:0, one launch (start us, length us, event | category | flops | bytes accessed | tf_op | source)
XLA Modules:
  0.0 29.4 jit_solution(6406337364600884424)
XLA Ops:
  0.0 4.1 %collective-permute-start = (f32[64,256]{1,0:T(8,128)}, f32[64,256]{1,0:T(8,128)S(1)}, u32[]{:S(2)}, u32[]{:S(2)}) collective-permute-start(f32[64,256]{1,0:T(8,128)} %bitcast.28), channel_id=1, source_target_pairs={{0,8},{1,9},{2,10},{3,11},{4,12},{5,13},{6,14},{7,15},{8,0},{9,1},... | collective-permute-start | bytes 196616 | tf_op jit(solution)/shard_map/ppermute | solution.py:411
  4.1 0.8 %slice_bitcast_fusion.2 = (f32[1,2,16,256]{3,2,1,0:T(8,128)S(1)}, f32[1,1,2,16,256]{4,3,2,1,0:T(8,128)S(1)}) fusion(f32[2,2,1,16,256]{4,3,2,1,0:T(8,128)} %param.3), kind=kLoop, calls=%fused_computation.11 | loop fusion | bytes 131072 | tf_op jit(solution)/shard_map/stack;squeeze | solution.py:414
  4.9 3.1 %collective-permute-done = f32[64,256]{1,0:T(8,128)S(1)} collective-permute-done((f32[64,256]{1,0:T(8,128)}, f32[64,256]{1,0:T(8,128)S(1)}, u32[]{:S(2)}, u32[]{:S(2)}) %collective-permute-start) | collective-permute-done | bytes 65568 | tf_op jit(solution)/shard_map/ppermute | solution.py:411
  7.9 1.8 %collective-permute-start.6 = (f32[2,2,16,256]{3,2,1,0:T(8,128)S(1)}, f32[2,2,16,256]{3,2,1,0:T(8,128)S(1)}, u32[]{:S(2)}, u32[]{:S(2)}) collective-permute-start(f32[2,2,16,256]{3,2,1,0:T(8,128)S(1)} %pad_maximum_fusion.5), channel_id=1, source_target_pairs={{0,16},{1,3},{2,18},{3,1},{4,20},{5,7},{6,22},{7,5},{8,24},{9,11},... | collective-permute-start | bytes 196616 | tf_op jit(solution)/shard_map/ppermute | solution.py:411
  9.7 0.4 %collective-permute-start.1 = (bf16[2,2,16,256]{3,2,1,0:T(8,128)(2,1)S(1)}, bf16[2,2,16,256]{3,2,1,0:T(8,128)(2,1)S(1)}, u32[]{:S(2)}, u32[]{:S(2)}) collective-permute-start(bf16[2,2,16,256]{3,2,1,0:T(8,128)(2,1)S(1)} %bitcast.25), channel_id=1, source_target_pairs={{0,16},{1,17},{2,18},{3,19},{4,20},{5,21},{6,22},{7,23},{8,24},{9,... | collective-permute-start | bytes 98312 | tf_op jit(solution)/shard_map/ppermute | solution.py:411
  10.1 2.2 %collective-permute-done.6 = f32[2,2,16,256]{3,2,1,0:T(8,128)S(1)} collective-permute-done((f32[2,2,16,256]{3,2,1,0:T(8,128)S(1)}, f32[2,2,16,256]{3,2,1,0:T(8,128)S(1)}, u32[]{:S(2)}, u32[]{:S(2)}) %collective-permute-start.6) | collective-permute-done | bytes 65568 | tf_op jit(solution)/shard_map/ppermute | solution.py:411
  12.3 1.0 %collective-permute-start.7 = (f32[4,2,16,256]{3,2,1,0:T(8,128)S(1)}, f32[4,2,16,256]{3,2,1,0:T(8,128)S(1)}, u32[]{:S(2)}, u32[]{:S(2)}) collective-permute-start(f32[4,2,16,256]{3,2,1,0:T(8,128)S(1)} %pad_maximum_fusion.2), channel_id=1, source_target_pairs={{0,4},{1,5},{2,6},{3,7},{4,0},{5,1},{6,2},{7,3},{8,12},{9,13},{10,... | collective-permute-start | bytes 393224 | tf_op jit(solution)/shard_map/ppermute | solution.py:411
  13.3 0.4 %collective-permute-done.1 = bf16[2,2,16,256]{3,2,1,0:T(8,128)(2,1)S(1)} collective-permute-done((bf16[2,2,16,256]{3,2,1,0:T(8,128)(2,1)S(1)}, bf16[2,2,16,256]{3,2,1,0:T(8,128)(2,1)S(1)}, u32[]{:S(2)}, u32[]{:S(2)}) %collective-permute-start.1) | collective-permute-done | bytes 32800 | tf_op jit(solution)/shard_map/ppermute | solution.py:411
  13.7 1.6 %collective-permute-start.2 = (bf16[2,3,2,16,256]{4,3,2,1,0:T(8,128)(2,1)S(1)}, bf16[2,3,2,16,256]{4,3,2,1,0:T(8,128)(2,1)S(1)}, u32[]{:S(2)}, u32[]{:S(2)}) collective-permute-start(bf16[2,3,2,16,256]{4,3,2,1,0:T(8,128)(2,1)S(1)} %pad_maximum_fusion.3), channel_id=1, source_target_pairs={{0,2},{1,3},{2,0},{3,1},{4,6},{5,7},{6,4},{7,5},{8,10},{9,11},{10,... | collective-permute-start | bytes 294920 | tf_op jit(solution)/shard_map/ppermute | solution.py:411
  15.3 2.0 %collective-permute-done.7 = f32[4,2,16,256]{3,2,1,0:T(8,128)S(1)} collective-permute-done((f32[4,2,16,256]{3,2,1,0:T(8,128)S(1)}, f32[4,2,16,256]{3,2,1,0:T(8,128)S(1)}, u32[]{:S(2)}, u32[]{:S(2)}) %collective-permute-start.7) | collective-permute-done | bytes 131104 | tf_op jit(solution)/shard_map/ppermute | solution.py:411
  17.3 0.0 copy-start
  17.4 0.0 copy-start.1
  17.4 1.8 %collective-permute-start.9 = (f32[8,2,16,256]{3,2,1,0:T(8,128)S(1)}, f32[8,2,16,256]{3,2,1,0:T(8,128)S(1)}, u32[]{:S(2)}, u32[]{:S(2)}) collective-permute-start(f32[8,2,16,256]{3,2,1,0:T(8,128)S(1)} %pad_maximum_fusion.refs_0_), channel_id=1, source_target_pairs={{0,2},{1,17},{2,0},{3,19},{4,6},{5,21},{6,4},{7,23},{8,10},{9,25},... | collective-permute-start | bytes 786440 | tf_op jit(solution)/shard_map/ppermute | solution.py:411
  19.2 0.0 collective-permute-done.2
  19.2 0.5 %collective-permute-start.3 = (bf16[4,3,2,16,256]{4,3,2,1,0:T(8,128)(2,1)S(1)}, bf16[4,3,2,16,256]{4,3,2,1,0:T(8,128)(2,1)S(1)}, u32[]{:S(2)}, u32[]{:S(2)}) collective-permute-start(bf16[4,3,2,16,256]{4,3,2,1,0:T(8,128)(2,1)S(1)} %pad_maximum_fusion.1.refs_0_), channel_id=1, source_target_pairs={{0,4},{1,5},{2,6},{3,7},{4,0},{5,1},{6,2},{7,3},{8,12},{9,13},{10,... | collective-permute-start | bytes 589832 | tf_op jit(solution)/shard_map/ppermute | solution.py:411
  19.7 0.0 collective-permute-start.8
  19.7 4.1 %collective-permute-done.9.refs_0_ = f32[8,2,16,256]{3,2,1,0:T(8,128)S(1)} collective-permute-done((f32[8,2,16,256]{3,2,1,0:T(8,128)S(1)}, f32[8,2,16,256]{3,2,1,0:T(8,128)S(1)}, u32[]{:S(2)}, u32[]{:S(2)}) %collective-permute-start.9) | collective-permute-done | bytes 262176 | tf_op jit(solution)/shard_map/ppermute | solution.py:411
  23.8 0.0 collective-permute-start.10
  23.8 0.5 %collective-permute-start.4 = (bf16[4,3,2,16,256]{4,3,2,1,0:T(8,128)(2,1)S(1)}, bf16[4,3,2,16,256]{4,3,2,1,0:T(8,128)(2,1)S(1)}, u32[]{:S(2)}, u32[]{:S(2)}) collective-permute-start(bf16[4,3,2,16,256]{4,3,2,1,0:T(8,128)(2,1)S(1)} %pad_maximum_fusion.1.refs_0_), channel_id=1, source_target_pairs={{0,1},{1,0},{2,3},{3,2},{4,5},{5,4},{6,7},{7,6},{8,9},{9,8},{10,11... | collective-permute-start | bytes 589832 | tf_op jit(solution)/shard_map/ppermute | solution.py:411
  24.3 0.6 %collective-permute-done.3.refs_1_ = bf16[4,3,2,16,256]{4,3,2,1,0:T(8,128)(2,1)S(1)} collective-permute-done((bf16[4,3,2,16,256]{4,3,2,1,0:T(8,128)(2,1)S(1)}, bf16[4,3,2,16,256]{4,3,2,1,0:T(8,128)(2,1)S(1)}, u32[]{:S(2)}, u32[]{:S(2)}) %collective-permute-start.3) | collective-permute-done | bytes 196640 | tf_op jit(solution)/shard_map/ppermute | solution.py:411
  24.9 0.0 collective-permute-start.5
  24.9 0.0 collective-permute-done.8.refs_1_
  24.9 0.0 copy-done
  25.0 0.0 copy-done.1
  25.0 0.6 %early_stage.1 = (f32[2,32,16,256]{3,2,1,0:T(8,128)S(1)}, bf16[2,32,16,256]{3,2,1,0:T(8,128)(2,1)S(1)}, f32[2,32,16,256]{3,2,1,0:T(8,128)S(1)}, f32[2,256,256]{2...) custom-call(f32[8,2,16,256]{3,2,1,0:T(8,128)S(1)} %pad_maximum_fusion.refs_0_, ...), custom_call_target="tpu_custom_call" | custom-call | tf_op jit(solution)/shard_map/early_stage/pallas_call | solution.py:434
  25.6 0.0 collective-permute-done.10.refs_1_
  25.6 0.8 %first_stage.1 = (f32[2,32,16,256]{3,2,1,0:T(8,128)S(1)}, bf16[2,32,16,256]{3,2,1,0:T(8,128)(2,1)S(1)}, f32[2,32,16,256]{3,2,1,0:T(8,128)S(1)}, bf16[2,512,256]{2,1,0:T(8,128)(2,1)S(1)}, f32[2,256,256]{2,1,0:T(8,128)S(1)}) custom-call(f32[8,2,16,256]{3,2,1,0:T(8,128)S(1)} %collective-permute-done.9.refs_0_, ...), custom_call_target="tpu_custom_call", output_to_operand_aliasing={{0}: (4, {}), {1}: (5, {}), {2}: (6, {})} | custom-call | tf_op jit(solution)/shard_map/first_stage/pallas_call | solution.py:437
  26.4 0.0 collective-permute-done.4.refs_2_
  26.4 0.0 collective-permute-done.5.refs_3_
  26.4 3.0 %second_stage.1 = f32[2,2,16,256]{3,2,1,0:T(8,128)} custom-call(bf16[4,3,2,16,256]{4,3,2,1,0:T(8,128)(2,1)S(1)} %pad_maximum_fusion.1.refs_0_, bf16[4,3,2,16,256]{4,3,2,1,0:T(8,128)(2,1)S(1)} %collective-permute-done.3.refs_1_, bf16[4,3,2,16,256]{4,3,2,1,0:T(8,128)(2,1)S(1)} %collective-permute-done.4.refs_2_, ...), custom_call_target="tpu_custom_call" | custom-call | tf_op jit(solution)/shard_map/second_stage/pallas_call | solution.py:438
  (7 shorter events, 0.1 us)
Async XLA Ops:
  0.0 7.9 %collective-permute-start = (f32[64,256]{1,0:T(8,128)}, f32[64,256]{1,0:T(8,128)S(1)}, u32[]{:S(2)}, u32[]{:S(2)}) collective-permute-start(f32[64,256]{1,0:T(8,128)} %bitcast.28), channel_id=1, source_target_pairs={{0,8},{1,9},{2,10},{3,11},{4,12},{5,13},{6,14},{7,15},{8,0},{9,1},... | collective-permute-start | bytes 196616 | tf_op jit(solution)/shard_map/ppermute | solution.py:411
  7.9 4.3 %collective-permute-start.6 = (f32[2,2,16,256]{3,2,1,0:T(8,128)S(1)}, f32[2,2,16,256]{3,2,1,0:T(8,128)S(1)}, u32[]{:S(2)}, u32[]{:S(2)}) collective-permute-start(f32[2,2,16,256]{3,2,1,0:T(8,128)S(1)} %pad_maximum_fusion.5), channel_id=1, source_target_pairs={{0,16},{1,3},{2,18},{3,1},{4,20},{5,7},{6,22},{7,5},{8,24},{9,11},... | collective-permute-start | bytes 196616 | tf_op jit(solution)/shard_map/ppermute | solution.py:411
  9.7 4.0 %collective-permute-start.1 = (bf16[2,2,16,256]{3,2,1,0:T(8,128)(2,1)S(1)}, bf16[2,2,16,256]{3,2,1,0:T(8,128)(2,1)S(1)}, u32[]{:S(2)}, u32[]{:S(2)}) collective-permute-start(bf16[2,2,16,256]{3,2,1,0:T(8,128)(2,1)S(1)} %bitcast.25), channel_id=1, source_target_pairs={{0,16},{1,17},{2,18},{3,19},{4,20},{5,21},{6,22},{7,23},{8,24},{9,... | collective-permute-start | bytes 98312 | tf_op jit(solution)/shard_map/ppermute | solution.py:411
  12.3 5.0 %collective-permute-start.7 = (f32[4,2,16,256]{3,2,1,0:T(8,128)S(1)}, f32[4,2,16,256]{3,2,1,0:T(8,128)S(1)}, u32[]{:S(2)}, u32[]{:S(2)}) collective-permute-start(f32[4,2,16,256]{3,2,1,0:T(8,128)S(1)} %pad_maximum_fusion.2), channel_id=1, source_target_pairs={{0,4},{1,5},{2,6},{3,7},{4,0},{5,1},{6,2},{7,3},{8,12},{9,13},{10,... | collective-permute-start | bytes 393224 | tf_op jit(solution)/shard_map/ppermute | solution.py:411
  13.7 5.5 %collective-permute-start.2 = (bf16[2,3,2,16,256]{4,3,2,1,0:T(8,128)(2,1)S(1)}, bf16[2,3,2,16,256]{4,3,2,1,0:T(8,128)(2,1)S(1)}, u32[]{:S(2)}, u32[]{:S(2)}) collective-permute-start(bf16[2,3,2,16,256]{4,3,2,1,0:T(8,128)(2,1)S(1)} %pad_maximum_fusion.3), channel_id=1, source_target_pairs={{0,2},{1,3},{2,0},{3,1},{4,6},{5,7},{6,4},{7,5},{8,10},{9,11},{10,... | collective-permute-start | bytes 294920 | tf_op jit(solution)/shard_map/ppermute | solution.py:411
  17.3 7.6 %copy-start = (f32[32,32]{1,0:T(8,128)S(1)}, f32[32,32]{1,0:T(8,128)}, u32[]{:S(2)}) copy-start(f32[32,32]{1,0:T(8,128)} %refs_2_.1) | copy-start | bytes 12292
  17.4 7.6 %copy-start.1 = (f32[32,32]{1,0:T(8,128)S(1)}, f32[32,32]{1,0:T(8,128)}, u32[]{:S(2)}) copy-start(f32[32,32]{1,0:T(8,128)} %refs_3_.1) | copy-start | bytes 12292
  17.4 6.4 %collective-permute-start.9 = (f32[8,2,16,256]{3,2,1,0:T(8,128)S(1)}, f32[8,2,16,256]{3,2,1,0:T(8,128)S(1)}, u32[]{:S(2)}, u32[]{:S(2)}) collective-permute-start(f32[8,2,16,256]{3,2,1,0:T(8,128)S(1)} %pad_maximum_fusion.refs_0_), channel_id=1, source_target_pairs={{0,2},{1,17},{2,0},{3,19},{4,6},{5,21},{6,4},{7,23},{8,10},{9,25},... | collective-permute-start | bytes 786440 | tf_op jit(solution)/shard_map/ppermute | solution.py:411
  19.2 5.7 %collective-permute-start.3 = (bf16[4,3,2,16,256]{4,3,2,1,0:T(8,128)(2,1)S(1)}, bf16[4,3,2,16,256]{4,3,2,1,0:T(8,128)(2,1)S(1)}, u32[]{:S(2)}, u32[]{:S(2)}) collective-permute-start(bf16[4,3,2,16,256]{4,3,2,1,0:T(8,128)(2,1)S(1)} %pad_maximum_fusion.1.refs_0_), channel_id=1, source_target_pairs={{0,4},{1,5},{2,6},{3,7},{4,0},{5,1},{6,2},{7,3},{8,12},{9,13},{10,... | collective-permute-start | bytes 589832 | tf_op jit(solution)/shard_map/ppermute | solution.py:411
  19.7 5.2 %collective-permute-start.8 = (f32[8,2,16,256]{3,2,1,0:T(8,128)S(1)}, f32[8,2,16,256]{3,2,1,0:T(8,128)S(1)}, u32[]{:S(2)}, u32[]{:S(2)}) collective-permute-start(f32[8,2,16,256]{3,2,1,0:T(8,128)S(1)} %pad_maximum_fusion.refs_0_), channel_id=1, source_target_pairs={{0,1},{1,0},{2,3},{3,2},{4,5},{5,4},{6,7},{7,6},{8,9},{9,8},{10,11... | collective-permute-start | bytes 786440 | tf_op jit(solution)/shard_map/ppermute | solution.py:411
  23.8 1.8 %collective-permute-start.10 = (f32[8,2,16,256]{3,2,1,0:T(8,128)S(1)}, f32[8,2,16,256]{3,2,1,0:T(8,128)S(1)}, u32[]{:S(2)}, u32[]{:S(2)}) collective-permute-start(f32[8,2,16,256]{3,2,1,0:T(8,128)S(1)} %collective-permute-done.9.refs_0_), channel_id=1, source_target_pairs={{0,1},{1,0},{2,3},{3,2},{4,5},{5,4},{6,7},{7,6},{8,9},{9,8},{10,11... | collective-permute-start | bytes 786440 | tf_op jit(solution)/shard_map/ppermute | solution.py:411
  23.8 2.6 %collective-permute-start.4 = (bf16[4,3,2,16,256]{4,3,2,1,0:T(8,128)(2,1)S(1)}, bf16[4,3,2,16,256]{4,3,2,1,0:T(8,128)(2,1)S(1)}, u32[]{:S(2)}, u32[]{:S(2)}) collective-permute-start(bf16[4,3,2,16,256]{4,3,2,1,0:T(8,128)(2,1)S(1)} %pad_maximum_fusion.1.refs_0_), channel_id=1, source_target_pairs={{0,1},{1,0},{2,3},{3,2},{4,5},{5,4},{6,7},{7,6},{8,9},{9,8},{10,11... | collective-permute-start | bytes 589832 | tf_op jit(solution)/shard_map/ppermute | solution.py:411
  24.9 1.5 %collective-permute-start.5 = (bf16[4,3,2,16,256]{4,3,2,1,0:T(8,128)(2,1)S(1)}, bf16[4,3,2,16,256]{4,3,2,1,0:T(8,128)(2,1)S(1)}, u32[]{:S(2)}, u32[]{:S(2)}) collective-permute-start(bf16[4,3,2,16,256]{4,3,2,1,0:T(8,128)(2,1)S(1)} %collective-permute-done.3.refs_1_), channel_id=1, source_target_pairs={{0,1},{1,0},{2,3},{3,2},{4,5},{5,4},{6,7},{7,6},{8,9},{9,8},{10,11... | collective-permute-start | bytes 589832 | tf_op jit(solution)/shard_map/ppermute | solution.py:411

commit v3 on v2

--- a/solution.py
+++ b/solution.py
@@ -190,7 +190,9 @@
     return weights, jnp.concatenate([high, high, low])
 
 
-def turned_by(table, high, low):
+def turned_by(table, high, low=None):
+    if low is None:
+        return bf16_dot(jnp.concatenate([high, high], axis=1), table[high.shape[1] :])
     return bf16_dot(jnp.concatenate([low, high, high], axis=1), table)
 
 
@@ -231,6 +233,24 @@
             put(me ^ (flip ^ mask), targets, (values, highs, base), index, stripe)
 
 
+def take_second(sources, late, me, offsets, tp_count, stripe, table, targets):
+    count = len(offsets) // 2
+    for flip in range(2):
+        for plane in range(2):
+            highs = [rows_of(sources[flip][:, plane, part]) for part in range(2)]
+            values = [high.astype(jnp.float32) for high in highs]
+            if plane == 0:
+                lows = [rows_of(sources[flip][:, 2, part]) for part in range(2)]
+                values = [values[part] + lows[part].astype(jnp.float32) for part in range(2)]
+                turned = [turned_by(table, highs[part], lows[part]) for part in range(2)]
+            else:
+                turned = [turned_by(table, high) for high in highs]
+            base = started(values, turned)
+            for index in range(count):
+                device = me ^ (flip ^ offsets[late * count + index] ^ (plane * tp_count))
+                put(device, targets, (values, highs, base), index, stripe)
+
+
 def own_place(tp_count):
     return lax.axis_index("ta") * tp_count + lax.axis_index("tp")
 
@@ -244,11 +264,12 @@
     return [pl.BlockSpec(memory_space=pltpu.VMEM)] * count
 
 
-def early_stage(masks, tp_count, stripe, block_rows, factor):
-    offsets = [offsets_of(each) for each in masks]
+def early_stage(first_masks, second_masks, tp_count, stripe, block_rows, factor):
+    offsets = [offsets_of(each) for each in first_masks]
+    second_offsets = offsets_of(second_masks)
 
     def kernel(*refs):
-        hamiltonian, interaction, diagonal, last, table_out = refs[2:4] + refs[7:]
+        hamiltonian, interaction, diagonal, last, table_out = refs[4:6] + refs[12:]
         me = own_place(tp_count)
         weights, table = tables_of(hamiltonian, interaction, block_rows)
         weights = jnp.concatenate([weights] * (block_rows // NO))
@@ -258,7 +279,8 @@
             jnp.concatenate([weights] * 2), lax.axis_index("ta") * (block_rows // NO)
         )
         table_out[...] = table
-        take_first(refs[:2], 0, me, offsets, stripe, table, refs[4:7])
+        take_first(refs[:2], 0, me, offsets, stripe, table, refs[6:9])
+        take_second(refs[2:4], 0, me, second_offsets, tp_count, stripe, table, refs[9:12])
 
     shapes = kept_shapes(tp_count, stripe, block_rows)
     tables = [
@@ -268,9 +290,9 @@
     ]
     return pl.pallas_call(
         kernel,
-        out_shape=shapes + tables,
-        in_specs=in_vmem(4),
-        out_specs=in_vmem(6),
+        out_shape=shapes + shapes + tables,
+        in_specs=in_vmem(6),
+        out_specs=in_vmem(9),
         compiler_params=pltpu.CompilerParams(vmem_limit_bytes=16 << 20),
         name="early_stage",
     )
@@ -310,39 +332,19 @@
 
 def second_stage(masks, tp_count, stripe, block_rows, factor):
     offsets = offsets_of(masks)
-    half_count = len(offsets) // 2
     order_size = 2 * block_rows
     scale = 0.5 * factor
 
     def kernel(*refs):
-        diagonal, last_weights, table = refs[4], refs[5], refs[6][...]
-        lows, bases, window, squares = refs[7:11]
-        out, highs, rests, nexts, low_next = refs[11:]
+        diagonal, last_weights, table = refs[2], refs[3], refs[4][...]
+        lows, bases, window, squares = refs[5:9]
+        out, targets, nexts, low_next = refs[12], refs[13:16], refs[16], refs[17]
         ta_place = lax.axis_index("ta")
         tp_place = lax.axis_index("tp")
         me = own_place(tp_count)
-        blank = jnp.zeros((stripe, block_rows), jnp.bfloat16)
-        for flip in range(2):
-            for index, mask in enumerate(offsets):
-                late, slot = divmod(index, half_count)
-                device = me ^ (flip ^ mask)
-                other = device ^ tp_count
-                source = refs[2 * flip + late]
-                for part in range(2):
-                    highs[part, device] = source[slot, 0, part]
-                    highs[part, other] = source[slot, 1, part]
-                    rests[part, device] = source[slot, 2, part]
-                    rests[part, other] = blank
-        high = [whole(highs, block) for block in range(2)]
-        rest = [whole(rests, block) for block in range(2)]
-        full = [
-            [high[block][k].astype(jnp.float32) + rest[block][k].astype(jnp.float32) for k in range(2)]
-            for block in range(2)
-        ]
-        base = [
-            started(full[block], [turned_by(table, high[block][k], rest[block][k]) for k in range(2)])
-            for block in range(2)
-        ]
+        take_second(refs[:2], 1, me, offsets, tp_count, stripe, table, targets)
+        second_values, second_highs, second_bases = targets
+        high = [whole(second_highs, block) for block in range(2)]
 
         def stored(block, group, real, imag):
             for part, result in ((0, real), (1, imag)):
@@ -353,14 +355,15 @@
 
         stored(0, 0, *whole(bases, 0))
         memory = products(high[0], [window[0], window[1]])
-        stored(0, 1, base[0][0] + scale * memory[1], base[0][1] - scale * memory[0])
+        start = whole(second_bases, 0)
+        stored(0, 1, start[0] + scale * memory[1], start[1] - scale * memory[0])
         later = [
             window_of([squares[0], squares[1]], mirrored(high[0])),
-            window_of(squares_of(full[1], diagonal[1]), mirrored(high[1])),
+            window_of(squares_of(whole(second_values, 1), diagonal[1]), mirrored(high[1])),
         ]
         later = [jnp.concatenate([later[0][k], later[1][k]]) for k in range(2)]
         for group in range(2):
-            start = whole(bases, 1) if group == 0 else base[1]
+            start = whole(bases if group == 0 else second_bases, 1)
             rows = whole(lows, 0) + whole(lows, 1) if group == 0 else high[0] + high[1]
             memory = products(rows, later)
             stored(1, group, start[0] + scale * memory[1], start[1] - scale * memory[0])
@@ -385,11 +388,12 @@
 
     return pl.pallas_call(
         kernel,
-        out_shape=jax.ShapeDtypeStruct((2, 2, stripe, block_rows), jnp.float32),
-        in_specs=in_vmem(11),
-        out_specs=in_vmem(1)[0],
-        scratch_shapes=[pltpu.VMEM((2, 2 * tp_count, stripe, block_rows), jnp.bfloat16)] * 2
-        + [
+        out_shape=[jax.ShapeDtypeStruct((2, 2, stripe, block_rows), jnp.float32)]
+        + kept_shapes(tp_count, stripe, block_rows),
+        in_specs=in_vmem(12),
+        out_specs=in_vmem(4),
+        input_output_aliases={9: 1, 10: 2, 11: 3},
+        scratch_shapes=[
             pltpu.VMEM((2, 2, 2, block_rows, block_rows), jnp.float32),
             pltpu.VMEM((2, 2, block_rows, order_size), jnp.bfloat16),
         ],
@@ -427,16 +431,19 @@
             second = jnp.concatenate(second_parts)
     first_parts += [exchanged(first_parts[0], 1)]
     first_parts += [exchanged(first_parts[1], 1)]
-    second_parts += [exchanged(part, 1) for part in second_parts]
+    second_parts += [exchanged(second_parts[0], 1)]
+    second_parts += [exchanged(second_parts[1], 1)]
     first_masks = [[mask] + each for each in first_masks]
     second_masks = [mask] + [later for later in second_masks if later != tp_count]
     sizes = (tp_count, stripe, block_rows, factor)
-    *kept, weights, last, table = early_stage(first_masks, *sizes)(
-        *first_parts[::2], hamiltonian, interaction
-    )
-    _, *known = first_stage(first_masks, *sizes)(*first_parts[1::2], weights, table, *kept)
-    result = second_stage(second_masks, *sizes)(*second_parts, weights, last, table, *known)
-    return result[:, :, None]
+    *kept, weights, last, table = early_stage(first_masks, second_masks, *sizes)(
+        *first_parts[::2], *second_parts[::2], hamiltonian, interaction
+    )
+    _, *known = first_stage(first_masks, *sizes)(*first_parts[1::2], weights, table, *kept[:3])
+    result = second_stage(second_masks, *sizes)(
+        *second_parts[1::2], weights, last, table, *known, *kept[3:]
+    )
+    return result[0][:, :, None]
 
 
 def solution(mesh):

time: 29.6 us -> 30.7 us (1.037)
  waiting for transfers between devices: 12.4 us -> 13.1 us
  Pallas kernels: 4.37 us -> 4.83 us
    ppermute x11, waiting for transfers between devices: 12.4 us -> 13.1 us  [exchanged(): lax.ppermute(block, ('ta', 'tp'), [(i, i ^ masks[i % 2]) for i in range(c...]
    pallas_call x2, Pallas kernels: 1.4 us -> 1.92 us  [the longest x1 1.11 us: replicated(): early_stage(first_masks, second_masks, *sizes)]
  transfers between devices with their start and end apart: 11 -> 11, of which waited for: 6 -> 7; matrix products, arithmetic and copies ran while one was open for 3% -> 3% of each run, Pallas kernels for 5% -> 6%
where the time goes in v3:
time: 30.7 us; the launch traced here: 30.5 us
  waiting for transfers between devices  13.1 us (43%)
  starting transfers between devices  11.6 us (38%)
  Pallas kernels  4.83 us (16%)
  local copies, waits for them, and re-layouts  0.82 us (3%)
    ppermute x11, waiting for transfers between devices, exchanged(): lax.ppermute(block, ('ta', 'tp'), [(i, i ^ masks[i % 2]) for i in range(c...  13.1 us
    ppermute x11, starting transfers between devices, exchanged(): lax.ppermute(block, ('ta', 'tp'), [(i, i ^ masks[i % 2]) for i in range(c...  11.6 us
    pallas_call x1, Pallas kernels, replicated(): second_stage(second_masks, *sizes)  2.91 us
    pallas_call x1, Pallas kernels, replicated(): early_stage(first_masks, second_masks, *sizes)  1.11 us
    pallas_call x1, Pallas kernels, replicated(): first_stage(first_masks, *sizes)  0.81 us
    another operation x2, local copies, waits for them, and re-layouts, replicated(): first = jnp.stack([green[:, 0, 0], arriving[:, 0, 0]])  0.8 us
  transfers between devices with their start and end apart: 11, of which 7 were waited for; matrix products, arithmetic and copies ran while one was open for 3% of the time, Pallas kernels for 6%

profile of v3, /device:TPU:0, one launch (start us, length us, event | category | flops | bytes accessed | tf_op | source)
XLA Modules:
  0.0 30.5 jit_solution(4672613626523784204)
XLA Ops:
  0.0 4.1 %collective-permute-start = (f32[64,256]{1,0:T(8,128)}, f32[64,256]{1,0:T(8,128)S(1)}, u32[]{:S(2)}, u32[]{:S(2)}) collective-permute-start(f32[64,256]{1,0:T(8,128)} %bitcast.28), channel_id=1, source_target_pairs={{0,8},{1,9},{2,10},{3,11},{4,12},{5,13},{6,14},{7,15},{8,0},{9,1},... | collective-permute-start | bytes 196616 | tf_op jit(solution)/shard_map/ppermute | solution.py:415
  4.1 0.8 %slice_bitcast_fusion.2 = (f32[1,2,16,256]{3,2,1,0:T(8,128)S(1)}, f32[1,1,2,16,256]{4,3,2,1,0:T(8,128)S(1)}) fusion(f32[2,2,1,16,256]{4,3,2,1,0:T(8,128)} %param.3), kind=kLoop, calls=%fused_computation.11 | loop fusion | bytes 131072 | tf_op jit(solution)/shard_map/stack;squeeze | solution.py:418
  4.9 3.1 %collective-permute-done = f32[64,256]{1,0:T(8,128)S(1)} collective-permute-done((f32[64,256]{1,0:T(8,128)}, f32[64,256]{1,0:T(8,128)S(1)}, u32[]{:S(2)}, u32[]{:S(2)}) %collective-permute-start) | collective-permute-done | bytes 65568 | tf_op jit(solution)/shard_map/ppermute | solution.py:415
  7.9 1.8 %collective-permute-start.5 = (f32[2,2,16,256]{3,2,1,0:T(8,128)S(1)}, f32[2,2,16,256]{3,2,1,0:T(8,128)S(1)}, u32[]{:S(2)}, u32[]{:S(2)}) collective-permute-start(f32[2,2,16,256]{3,2,1,0:T(8,128)S(1)} %pad_maximum_fusion.5), channel_id=1, source_target_pairs={{0,16},{1,3},{2,18},{3,1},{4,20},{5,7},{6,22},{7,5},{8,24},{9,11},... | collective-permute-start | bytes 196616 | tf_op jit(solution)/shard_map/ppermute | solution.py:415
  9.7 0.4 %collective-permute-start.1 = (bf16[2,2,16,256]{3,2,1,0:T(8,128)(2,1)S(1)}, bf16[2,2,16,256]{3,2,1,0:T(8,128)(2,1)S(1)}, u32[]{:S(2)}, u32[]{:S(2)}) collective-permute-start(bf16[2,2,16,256]{3,2,1,0:T(8,128)(2,1)S(1)} %bitcast.25), channel_id=1, source_target_pairs={{0,16},{1,17},{2,18},{3,19},{4,20},{5,21},{6,22},{7,23},{8,24},{9,... | collective-permute-start | bytes 98312 | tf_op jit(solution)/shard_map/ppermute | solution.py:415
  10.1 2.2 %collective-permute-done.5 = f32[2,2,16,256]{3,2,1,0:T(8,128)S(1)} collective-permute-done((f32[2,2,16,256]{3,2,1,0:T(8,128)S(1)}, f32[2,2,16,256]{3,2,1,0:T(8,128)S(1)}, u32[]{:S(2)}, u32[]{:S(2)}) %collective-permute-start.5) | collective-permute-done | bytes 65568 | tf_op jit(solution)/shard_map/ppermute | solution.py:415
  12.3 1.0 %collective-permute-start.6 = (f32[4,2,16,256]{3,2,1,0:T(8,128)S(1)}, f32[4,2,16,256]{3,2,1,0:T(8,128)S(1)}, u32[]{:S(2)}, u32[]{:S(2)}) collective-permute-start(f32[4,2,16,256]{3,2,1,0:T(8,128)S(1)} %pad_maximum_fusion.2), channel_id=1, source_target_pairs={{0,4},{1,5},{2,6},{3,7},{4,0},{5,1},{6,2},{7,3},{8,12},{9,13},{10,... | collective-permute-start | bytes 393224 | tf_op jit(solution)/shard_map/ppermute | solution.py:415
  13.3 0.4 %collective-permute-done.1 = bf16[2,2,16,256]{3,2,1,0:T(8,128)(2,1)S(1)} collective-permute-done((bf16[2,2,16,256]{3,2,1,0:T(8,128)(2,1)S(1)}, bf16[2,2,16,256]{3,2,1,0:T(8,128)(2,1)S(1)}, u32[]{:S(2)}, u32[]{:S(2)}) %collective-permute-start.1) | collective-permute-done | bytes 32800 | tf_op jit(solution)/shard_map/ppermute | solution.py:415
  13.7 1.6 %collective-permute-start.2 = (bf16[2,3,2,16,256]{4,3,2,1,0:T(8,128)(2,1)S(1)}, bf16[2,3,2,16,256]{4,3,2,1,0:T(8,128)(2,1)S(1)}, u32[]{:S(2)}, u32[]{:S(2)}) collective-permute-start(bf16[2,3,2,16,256]{4,3,2,1,0:T(8,128)(2,1)S(1)} %pad_maximum_fusion.3), channel_id=1, source_target_pairs={{0,2},{1,3},{2,0},{3,1},{4,6},{5,7},{6,4},{7,5},{8,10},{9,11},{10,... | collective-permute-start | bytes 294920 | tf_op jit(solution)/shard_map/ppermute | solution.py:415
  15.3 2.0 %collective-permute-done.6 = f32[4,2,16,256]{3,2,1,0:T(8,128)S(1)} collective-permute-done((f32[4,2,16,256]{3,2,1,0:T(8,128)S(1)}, f32[4,2,16,256]{3,2,1,0:T(8,128)S(1)}, u32[]{:S(2)}, u32[]{:S(2)}) %collective-permute-start.6) | collective-permute-done | bytes 131104 | tf_op jit(solution)/shard_map/ppermute | solution.py:415
  17.3 0.0 copy-start
  17.4 0.0 copy-start.1
  17.4 1.8 %collective-permute-start.9 = (f32[8,2,16,256]{3,2,1,0:T(8,128)S(1)}, f32[8,2,16,256]{3,2,1,0:T(8,128)S(1)}, u32[]{:S(2)}, u32[]{:S(2)}) collective-permute-start(f32[8,2,16,256]{3,2,1,0:T(8,128)S(1)} %pad_maximum_fusion.refs_0_), channel_id=1, source_target_pairs={{0,2},{1,17},{2,0},{3,19},{4,6},{5,21},{6,4},{7,23},{8,10},{9,25},... | collective-permute-start | bytes 786440 | tf_op jit(solution)/shard_map/ppermute | solution.py:415
  19.2 0.0 collective-permute-done.2
  19.2 0.5 %collective-permute-start.3 = (bf16[4,3,2,16,256]{4,3,2,1,0:T(8,128)(2,1)S(1)}, bf16[4,3,2,16,256]{4,3,2,1,0:T(8,128)(2,1)S(1)}, u32[]{:S(2)}, u32[]{:S(2)}) collective-permute-start(bf16[4,3,2,16,256]{4,3,2,1,0:T(8,128)(2,1)S(1)} %pad_maximum_fusion.1.refs_2_), channel_id=1, source_target_pairs={{0,4},{1,5},{2,6},{3,7},{4,0},{5,1},{6,2},{7,3},{8,12},{9,13},{10,... | collective-permute-start | bytes 589832 | tf_op jit(solution)/shard_map/ppermute | solution.py:415
  19.7 0.0 collective-permute-start.7
  19.7 4.1 %collective-permute-done.9.refs_0_ = f32[8,2,16,256]{3,2,1,0:T(8,128)S(1)} collective-permute-done((f32[8,2,16,256]{3,2,1,0:T(8,128)S(1)}, f32[8,2,16,256]{3,2,1,0:T(8,128)S(1)}, u32[]{:S(2)}, u32[]{:S(2)}) %collective-permute-start.9) | collective-permute-done | bytes 262176 | tf_op jit(solution)/shard_map/ppermute | solution.py:415
  23.8 0.0 collective-permute-start.10
  23.8 0.5 %collective-permute-start.8 = (bf16[4,3,2,16,256]{4,3,2,1,0:T(8,128)(2,1)S(1)}, bf16[4,3,2,16,256]{4,3,2,1,0:T(8,128)(2,1)S(1)}, u32[]{:S(2)}, u32[]{:S(2)}) collective-permute-start(bf16[4,3,2,16,256]{4,3,2,1,0:T(8,128)(2,1)S(1)} %pad_maximum_fusion.1.refs_2_), channel_id=1, source_target_pairs={{0,1},{1,0},{2,3},{3,2},{4,5},{5,4},{6,7},{7,6},{8,9},{9,8},{10,11... | collective-permute-start | bytes 589832 | tf_op jit(solution)/shard_map/ppermute | solution.py:415
  24.3 0.6 %collective-permute-done.3.refs_0_ = bf16[4,3,2,16,256]{4,3,2,1,0:T(8,128)(2,1)S(1)} collective-permute-done((bf16[4,3,2,16,256]{4,3,2,1,0:T(8,128)(2,1)S(1)}, bf16[4,3,2,16,256]{4,3,2,1,0:T(8,128)(2,1)S(1)}, u32[]{:S(2)}, u32[]{:S(2)}) %collective-permute-start.3) | collective-permute-done | bytes 196640 | tf_op jit(solution)/shard_map/ppermute | solution.py:415
  24.9 0.0 collective-permute-start.4
  24.9 0.7 %collective-permute-done.8.refs_3_ = bf16[4,3,2,16,256]{4,3,2,1,0:T(8,128)(2,1)S(1)} collective-permute-done((bf16[4,3,2,16,256]{4,3,2,1,0:T(8,128)(2,1)S(1)}, bf16[4,3,2,16,256]{4,3,2,1,0:T(8,128)(2,1)S(1)}, u32[]{:S(2)}, u32[]{:S(2)}) %collective-permute-start.8) | collective-permute-done | bytes 196640 | tf_op jit(solution)/shard_map/ppermute | solution.py:415
  25.6 0.0 collective-permute-done.7.refs_1_
  25.6 0.0 copy-done
  25.6 0.0 copy-done.1
  25.6 1.1 %early_stage.1 = (f32[2,32,16,256]{3,2,1,0:T(8,128)S(1)}, bf16[2,32,16,256]{3,2,1,0:T(8,128)(2,1)S(1)}, f32[2,32,16,256]{3,2,1,0:T(8,128)S(1)}, f32[2,32,16,256]...) custom-call(f32[8,2,16,256]{3,2,1,0:T(8,128)S(1)} %pad_maximum_fusio, ...), custom_call_target="tpu_custom_call" | custom-call | tf_op jit(solution)/shard_map/early_stage/pallas_call | solution.py:439
  26.7 0.0 collective-permute-done.10.refs_1_
  26.7 0.8 %first_stage.1 = (f32[2,32,16,256]{3,2,1,0:T(8,128)S(1)}, bf16[2,32,16,256]{3,2,1,0:T(8,128)(2,1)S(1)}, f32[2,32,16,256]{3,2,1,0:T(8,128)S(1)}, bf16[2,512,256]{2,1,0:T(8,128)(2,1)S(1)}, f32[2,256,256]{2,1,0:T(8,128)S(1)}) custom-call(f32[8,2,16,256]{3,2,1,0:T(8,128)S(1)} %collective-permute-done.9.refs_0_, ...), custom_call_target="tpu_custom_call", output_to_operand_aliasing={{0}: (4, {}), {1}: (5, {}), {2}: (6, {})} | custom-call | tf_op jit(solution)/shard_map/first_stage/pallas_call | solution.py:442
  27.6 0.0 collective-permute-done.4.refs_1_
  27.6 2.9 %second_stage.1 = (f32[2,2,16,256]{3,2,1,0:T(8,128)}, f32[2,32,16,256]{3,2,1,0:T(8,128)S(1)}, bf16[2,32,16,256]{3,2,1,0:T(8,128)(2,1)S(1)}, f32[2,32,16,256]{3,2,1,0:T(8,128)S(1)}) custom-call(bf16[4,3,2,16,256]{4,3,2,1,0:T(8,128)(2,1)S(1)} %collective-permute-done.3.refs_0_, ...), custom_call_target="tpu_custom_call", output_to_operand_aliasing={{1}: (9, {}), {2}: (10, {}), {3}: (11, {})} | custom-call | tf_op jit(solution)/shard_map/second_stage/pallas_call | solution.py:443
  (7 shorter events, 0.1 us)
Async XLA Ops:
  0.0 7.9 %collective-permute-start = (f32[64,256]{1,0:T(8,128)}, f32[64,256]{1,0:T(8,128)S(1)}, u32[]{:S(2)}, u32[]{:S(2)}) collective-permute-start(f32[64,256]{1,0:T(8,128)} %bitcast.28), channel_id=1, source_target_pairs={{0,8},{1,9},{2,10},{3,11},{4,12},{5,13},{6,14},{7,15},{8,0},{9,1},... | collective-permute-start | bytes 196616 | tf_op jit(solution)/shard_map/ppermute | solution.py:415
  7.9 4.3 %collective-permute-start.5 = (f32[2,2,16,256]{3,2,1,0:T(8,128)S(1)}, f32[2,2,16,256]{3,2,1,0:T(8,128)S(1)}, u32[]{:S(2)}, u32[]{:S(2)}) collective-permute-start(f32[2,2,16,256]{3,2,1,0:T(8,128)S(1)} %pad_maximum_fusion.5), channel_id=1, source_target_pairs={{0,16},{1,3},{2,18},{3,1},{4,20},{5,7},{6,22},{7,5},{8,24},{9,11},... | collective-permute-start | bytes 196616 | tf_op jit(solution)/shard_map/ppermute | solution.py:415
  9.7 4.0 %collective-permute-start.1 = (bf16[2,2,16,256]{3,2,1,0:T(8,128)(2,1)S(1)}, bf16[2,2,16,256]{3,2,1,0:T(8,128)(2,1)S(1)}, u32[]{:S(2)}, u32[]{:S(2)}) collective-permute-start(bf16[2,2,16,256]{3,2,1,0:T(8,128)(2,1)S(1)} %bitcast.25), channel_id=1, source_target_pairs={{0,16},{1,17},{2,18},{3,19},{4,20},{5,21},{6,22},{7,23},{8,24},{9,... | collective-permute-start | bytes 98312 | tf_op jit(solution)/shard_map/ppermute | solution.py:415
  12.3 5.0 %collective-permute-start.6 = (f32[4,2,16,256]{3,2,1,0:T(8,128)S(1)}, f32[4,2,16,256]{3,2,1,0:T(8,128)S(1)}, u32[]{:S(2)}, u32[]{:S(2)}) collective-permute-start(f32[4,2,16,256]{3,2,1,0:T(8,128)S(1)} %pad_maximum_fusion.2), channel_id=1, source_target_pairs={{0,4},{1,5},{2,6},{3,7},{4,0},{5,1},{6,2},{7,3},{8,12},{9,13},{10,... | collective-permute-start | bytes 393224 | tf_op jit(solution)/shard_map/ppermute | solution.py:415
  13.7 5.5 %collective-permute-start.2 = (bf16[2,3,2,16,256]{4,3,2,1,0:T(8,128)(2,1)S(1)}, bf16[2,3,2,16,256]{4,3,2,1,0:T(8,128)(2,1)S(1)}, u32[]{:S(2)}, u32[]{:S(2)}) collective-permute-start(bf16[2,3,2,16,256]{4,3,2,1,0:T(8,128)(2,1)S(1)} %pad_maximum_fusion.3), channel_id=1, source_target_pairs={{0,2},{1,3},{2,0},{3,1},{4,6},{5,7},{6,4},{7,5},{8,10},{9,11},{10,... | collective-permute-start | bytes 294920 | tf_op jit(solution)/shard_map/ppermute | solution.py:415
  17.3 8.3 %copy-start = (f32[32,32]{1,0:T(8,128)S(1)}, f32[32,32]{1,0:T(8,128)}, u32[]{:S(2)}) copy-start(f32[32,32]{1,0:T(8,128)} %refs_4_.1) | copy-start | bytes 12292
  17.4 8.3 %copy-start.1 = (f32[32,32]{1,0:T(8,128)S(1)}, f32[32,32]{1,0:T(8,128)}, u32[]{:S(2)}) copy-start(f32[32,32]{1,0:T(8,128)} %refs_5_.1) | copy-start | bytes 12292
  17.4 6.4 %collective-permute-start.9 = (f32[8,2,16,256]{3,2,1,0:T(8,128)S(1)}, f32[8,2,16,256]{3,2,1,0:T(8,128)S(1)}, u32[]{:S(2)}, u32[]{:S(2)}) collective-permute-start(f32[8,2,16,256]{3,2,1,0:T(8,128)S(1)} %pad_maximum_fusion.refs_0_), channel_id=1, source_target_pairs={{0,2},{1,17},{2,0},{3,19},{4,6},{5,21},{6,4},{7,23},{8,10},{9,25},... | collective-permute-start | bytes 786440 | tf_op jit(solution)/shard_map/ppermute | solution.py:415
  19.2 5.7 %collective-permute-start.3 = (bf16[4,3,2,16,256]{4,3,2,1,0:T(8,128)(2,1)S(1)}, bf16[4,3,2,16,256]{4,3,2,1,0:T(8,128)(2,1)S(1)}, u32[]{:S(2)}, u32[]{:S(2)}) collective-permute-start(bf16[4,3,2,16,256]{4,3,2,1,0:T(8,128)(2,1)S(1)} %pad_maximum_fusion.1.refs_2_), channel_id=1, source_target_pairs={{0,4},{1,5},{2,6},{3,7},{4,0},{5,1},{6,2},{7,3},{8,12},{9,13},{10,... | collective-permute-start | bytes 589832 | tf_op jit(solution)/shard_map/ppermute | solution.py:415
  19.7 5.9 %collective-permute-start.7 = (f32[8,2,16,256]{3,2,1,0:T(8,128)S(1)}, f32[8,2,16,256]{3,2,1,0:T(8,128)S(1)}, u32[]{:S(2)}, u32[]{:S(2)}) collective-permute-start(f32[8,2,16,256]{3,2,1,0:T(8,128)S(1)} %pad_maximum_fusion.refs_0_), channel_id=1, source_target_pairs={{0,1},{1,0},{2,3},{3,2},{4,5},{5,4},{6,7},{7,6},{8,9},{9,8},{10,11... | collective-permute-start | bytes 786440 | tf_op jit(solution)/shard_map/ppermute | solution.py:415
  23.8 2.9 %collective-permute-start.10 = (f32[8,2,16,256]{3,2,1,0:T(8,128)S(1)}, f32[8,2,16,256]{3,2,1,0:T(8,128)S(1)}, u32[]{:S(2)}, u32[]{:S(2)}) collective-permute-start(f32[8,2,16,256]{3,2,1,0:T(8,128)S(1)} %collective-permute-done.9.refs_0_), channel_id=1, source_target_pairs={{0,1},{1,0},{2,3},{3,2},{4,5},{5,4},{6,7},{7,6},{8,9},{9,8},{10,11... | collective-permute-start | bytes 786440 | tf_op jit(solution)/shard_map/ppermute | solution.py:415
  23.8 1.8 %collective-permute-start.8 = (bf16[4,3,2,16,256]{4,3,2,1,0:T(8,128)(2,1)S(1)}, bf16[4,3,2,16,256]{4,3,2,1,0:T(8,128)(2,1)S(1)}, u32[]{:S(2)}, u32[]{:S(2)}) collective-permute-start(bf16[4,3,2,16,256]{4,3,2,1,0:T(8,128)(2,1)S(1)} %pad_maximum_fusion.1.refs_2_), channel_id=1, source_target_pairs={{0,1},{1,0},{2,3},{3,2},{4,5},{5,4},{6,7},{7,6},{8,9},{9,8},{10,11... | collective-permute-start | bytes 589832 | tf_op jit(solution)/shard_map/ppermute | solution.py:415
  24.9 2.6 %collective-permute-start.4 = (bf16[4,3,2,16,256]{4,3,2,1,0:T(8,128)(2,1)S(1)}, bf16[4,3,2,16,256]{4,3,2,1,0:T(8,128)(2,1)S(1)}, u32[]{:S(2)}, u32[]{:S(2)}) collective-permute-start(bf16[4,3,2,16,256]{4,3,2,1,0:T(8,128)(2,1)S(1)} %collective-permute-done.3.refs_0_), channel_id=1, source_target_pairs={{0,1},{1,0},{2,3},{3,2},{4,5},{5,4},{6,7},{7,6},{8,9},{9,8},{10,11... | collective-permute-start | bytes 589832 | tf_op jit(solution)/shard_map/ppermute | solution.py:415

commit v4 on v3

--- a/solution.py
+++ b/solution.py
@@ -235,12 +235,12 @@
 
 def take_second(sources, late, me, offsets, tp_count, stripe, table, targets):
     count = len(offsets) // 2
-    for flip in range(2):
+    for flip, (source, low_source, low_plane) in enumerate(sources):
         for plane in range(2):
-            highs = [rows_of(sources[flip][:, plane, part]) for part in range(2)]
+            highs = [rows_of(source[:, plane, part]) for part in range(2)]
             values = [high.astype(jnp.float32) for high in highs]
             if plane == 0:
-                lows = [rows_of(sources[flip][:, 2, part]) for part in range(2)]
+                lows = [rows_of(low_source[:, low_plane, part]) for part in range(2)]
                 values = [values[part] + lows[part].astype(jnp.float32) for part in range(2)]
                 turned = [turned_by(table, highs[part], lows[part]) for part in range(2)]
             else:
@@ -280,7 +280,8 @@
         )
         table_out[...] = table
         take_first(refs[:2], 0, me, offsets, stripe, table, refs[6:9])
-        take_second(refs[2:4], 0, me, second_offsets, tp_count, stripe, table, refs[9:12])
+        pieces = [(source, source, 2) for source in refs[2:4]]
+        take_second(pieces, 0, me, second_offsets, tp_count, stripe, table, refs[9:12])
 
     shapes = kept_shapes(tp_count, stripe, block_rows)
     tables = [
@@ -336,13 +337,14 @@
     scale = 0.5 * factor
 
     def kernel(*refs):
-        diagonal, last_weights, table = refs[2], refs[3], refs[4][...]
-        lows, bases, window, squares = refs[5:9]
-        out, targets, nexts, low_next = refs[12], refs[13:16], refs[16], refs[17]
+        diagonal, last_weights, table = refs[4], refs[5], refs[6][...]
+        lows, bases, window, squares = refs[7:11]
+        out, targets, nexts, low_next = refs[14], refs[15:18], refs[18], refs[19]
         ta_place = lax.axis_index("ta")
         tp_place = lax.axis_index("tp")
         me = own_place(tp_count)
-        take_second(refs[:2], 1, me, offsets, tp_count, stripe, table, targets)
+        pieces = [(refs[0], refs[1], 0), (refs[2], refs[3], 0)]
+        take_second(pieces, 1, me, offsets, tp_count, stripe, table, targets)
         second_values, second_highs, second_bases = targets
         high = [whole(second_highs, block) for block in range(2)]
 
@@ -390,9 +392,9 @@
         kernel,
         out_shape=[jax.ShapeDtypeStruct((2, 2, stripe, block_rows), jnp.float32)]
         + kept_shapes(tp_count, stripe, block_rows),
-        in_specs=in_vmem(12),
+        in_specs=in_vmem(14),
         out_specs=in_vmem(4),
-        input_output_aliases={9: 1, 10: 2, 11: 3},
+        input_output_aliases={11: 1, 12: 2, 13: 3},
         scratch_shapes=[
             pltpu.VMEM((2, 2, 2, block_rows, block_rows), jnp.float32),
             pltpu.VMEM((2, 2, block_rows, order_size), jnp.bfloat16),
@@ -420,28 +422,33 @@
     high = lax.reduce_precision(second, 8, 7)
     second = jnp.stack([high, second - high], 1).astype(jnp.bfloat16)
     first_parts = second_parts = ()
-    for first_mask, second_mask in zip(zip(*first_masks), second_masks):
+    steps = len(second_masks)
+    for step, (first_mask, second_mask) in enumerate(zip(zip(*first_masks), second_masks)):
         first_parts = [first, exchanged(first, first_mask)]
         first = jnp.concatenate(first_parts)
         if second_mask == tp_count:
             other_high = exchanged(second[:, 0], second_mask)[:, None]
             second = jnp.concatenate([second[:, :1], other_high, second[:, 1:]], 1)
         else:
-            second_parts = [second, exchanged(second, second_mask)]
-            second = jnp.concatenate(second_parts)
+            pieces = [second] if step + 1 < steps else [second[:, :2], second[:, 2:]]
+            second_parts = [second, exchanged(pieces[0], second_mask)]
+            if step + 1 == steps:
+                second_parts.append(exchanged(pieces[1], second_mask))
+            else:
+                second = jnp.concatenate(second_parts)
     first_parts += [exchanged(first_parts[0], 1)]
     first_parts += [exchanged(first_parts[1], 1)]
-    second_parts += [exchanged(second_parts[0], 1)]
-    second_parts += [exchanged(second_parts[1], 1)]
+    early_swapped = exchanged(second_parts[0], 1)
+    late_swapped = [exchanged(part, 1) for part in second_parts[1:]]
     first_masks = [[mask] + each for each in first_masks]
     second_masks = [mask] + [later for later in second_masks if later != tp_count]
     sizes = (tp_count, stripe, block_rows, factor)
     *kept, weights, last, table = early_stage(first_masks, second_masks, *sizes)(
-        *first_parts[::2], *second_parts[::2], hamiltonian, interaction
+        *first_parts[::2], second_parts[0], early_swapped, hamiltonian, interaction
     )
     _, *known = first_stage(first_masks, *sizes)(*first_parts[1::2], weights, table, *kept[:3])
     result = second_stage(second_masks, *sizes)(
-        *second_parts[1::2], weights, last, table, *known, *kept[3:]
+        *second_parts[1:], *late_swapped, weights, last, table, *known, *kept[3:]
     )
     return result[0][:, :, None]
 

time: 30.7 us -> 39.4 us (1.28)
  waiting for transfers between devices: 13.1 us -> 20.9 us
  starting transfers between devices: 11.6 us -> 12.5 us
    ppermute x11 -> x13, waiting for transfers between devices: 13.1 us -> 20.9 us  [exchanged(): lax.ppermute(block, ('ta', 'tp'), [(i, i ^ masks[i % 2]) for i in range(c...]
    ppermute x11 -> x13, starting transfers between devices: 11.6 us -> 12.5 us  [exchanged(): lax.ppermute(block, ('ta', 'tp'), [(i, i ^ masks[i % 2]) for i in range(c...]
  transfers between devices with their start and end apart: 11 -> 13, of which waited for: 7 -> 8; matrix products, arithmetic and copies ran while one was open for 3% -> 2% of each run, Pallas kernels for 6% -> 5%
where the time goes in v4:
time: 39.4 us; the launch traced here: 39.2 us
  waiting for transfers between devices  20.9 us (53%)
  starting transfers between devices  12.5 us (32%)
  Pallas kernels  4.83 us (12%)
  local copies, waits for them, and re-layouts  0.83 us (2%)
    ppermute x13, waiting for transfers between devices, exchanged(): lax.ppermute(block, ('ta', 'tp'), [(i, i ^ masks[i % 2]) for i in range(c...  20.9 us
    ppermute x13, starting transfers between devices, exchanged(): lax.ppermute(block, ('ta', 'tp'), [(i, i ^ masks[i % 2]) for i in range(c...  12.5 us
    pallas_call x1, Pallas kernels, replicated(): second_stage(second_masks, *sizes)  2.9 us
    pallas_call x1, Pallas kernels, replicated(): early_stage(first_masks, second_masks, *sizes)  1.12 us
    pallas_call x1, Pallas kernels, replicated(): first_stage(first_masks, *sizes)  0.81 us
    another operation x2, local copies, waits for them, and re-layouts, replicated(): first = jnp.stack([green[:, 0, 0], arriving[:, 0, 0]])  0.8 us
  transfers between devices with their start and end apart: 13, of which 8 were waited for; matrix products, arithmetic and copies ran while one was open for 2% of the time, Pallas kernels for 5%

profile of v4, /device:TPU:0, one launch (start us, length us, event | category | flops | bytes accessed | tf_op | source)
XLA Modules:
  0.0 39.2 jit_solution(17400113905364357905)
XLA Ops:
  0.0 4.1 %collective-permute-start = (f32[64,256]{1,0:T(8,128)}, f32[64,256]{1,0:T(8,128)S(1)}, u32[]{:S(2)}, u32[]{:S(2)}) collective-permute-start(f32[64,256]{1,0:T(8,128)} %bitcast.28), channel_id=1, source_target_pairs={{0,8},{1,9},{2,10},{3,11},{4,12},{5,13},{6,14},{7,15},{8,0},{9,1},... | collective-permute-start | bytes 196616 | tf_op jit(solution)/shard_map/ppermute | solution.py:417
  4.1 0.8 %slice_bitcast_fusion.2 = (f32[1,2,16,256]{3,2,1,0:T(8,128)S(1)}, f32[1,1,2,16,256]{4,3,2,1,0:T(8,128)S(1)}) fusion(f32[2,2,1,16,256]{4,3,2,1,0:T(8,128)} %param.3), kind=kLoop, calls=%fused_computation.11 | loop fusion | bytes 131072 | tf_op jit(solution)/shard_map/stack;squeeze | solution.py:420
  4.9 3.1 %collective-permute-done = f32[64,256]{1,0:T(8,128)S(1)} collective-permute-done((f32[64,256]{1,0:T(8,128)}, f32[64,256]{1,0:T(8,128)S(1)}, u32[]{:S(2)}, u32[]{:S(2)}) %collective-permute-start) | collective-permute-done | bytes 65568 | tf_op jit(solution)/shard_map/ppermute | solution.py:417
  7.9 1.8 %collective-permute-start.7 = (f32[2,2,16,256]{3,2,1,0:T(8,128)S(1)}, f32[2,2,16,256]{3,2,1,0:T(8,128)S(1)}, u32[]{:S(2)}, u32[]{:S(2)}) collective-permute-start(f32[2,2,16,256]{3,2,1,0:T(8,128)S(1)} %pad_maximum_fusion.5), channel_id=1, source_target_pairs={{0,16},{1,3},{2,18},{3,1},{4,20},{5,7},{6,22},{7,5},{8,24},{9,11},... | collective-permute-start | bytes 196616 | tf_op jit(solution)/shard_map/ppermute | solution.py:417
  9.7 2.6 %collective-permute-done.7 = f32[2,2,16,256]{3,2,1,0:T(8,128)S(1)} collective-permute-done((f32[2,2,16,256]{3,2,1,0:T(8,128)S(1)}, f32[2,2,16,256]{3,2,1,0:T(8,128)S(1)}, u32[]{:S(2)}, u32[]{:S(2)}) %collective-permute-start.7) | collective-permute-done | bytes 65568 | tf_op jit(solution)/shard_map/ppermute | solution.py:417
  12.3 0.7 %collective-permute-start.8 = (f32[4,2,16,256]{3,2,1,0:T(8,128)S(1)}, f32[4,2,16,256]{3,2,1,0:T(8,128)S(1)}, u32[]{:S(2)}, u32[]{:S(2)}) collective-permute-start(f32[4,2,16,256]{3,2,1,0:T(8,128)S(1)} %pad_maximum_fusion.2), channel_id=1, source_target_pairs={{0,4},{1,5},{2,6},{3,7},{4,0},{5,1},{6,2},{7,3},{8,12},{9,13},{10,... | collective-permute-start | bytes 393224 | tf_op jit(solution)/shard_map/ppermute | solution.py:417
  13.0 4.3 %collective-permute-done.8 = f32[4,2,16,256]{3,2,1,0:T(8,128)S(1)} collective-permute-done((f32[4,2,16,256]{3,2,1,0:T(8,128)S(1)}, f32[4,2,16,256]{3,2,1,0:T(8,128)S(1)}, u32[]{:S(2)}, u32[]{:S(2)}) %collective-permute-start.8) | collective-permute-done | bytes 131104 | tf_op jit(solution)/shard_map/ppermute | solution.py:417
  17.3 1.8 %collective-permute-start.11 = (f32[8,2,16,256]{3,2,1,0:T(8,128)S(1)}, f32[8,2,16,256]{3,2,1,0:T(8,128)S(1)}, u32[]{:S(2)}, u32[]{:S(2)}) collective-permute-start(f32[8,2,16,256]{3,2,1,0:T(8,128)S(1)} %pad_maximum_fusion.refs_0_), channel_id=1, source_target_pairs={{0,2},{1,17},{2,0},{3,19},{4,6},{5,21},{6,4},{7,23},{8,10},{9,25},... | collective-permute-start | bytes 786440 | tf_op jit(solution)/shard_map/ppermute | solution.py:417
  19.1 1.6 %collective-permute-start.1 = (bf16[2,2,16,256]{3,2,1,0:T(8,128)(2,1)S(1)}, bf16[2,2,16,256]{3,2,1,0:T(8,128)(2,1)S(1)}, u32[]{:S(2)}, u32[]{:S(2)}) collective-permute-start(bf16[2,2,16,256]{3,2,1,0:T(8,128)(2,1)S(1)} %bitcast.25), channel_id=1, source_target_pairs={{0,16},{1,17},{2,18},{3,19},{4,20},{5,21},{6,22},{7,23},{8,24},{9,... | collective-permute-start | bytes 98312 | tf_op jit(solution)/shard_map/ppermute | solution.py:417
  20.7 2.4 %collective-permute-done.1 = bf16[2,2,16,256]{3,2,1,0:T(8,128)(2,1)S(1)} collective-permute-done((bf16[2,2,16,256]{3,2,1,0:T(8,128)(2,1)S(1)}, bf16[2,2,16,256]{3,2,1,0:T(8,128)(2,1)S(1)}, u32[]{:S(2)}, u32[]{:S(2)}) %collective-permute-start.1) | collective-permute-done | bytes 32800 | tf_op jit(solution)/shard_map/ppermute | solution.py:417
  23.1 0.4 collective-permute-start.2
  23.5 0.0 collective-permute-start.9
  23.5 1.3 %collective-permute-done.11.refs_0_ = f32[8,2,16,256]{3,2,1,0:T(8,128)S(1)} collective-permute-done((f32[8,2,16,256]{3,2,1,0:T(8,128)S(1)}, f32[8,2,16,256]{3,2,1,0:T(8,128)S(1)}, u32[]{:S(2)}, u32[]{:S(2)}) %collective-permute-start.11) | collective-permute-done | bytes 262176 | tf_op jit(solution)/shard_map/ppermute | solution.py:417
  24.8 0.0 collective-permute-start.12
  24.8 3.0 %collective-permute-done.2 = bf16[2,3,2,16,256]{4,3,2,1,0:T(8,128)(2,1)S(1)} collective-permute-done((bf16[2,3,2,16,256]{4,3,2,1,0:T(8,128)(2,1)S(1)}, bf16[2,3,2,16,256]{4,3,2,1,0:T(8,128)(2,1)S(1)}, u32[]{:S(2)}, u32[]{:S(2)}) %collective-permute-start.2) | collective-permute-done | bytes 98336 | tf_op jit(solution)/shard_map/ppermute | solution.py:417
  27.9 0.0 copy-start
  27.9 0.0 copy-start.1
  27.9 0.5 %collective-permute-start.3 = (bf16[4,2,2,16,256]{4,3,2,1,0:T(8,128)(2,1)S(1)}, bf16[4,2,2,16,256]{4,3,2,1,0:T(8,128)(2,1)S(1)}, u32[]{:S(2)}, u32[]{:S(2)}) collective-permute-start(bf16[4,2,2,16,256]{4,3,2,1,0:T(8,128)(2,1)S(1)} %slice.34), channel_id=1, source_target_pairs={{0,4},{1,5},{2,6},{3,7},{4,0},{5,1},{6,2},{7,3},{8,12},{9,13},{10,... | collective-permute-start | bytes 393224 | tf_op jit(solution)/shard_map/ppermute | solution.py:417
  28.4 0.0 collective-permute-start.10
  28.4 1.6 %collective-permute-start.4 = (bf16[4,1,2,16,256]{4,3,2,1,0:T(8,128)(2,1)S(1)}, bf16[4,1,2,16,256]{4,3,2,1,0:T(8,128)(2,1)S(1)}, u32[]{:S(2)}, u32[]{:S(2)}) collective-permute-start(bf16[4,1,2,16,256]{4,3,2,1,0:T(8,128)(2,1)S(1)} %slice.35), channel_id=1, source_target_pairs={{0,4},{1,5},{2,6},{3,7},{4,0},{5,1},{6,2},{7,3},{8,12},{9,13},{10,... | collective-permute-start | bytes 196616 | tf_op jit(solution)/shard_map/ppermute | solution.py:417
  30.1 3.6 %collective-permute-done.3.refs_0_ = bf16[4,2,2,16,256]{4,3,2,1,0:T(8,128)(2,1)S(1)} collective-permute-done((bf16[4,2,2,16,256]{4,3,2,1,0:T(8,128)(2,1)S(1)}, bf16[4,2,2,16,256]{4,3,2,1,0:T(8,128)(2,1)S(1)}, u32[]{:S(2)}, u32[]{:S(2)}) %collective-permute-start.3) | collective-permute-done | bytes 131104 | tf_op jit(solution)/shard_map/ppermute | solution.py:417
  33.6 0.0 collective-permute-start.5
  33.6 0.7 %collective-permute-done.4.refs_1_ = bf16[4,1,2,16,256]{4,3,2,1,0:T(8,128)(2,1)S(1)} collective-permute-done((bf16[4,1,2,16,256]{4,3,2,1,0:T(8,128)(2,1)S(1)}, bf16[4,1,2,16,256]{4,3,2,1,0:T(8,128)(2,1)S(1)}, u32[]{:S(2)}, u32[]{:S(2)}) %collective-permute-start.4) | collective-permute-done | bytes 65568 | tf_op jit(solution)/shard_map/ppermute | solution.py:417
  34.3 0.0 collective-permute-start.6
  34.3 0.0 collective-permute-done.10.refs_3_
  34.3 0.0 collective-permute-done.9.refs_1_
  34.3 0.0 copy-done
  34.4 0.0 copy-done.1
  34.4 1.1 %early_stage.1 = (f32[2,32,16,256]{3,2,1,0:T(8,128)S(1)}, bf16[2,32,16,256]{3,2,1,0:T(8,128)(2,1)S(1)}, f32[2,32,16,256]{3,2,1,0:T(8,128)S(1)}, f32[2,32,16,256]...) custom-call(f32[8,2,16,256]{3,2,1,0:T(8,128)S(1)} %pad_maximum_fusio, ...), custom_call_target="tpu_custom_call" | custom-call | tf_op jit(solution)/shard_map/early_stage/pallas_call | solution.py:446
  35.5 0.0 collective-permute-done.12.refs_1_
  35.5 0.8 %first_stage.1 = (f32[2,32,16,256]{3,2,1,0:T(8,128)S(1)}, bf16[2,32,16,256]{3,2,1,0:T(8,128)(2,1)S(1)}, f32[2,32,16,256]{3,2,1,0:T(8,128)S(1)}, bf16[2,512,256]{2,1,0:T(8,128)(2,1)S(1)}, f32[2,256,256]{2,1,0:T(8,128)S(1)}) custom-call(f32[8,2,16,256]{3,2,1,0:T(8,128)S(1)} %collective-permute-done.11.refs_0, ...), custom_call_target="tpu_custom_call", output_to_operand_aliasing={{0}: (4, {}), {1}: (5, {}), {2}: (6, {})} | custom-call | tf_op jit(solution)/shard_map/first_stage/pallas_call | solution.py:449
  36.3 0.0 collective-permute-done.6.refs_3_
  36.3 0.0 collective-permute-done.5.refs_2_
  36.3 2.9 %second_stage.1 = (f32[2,2,16,256]{3,2,1,0:T(8,128)}, f32[2,32,16,256]{3,2,1,0:T(8,128)S(1)}, bf16[2,32,16,256]{3,2,1,0:T(8,128)(2,1)S(1)}, f32[2,32,16,256]{3,2,1,0:T(8,128)S(1)}) custom-call(bf16[4,2,2,16,256]{4,3,2,1,0:T(8,128)(2,1)S(1)} %collective-permute-done.3.refs_0_, ...), custom_call_target="tpu_custom_call", output_to_operand_aliasing={{1}: (11, {}), {2}: (12, {}), {3}: (13, {})} | custom-call | tf_op jit(solution)/shard_map/second_stage/pallas_call | solution.py:450
  (9 shorter events, 0.1 us)
Async XLA Ops:
  0.0 7.9 %collective-permute-start = (f32[64,256]{1,0:T(8,128)}, f32[64,256]{1,0:T(8,128)S(1)}, u32[]{:S(2)}, u32[]{:S(2)}) collective-permute-start(f32[64,256]{1,0:T(8,128)} %bitcast.28), channel_id=1, source_target_pairs={{0,8},{1,9},{2,10},{3,11},{4,12},{5,13},{6,14},{7,15},{8,0},{9,1},... | collective-permute-start | bytes 196616 | tf_op jit(solution)/shard_map/ppermute | solution.py:417
  7.9 4.3 %collective-permute-start.7 = (f32[2,2,16,256]{3,2,1,0:T(8,128)S(1)}, f32[2,2,16,256]{3,2,1,0:T(8,128)S(1)}, u32[]{:S(2)}, u32[]{:S(2)}) collective-permute-start(f32[2,2,16,256]{3,2,1,0:T(8,128)S(1)} %pad_maximum_fusion.5), channel_id=1, source_target_pairs={{0,16},{1,3},{2,18},{3,1},{4,20},{5,7},{6,22},{7,5},{8,24},{9,11},... | collective-permute-start | bytes 196616 | tf_op jit(solution)/shard_map/ppermute | solution.py:417
  12.3 5.0 %collective-permute-start.8 = (f32[4,2,16,256]{3,2,1,0:T(8,128)S(1)}, f32[4,2,16,256]{3,2,1,0:T(8,128)S(1)}, u32[]{:S(2)}, u32[]{:S(2)}) collective-permute-start(f32[4,2,16,256]{3,2,1,0:T(8,128)S(1)} %pad_maximum_fusion.2), channel_id=1, source_target_pairs={{0,4},{1,5},{2,6},{3,7},{4,0},{5,1},{6,2},{7,3},{8,12},{9,13},{10,... | collective-permute-start | bytes 393224 | tf_op jit(solution)/shard_map/ppermute | solution.py:417
  17.3 7.5 %collective-permute-start.11 = (f32[8,2,16,256]{3,2,1,0:T(8,128)S(1)}, f32[8,2,16,256]{3,2,1,0:T(8,128)S(1)}, u32[]{:S(2)}, u32[]{:S(2)}) collective-permute-start(f32[8,2,16,256]{3,2,1,0:T(8,128)S(1)} %pad_maximum_fusion.refs_0_), channel_id=1, source_target_pairs={{0,2},{1,17},{2,0},{3,19},{4,6},{5,21},{6,4},{7,23},{8,10},{9,25},... | collective-permute-start | bytes 786440 | tf_op jit(solution)/shard_map/ppermute | solution.py:417
  19.1 4.0 %collective-permute-start.1 = (bf16[2,2,16,256]{3,2,1,0:T(8,128)(2,1)S(1)}, bf16[2,2,16,256]{3,2,1,0:T(8,128)(2,1)S(1)}, u32[]{:S(2)}, u32[]{:S(2)}) collective-permute-start(bf16[2,2,16,256]{3,2,1,0:T(8,128)(2,1)S(1)} %bitcast.25), channel_id=1, source_target_pairs={{0,16},{1,17},{2,18},{3,19},{4,20},{5,21},{6,22},{7,23},{8,24},{9,... | collective-permute-start | bytes 98312 | tf_op jit(solution)/shard_map/ppermute | solution.py:417
  23.1 4.7 %collective-permute-start.2 = (bf16[2,3,2,16,256]{4,3,2,1,0:T(8,128)(2,1)S(1)}, bf16[2,3,2,16,256]{4,3,2,1,0:T(8,128)(2,1)S(1)}, u32[]{:S(2)}, u32[]{:S(2)}) collective-permute-start(bf16[2,3,2,16,256]{4,3,2,1,0:T(8,128)(2,1)S(1)} %pad_maximum_fusion.3), channel_id=1, source_target_pairs={{0,2},{1,3},{2,0},{3,1},{4,6},{5,7},{6,4},{7,5},{8,10},{9,11},{10,... | collective-permute-start | bytes 294920 | tf_op jit(solution)/shard_map/ppermute | solution.py:417
  23.5 10.8 %collective-permute-start.9 = (f32[8,2,16,256]{3,2,1,0:T(8,128)S(1)}, f32[8,2,16,256]{3,2,1,0:T(8,128)S(1)}, u32[]{:S(2)}, u32[]{:S(2)}) collective-permute-start(f32[8,2,16,256]{3,2,1,0:T(8,128)S(1)} %pad_maximum_fusion.refs_0_), channel_id=1, source_target_pairs={{0,1},{1,0},{2,3},{3,2},{4,5},{5,4},{6,7},{7,6},{8,9},{9,8},{10,11... | collective-permute-start | bytes 786440 | tf_op jit(solution)/shard_map/ppermute | solution.py:417
  24.8 10.7 %collective-permute-start.12 = (f32[8,2,16,256]{3,2,1,0:T(8,128)S(1)}, f32[8,2,16,256]{3,2,1,0:T(8,128)S(1)}, u32[]{:S(2)}, u32[]{:S(2)}) collective-permute-start(f32[8,2,16,256]{3,2,1,0:T(8,128)S(1)} %collective-permute-done.11.refs_0_), channel_id=1, source_target_pairs={{0,1},{1,0},{2,3},{3,2},{4,5},{5,4},{6,7},{7,6},{8,9},{9,8},{10,11... | collective-permute-start | bytes 786440 | tf_op jit(solution)/shard_map/ppermute | solution.py:417
  27.9 6.5 %copy-start = (f32[32,32]{1,0:T(8,128)S(1)}, f32[32,32]{1,0:T(8,128)}, u32[]{:S(2)}) copy-start(f32[32,32]{1,0:T(8,128)} %refs_4_.1) | copy-start | bytes 12292
  27.9 6.5 %copy-start.1 = (f32[32,32]{1,0:T(8,128)S(1)}, f32[32,32]{1,0:T(8,128)}, u32[]{:S(2)}) copy-start(f32[32,32]{1,0:T(8,128)} %refs_5_.1) | copy-start | bytes 12292
  27.9 5.7 %collective-permute-start.3 = (bf16[4,2,2,16,256]{4,3,2,1,0:T(8,128)(2,1)S(1)}, bf16[4,2,2,16,256]{4,3,2,1,0:T(8,128)(2,1)S(1)}, u32[]{:S(2)}, u32[]{:S(2)}) collective-permute-start(bf16[4,2,2,16,256]{4,3,2,1,0:T(8,128)(2,1)S(1)} %slice.34), channel_id=1, source_target_pairs={{0,4},{1,5},{2,6},{3,7},{4,0},{5,1},{6,2},{7,3},{8,12},{9,13},{10,... | collective-permute-start | bytes 393224 | tf_op jit(solution)/shard_map/ppermute | solution.py:417
  28.4 5.9 %collective-permute-start.10 = (bf16[4,3,2,16,256]{4,3,2,1,0:T(8,128)(2,1)S(1)}, bf16[4,3,2,16,256]{4,3,2,1,0:T(8,128)(2,1)S(1)}, u32[]{:S(2)}, u32[]{:S(2)}) collective-permute-start(bf16[4,3,2,16,256]{4,3,2,1,0:T(8,128)(2,1)S(1)} %pad_maximum_fusion.1.refs_2_), channel_id=1, source_target_pairs={{0,1},{1,0},{2,3},{3,2},{4,5},{5,4},{6,7},{7,6},{8,9},{9,8},{10,11... | collective-permute-start | bytes 589832 | tf_op jit(solution)/shard_map/ppermute | solution.py:417
  28.4 5.9 %collective-permute-start.4 = (bf16[4,1,2,16,256]{4,3,2,1,0:T(8,128)(2,1)S(1)}, bf16[4,1,2,16,256]{4,3,2,1,0:T(8,128)(2,1)S(1)}, u32[]{:S(2)}, u32[]{:S(2)}) collective-permute-start(bf16[4,1,2,16,256]{4,3,2,1,0:T(8,128)(2,1)S(1)} %slice.35), channel_id=1, source_target_pairs={{0,4},{1,5},{2,6},{3,7},{4,0},{5,1},{6,2},{7,3},{8,12},{9,13},{10,... | collective-permute-start | bytes 196616 | tf_op jit(solution)/shard_map/ppermute | solution.py:417
  33.6 2.7 %collective-permute-start.5 = (bf16[4,2,2,16,256]{4,3,2,1,0:T(8,128)(2,1)S(1)}, bf16[4,2,2,16,256]{4,3,2,1,0:T(8,128)(2,1)S(1)}, u32[]{:S(2)}, u32[]{:S(2)}) collective-permute-start(bf16[4,2,2,16,256]{4,3,2,1,0:T(8,128)(2,1)S(1)} %collective-permute-done.3.refs_0_), channel_id=1, source_target_pairs={{0,1},{1,0},{2,3},{3,2},{4,5},{5,4},{6,7},{7,6},{8,9},{9,8},{10,11... | collective-permute-start | bytes 393224 | tf_op jit(solution)/shard_map/ppermute | solution.py:417
  34.3 2.0 %collective-permute-start.6 = (bf16[4,1,2,16,256]{4,3,2,1,0:T(8,128)(2,1)S(1)}, bf16[4,1,2,16,256]{4,3,2,1,0:T(8,128)(2,1)S(1)}, u32[]{:S(2)}, u32[]{:S(2)}) collective-permute-start(bf16[4,1,2,16,256]{4,3,2,1,0:T(8,128)(2,1)S(1)} %collective-permute-done.4.refs_1_), channel_id=1, source_target_pairs={{0,1},{1,0},{2,3},{3,2},{4,5},{5,4},{6,7},{7,6},{8,9},{9,8},{10,11... | collective-permute-start | bytes 196616 | tf_op jit(solution)/shard_map/ppermute | solution.py:417

commit v5 on v3

--- a/solution.py
+++ b/solution.py
@@ -235,12 +235,12 @@
 
 def take_second(sources, late, me, offsets, tp_count, stripe, table, targets):
     count = len(offsets) // 2
-    for flip in range(2):
+    for flip, source in sources:
         for plane in range(2):
-            highs = [rows_of(sources[flip][:, plane, part]) for part in range(2)]
+            highs = [rows_of(source[:, plane, part]) for part in range(2)]
             values = [high.astype(jnp.float32) for high in highs]
             if plane == 0:
-                lows = [rows_of(sources[flip][:, 2, part]) for part in range(2)]
+                lows = [rows_of(source[:, 2, part]) for part in range(2)]
                 values = [values[part] + lows[part].astype(jnp.float32) for part in range(2)]
                 turned = [turned_by(table, highs[part], lows[part]) for part in range(2)]
             else:
@@ -280,7 +280,7 @@
         )
         table_out[...] = table
         take_first(refs[:2], 0, me, offsets, stripe, table, refs[6:9])
-        take_second(refs[2:4], 0, me, second_offsets, tp_count, stripe, table, refs[9:12])
+        take_second(enumerate(refs[2:4]), 0, me, second_offsets, tp_count, stripe, table, refs[9:12])
 
     shapes = kept_shapes(tp_count, stripe, block_rows)
     tables = [
@@ -298,14 +298,19 @@
     )
 
 
-def first_stage(masks, tp_count, stripe, block_rows, factor):
+def first_stage(masks, second_masks, tp_count, stripe, block_rows, factor):
     offsets = [offsets_of(each) for each in masks]
+    second_offsets = offsets_of(second_masks)
     scale = 0.5 * factor
 
     def kernel(*refs):
         weights, table = refs[2], refs[3][...]
-        targets, window, squares = refs[7:10], refs[10], refs[11]
-        take_first(refs[:2], 1, own_place(tp_count), offsets, stripe, table, targets)
+        me = own_place(tp_count)
+        targets, window, squares = refs[11:14], refs[17], refs[18]
+        take_second(
+            [(0, refs[7])], 1, me, second_offsets, tp_count, stripe, table, refs[14:17]
+        )
+        take_first(refs[:2], 1, me, offsets, stripe, table, targets)
         values, highs, bases = targets
         high = whole(highs, 0)
         made = window_of(squares_of(whole(values, 0), weights[1]), mirrored(high))
@@ -320,11 +325,11 @@
     square = jax.ShapeDtypeStruct((2, 2 * block_rows, block_rows), jnp.bfloat16)
     return pl.pallas_call(
         kernel,
-        out_shape=kept_shapes(tp_count, stripe, block_rows)
+        out_shape=kept_shapes(tp_count, stripe, block_rows) * 2
         + [square, jax.ShapeDtypeStruct((2, block_rows, block_rows), jnp.float32)],
-        in_specs=in_vmem(7),
-        out_specs=in_vmem(5),
-        input_output_aliases={4: 0, 5: 1, 6: 2},
+        in_specs=in_vmem(11),
+        out_specs=in_vmem(8),
+        input_output_aliases={4: 0, 5: 1, 6: 2, 8: 3, 9: 4, 10: 5},
         compiler_params=pltpu.CompilerParams(vmem_limit_bytes=16 << 20),
         name="first_stage",
     )
@@ -336,13 +341,13 @@
     scale = 0.5 * factor
 
     def kernel(*refs):
-        diagonal, last_weights, table = refs[2], refs[3], refs[4][...]
-        lows, bases, window, squares = refs[5:9]
-        out, targets, nexts, low_next = refs[12], refs[13:16], refs[16], refs[17]
+        diagonal, last_weights, table = refs[1], refs[2], refs[3][...]
+        lows, bases, window, squares = refs[4:8]
+        out, targets, nexts, low_next = refs[11], refs[12:15], refs[15], refs[16]
         ta_place = lax.axis_index("ta")
         tp_place = lax.axis_index("tp")
         me = own_place(tp_count)
-        take_second(refs[:2], 1, me, offsets, tp_count, stripe, table, targets)
+        take_second([(1, refs[0])], 1, me, offsets, tp_count, stripe, table, targets)
         second_values, second_highs, second_bases = targets
         high = [whole(second_highs, block) for block in range(2)]
 
@@ -390,9 +395,9 @@
         kernel,
         out_shape=[jax.ShapeDtypeStruct((2, 2, stripe, block_rows), jnp.float32)]
         + kept_shapes(tp_count, stripe, block_rows),
-        in_specs=in_vmem(12),
+        in_specs=in_vmem(11),
         out_specs=in_vmem(4),
-        input_output_aliases={9: 1, 10: 2, 11: 3},
+        input_output_aliases={8: 1, 9: 2, 10: 3},
         scratch_shapes=[
             pltpu.VMEM((2, 2, 2, block_rows, block_rows), jnp.float32),
             pltpu.VMEM((2, 2, block_rows, order_size), jnp.bfloat16),
@@ -439,9 +444,11 @@
     *kept, weights, last, table = early_stage(first_masks, second_masks, *sizes)(
         *first_parts[::2], *second_parts[::2], hamiltonian, interaction
     )
-    _, *known = first_stage(first_masks, *sizes)(*first_parts[1::2], weights, table, *kept[:3])
+    known = first_stage(first_masks, second_masks, *sizes)(
+        *first_parts[1::2], weights, table, *kept[:3], second_parts[1], *kept[3:]
+    )
     result = second_stage(second_masks, *sizes)(
-        *second_parts[1::2], weights, last, table, *known, *kept[3:]
+        second_parts[3], weights, last, table, *known[1:3], *known[6:], *known[3:6]
     )
     return result[0][:, :, None]
 

time: 30.7 us -> 30.6 us (level)
  transfers between devices with their start and end apart: 11 -> 11, of which waited for: 7 -> 7; matrix products, arithmetic and copies ran while one was open for 3% -> 3% of each run, Pallas kernels for 6% -> 7%
where the time goes in v5:
time: 30.6 us; the launch traced here: 30.5 us
  waiting for transfers between devices  13.1 us (43%)
  starting transfers between devices  11.6 us (38%)
  Pallas kernels  4.82 us (16%)
  local copies, waits for them, and re-layouts  0.82 us (3%)
    ppermute x11, waiting for transfers between devices, exchanged(): lax.ppermute(block, ('ta', 'tp'), [(i, i ^ masks[i % 2]) for i in range(c...  13.1 us
    ppermute x11, starting transfers between devices, exchanged(): lax.ppermute(block, ('ta', 'tp'), [(i, i ^ masks[i % 2]) for i in range(c...  11.6 us
    pallas_call x1, Pallas kernels, replicated(): second_stage(second_masks, *sizes)  2.65 us
    pallas_call x1, Pallas kernels, replicated(): early_stage(first_masks, second_masks, *sizes)  1.11 us
    pallas_call x1, Pallas kernels, replicated(): first_stage(first_masks, second_masks, *sizes)  1.05 us
    another operation x2, local copies, waits for them, and re-layouts, replicated(): first = jnp.stack([green[:, 0, 0], arriving[:, 0, 0]])  0.8 us
  transfers between devices with their start and end apart: 11, of which 7 were waited for; matrix products, arithmetic and copies ran while one was open for 3% of the time, Pallas kernels for 7%

profile of v5, /device:TPU:0, one launch (start us, length us, event | category | flops | bytes accessed | tf_op | source)
XLA Modules:
  0.0 30.5 jit_solution(8199390813650820172)
XLA Ops:
  0.0 4.1 %collective-permute-start = (f32[64,256]{1,0:T(8,128)}, f32[64,256]{1,0:T(8,128)S(1)}, u32[]{:S(2)}, u32[]{:S(2)}) collective-permute-start(f32[64,256]{1,0:T(8,128)} %bitcast.28), channel_id=1, source_target_pairs={{0,8},{1,9},{2,10},{3,11},{4,12},{5,13},{6,14},{7,15},{8,0},{9,1},... | collective-permute-start | bytes 196616 | tf_op jit(solution)/shard_map/ppermute | solution.py:420
  4.1 0.8 %slice_bitcast_fusion.2 = (f32[1,2,16,256]{3,2,1,0:T(8,128)S(1)}, f32[1,1,2,16,256]{4,3,2,1,0:T(8,128)S(1)}) fusion(f32[2,2,1,16,256]{4,3,2,1,0:T(8,128)} %param.3), kind=kLoop, calls=%fused_computation.11 | loop fusion | bytes 131072 | tf_op jit(solution)/shard_map/stack;squeeze | solution.py:423
  4.9 3.1 %collective-permute-done = f32[64,256]{1,0:T(8,128)S(1)} collective-permute-done((f32[64,256]{1,0:T(8,128)}, f32[64,256]{1,0:T(8,128)S(1)}, u32[]{:S(2)}, u32[]{:S(2)}) %collective-permute-start) | collective-permute-done | bytes 65568 | tf_op jit(solution)/shard_map/ppermute | solution.py:420
  7.9 1.8 %collective-permute-start.5 = (f32[2,2,16,256]{3,2,1,0:T(8,128)S(1)}, f32[2,2,16,256]{3,2,1,0:T(8,128)S(1)}, u32[]{:S(2)}, u32[]{:S(2)}) collective-permute-start(f32[2,2,16,256]{3,2,1,0:T(8,128)S(1)} %pad_maximum_fusion.5), channel_id=1, source_target_pairs={{0,16},{1,3},{2,18},{3,1},{4,20},{5,7},{6,22},{7,5},{8,24},{9,11},... | collective-permute-start | bytes 196616 | tf_op jit(solution)/shard_map/ppermute | solution.py:420
  9.7 0.4 %collective-permute-start.1 = (bf16[2,2,16,256]{3,2,1,0:T(8,128)(2,1)S(1)}, bf16[2,2,16,256]{3,2,1,0:T(8,128)(2,1)S(1)}, u32[]{:S(2)}, u32[]{:S(2)}) collective-permute-start(bf16[2,2,16,256]{3,2,1,0:T(8,128)(2,1)S(1)} %bitcast.25), channel_id=1, source_target_pairs={{0,16},{1,17},{2,18},{3,19},{4,20},{5,21},{6,22},{7,23},{8,24},{9,... | collective-permute-start | bytes 98312 | tf_op jit(solution)/shard_map/ppermute | solution.py:420
  10.1 2.2 %collective-permute-done.5 = f32[2,2,16,256]{3,2,1,0:T(8,128)S(1)} collective-permute-done((f32[2,2,16,256]{3,2,1,0:T(8,128)S(1)}, f32[2,2,16,256]{3,2,1,0:T(8,128)S(1)}, u32[]{:S(2)}, u32[]{:S(2)}) %collective-permute-start.5) | collective-permute-done | bytes 65568 | tf_op jit(solution)/shard_map/ppermute | solution.py:420
  12.3 1.0 %collective-permute-start.6 = (f32[4,2,16,256]{3,2,1,0:T(8,128)S(1)}, f32[4,2,16,256]{3,2,1,0:T(8,128)S(1)}, u32[]{:S(2)}, u32[]{:S(2)}) collective-permute-start(f32[4,2,16,256]{3,2,1,0:T(8,128)S(1)} %pad_maximum_fusion.2), channel_id=1, source_target_pairs={{0,4},{1,5},{2,6},{3,7},{4,0},{5,1},{6,2},{7,3},{8,12},{9,13},{10,... | collective-permute-start | bytes 393224 | tf_op jit(solution)/shard_map/ppermute | solution.py:420
  13.3 0.4 %collective-permute-done.1 = bf16[2,2,16,256]{3,2,1,0:T(8,128)(2,1)S(1)} collective-permute-done((bf16[2,2,16,256]{3,2,1,0:T(8,128)(2,1)S(1)}, bf16[2,2,16,256]{3,2,1,0:T(8,128)(2,1)S(1)}, u32[]{:S(2)}, u32[]{:S(2)}) %collective-permute-start.1) | collective-permute-done | bytes 32800 | tf_op jit(solution)/shard_map/ppermute | solution.py:420
  13.7 1.6 %collective-permute-start.2 = (bf16[2,3,2,16,256]{4,3,2,1,0:T(8,128)(2,1)S(1)}, bf16[2,3,2,16,256]{4,3,2,1,0:T(8,128)(2,1)S(1)}, u32[]{:S(2)}, u32[]{:S(2)}) collective-permute-start(bf16[2,3,2,16,256]{4,3,2,1,0:T(8,128)(2,1)S(1)} %pad_maximum_fusion.3), channel_id=1, source_target_pairs={{0,2},{1,3},{2,0},{3,1},{4,6},{5,7},{6,4},{7,5},{8,10},{9,11},{10,... | collective-permute-start | bytes 294920 | tf_op jit(solution)/shard_map/ppermute | solution.py:420
  15.3 2.0 %collective-permute-done.6 = f32[4,2,16,256]{3,2,1,0:T(8,128)S(1)} collective-permute-done((f32[4,2,16,256]{3,2,1,0:T(8,128)S(1)}, f32[4,2,16,256]{3,2,1,0:T(8,128)S(1)}, u32[]{:S(2)}, u32[]{:S(2)}) %collective-permute-start.6) | collective-permute-done | bytes 131104 | tf_op jit(solution)/shard_map/ppermute | solution.py:420
  17.3 0.0 copy-start
  17.4 0.0 copy-start.1
  17.4 1.8 %collective-permute-start.9 = (f32[8,2,16,256]{3,2,1,0:T(8,128)S(1)}, f32[8,2,16,256]{3,2,1,0:T(8,128)S(1)}, u32[]{:S(2)}, u32[]{:S(2)}) collective-permute-start(f32[8,2,16,256]{3,2,1,0:T(8,128)S(1)} %pad_maximum_fusion.refs_0_), channel_id=1, source_target_pairs={{0,2},{1,17},{2,0},{3,19},{4,6},{5,21},{6,4},{7,23},{8,10},{9,25},... | collective-permute-start | bytes 786440 | tf_op jit(solution)/shard_map/ppermute | solution.py:420
  19.2 0.0 collective-permute-done.2
  19.2 0.5 %collective-permute-start.3 = (bf16[4,3,2,16,256]{4,3,2,1,0:T(8,128)(2,1)S(1)}, bf16[4,3,2,16,256]{4,3,2,1,0:T(8,128)(2,1)S(1)}, u32[]{:S(2)}, u32[]{:S(2)}) collective-permute-start(bf16[4,3,2,16,256]{4,3,2,1,0:T(8,128)(2,1)S(1)} %pad_maximum_fusion.1.refs_2_), channel_id=1, source_target_pairs={{0,4},{1,5},{2,6},{3,7},{4,0},{5,1},{6,2},{7,3},{8,12},{9,13},{10,... | collective-permute-start | bytes 589832 | tf_op jit(solution)/shard_map/ppermute | solution.py:420
  19.7 0.0 collective-permute-start.7
  19.7 4.1 %collective-permute-done.9.refs_0_ = f32[8,2,16,256]{3,2,1,0:T(8,128)S(1)} collective-permute-done((f32[8,2,16,256]{3,2,1,0:T(8,128)S(1)}, f32[8,2,16,256]{3,2,1,0:T(8,128)S(1)}, u32[]{:S(2)}, u32[]{:S(2)}) %collective-permute-start.9) | collective-permute-done | bytes 262176 | tf_op jit(solution)/shard_map/ppermute | solution.py:420
  23.8 0.0 collective-permute-start.10
  23.8 0.5 %collective-permute-start.8 = (bf16[4,3,2,16,256]{4,3,2,1,0:T(8,128)(2,1)S(1)}, bf16[4,3,2,16,256]{4,3,2,1,0:T(8,128)(2,1)S(1)}, u32[]{:S(2)}, u32[]{:S(2)}) collective-permute-start(bf16[4,3,2,16,256]{4,3,2,1,0:T(8,128)(2,1)S(1)} %pad_maximum_fusion.1.refs_2_), channel_id=1, source_target_pairs={{0,1},{1,0},{2,3},{3,2},{4,5},{5,4},{6,7},{7,6},{8,9},{9,8},{10,11... | collective-permute-start | bytes 589832 | tf_op jit(solution)/shard_map/ppermute | solution.py:420
  24.3 0.6 %collective-permute-done.3.refs_7_ = bf16[4,3,2,16,256]{4,3,2,1,0:T(8,128)(2,1)S(1)} collective-permute-done((bf16[4,3,2,16,256]{4,3,2,1,0:T(8,128)(2,1)S(1)}, bf16[4,3,2,16,256]{4,3,2,1,0:T(8,128)(2,1)S(1)}, u32[]{:S(2)}, u32[]{:S(2)}) %collective-permute-start.3) | collective-permute-done | bytes 196640 | tf_op jit(solution)/shard_map/ppermute | solution.py:420
  24.9 0.0 collective-permute-start.4
  24.9 0.7 %collective-permute-done.8.refs_3_ = bf16[4,3,2,16,256]{4,3,2,1,0:T(8,128)(2,1)S(1)} collective-permute-done((bf16[4,3,2,16,256]{4,3,2,1,0:T(8,128)(2,1)S(1)}, bf16[4,3,2,16,256]{4,3,2,1,0:T(8,128)(2,1)S(1)}, u32[]{:S(2)}, u32[]{:S(2)}) %collective-permute-start.8) | collective-permute-done | bytes 196640 | tf_op jit(solution)/shard_map/ppermute | solution.py:420
  25.6 0.0 collective-permute-done.7.refs_1_
  25.6 0.0 copy-done
  25.6 0.0 copy-done.1
  25.6 1.1 %early_stage.1 = (f32[2,32,16,256]{3,2,1,0:T(8,128)S(1)}, bf16[2,32,16,256]{3,2,1,0:T(8,128)(2,1)S(1)}, f32[2,32,16,256]{3,2,1,0:T(8,128)S(1)}, f32[2,32,16,256]...) custom-call(f32[8,2,16,256]{3,2,1,0:T(8,128)S(1)} %pad_maximum_fusio, ...), custom_call_target="tpu_custom_call" | custom-call | tf_op jit(solution)/shard_map/early_stage/pallas_call | solution.py:444
  26.7 0.0 collective-permute-done.10.refs_1_
  26.7 1.1 %first_stage.1 = (f32[2,32,16,256]{3,2,1,0:T(8,128)S(1)}, bf16[2,32,16,256]{3,2,1,0:T(8,128)(2,1)S(1)}, f32[2,32,16,256]{3,2,1,0:T(8,128)S(1)}, f32[2,32,16,256]...) custom-call(f32[8,2,16,256]{3,2,1,0:T(8,128)S(1)} %collective-permut, ...), custom_call_target="tpu_custom_call", output_to_operand_aliasing={{0}: (4, {}), {1}: (5, {}), {2}: (6, {}), {3}: (8, {}), {4}... | custom-call | tf_op jit(solution)/shard_map/first_stage/pallas_call | solution.py:447
  27.8 0.0 collective-permute-done.4.refs_0_
  27.8 2.7 %second_stage.1 = (f32[2,2,16,256]{3,2,1,0:T(8,128)}, f32[2,32,16,256]{3,2,1,0:T(8,128)S(1)}, bf16[2,32,16,256]{3,2,1,0:T(8,128)(2,1)S(1)}, f32[2,32,16,256]{3,2,1,0:T(8,128)S(1)}) custom-call(bf16[4,3,2,16,256]{4,3,2,1,0:T(8,128)(2,1)S(1)} %collective-permute-done.4.refs_0_, ...), custom_call_target="tpu_custom_call", output_to_operand_aliasing={{1}: (8, {}), {2}: (9, {}), {3}: (10, {})} | custom-call | tf_op jit(solution)/shard_map/second_stage/pallas_call | solution.py:450
  (7 shorter events, 0.1 us)
Async XLA Ops:
  0.0 7.9 %collective-permute-start = (f32[64,256]{1,0:T(8,128)}, f32[64,256]{1,0:T(8,128)S(1)}, u32[]{:S(2)}, u32[]{:S(2)}) collective-permute-start(f32[64,256]{1,0:T(8,128)} %bitcast.28), channel_id=1, source_target_pairs={{0,8},{1,9},{2,10},{3,11},{4,12},{5,13},{6,14},{7,15},{8,0},{9,1},... | collective-permute-start | bytes 196616 | tf_op jit(solution)/shard_map/ppermute | solution.py:420
  7.9 4.3 %collective-permute-start.5 = (f32[2,2,16,256]{3,2,1,0:T(8,128)S(1)}, f32[2,2,16,256]{3,2,1,0:T(8,128)S(1)}, u32[]{:S(2)}, u32[]{:S(2)}) collective-permute-start(f32[2,2,16,256]{3,2,1,0:T(8,128)S(1)} %pad_maximum_fusion.5), channel_id=1, source_target_pairs={{0,16},{1,3},{2,18},{3,1},{4,20},{5,7},{6,22},{7,5},{8,24},{9,11},... | collective-permute-start | bytes 196616 | tf_op jit(solution)/shard_map/ppermute | solution.py:420
  9.7 4.0 %collective-permute-start.1 = (bf16[2,2,16,256]{3,2,1,0:T(8,128)(2,1)S(1)}, bf16[2,2,16,256]{3,2,1,0:T(8,128)(2,1)S(1)}, u32[]{:S(2)}, u32[]{:S(2)}) collective-permute-start(bf16[2,2,16,256]{3,2,1,0:T(8,128)(2,1)S(1)} %bitcast.25), channel_id=1, source_target_pairs={{0,16},{1,17},{2,18},{3,19},{4,20},{5,21},{6,22},{7,23},{8,24},{9,... | collective-permute-start | bytes 98312 | tf_op jit(solution)/shard_map/ppermute | solution.py:420
  12.3 5.0 %collective-permute-start.6 = (f32[4,2,16,256]{3,2,1,0:T(8,128)S(1)}, f32[4,2,16,256]{3,2,1,0:T(8,128)S(1)}, u32[]{:S(2)}, u32[]{:S(2)}) collective-permute-start(f32[4,2,16,256]{3,2,1,0:T(8,128)S(1)} %pad_maximum_fusion.2), channel_id=1, source_target_pairs={{0,4},{1,5},{2,6},{3,7},{4,0},{5,1},{6,2},{7,3},{8,12},{9,13},{10,... | collective-permute-start | bytes 393224 | tf_op jit(solution)/shard_map/ppermute | solution.py:420
  13.7 5.5 %collective-permute-start.2 = (bf16[2,3,2,16,256]{4,3,2,1,0:T(8,128)(2,1)S(1)}, bf16[2,3,2,16,256]{4,3,2,1,0:T(8,128)(2,1)S(1)}, u32[]{:S(2)}, u32[]{:S(2)}) collective-permute-start(bf16[2,3,2,16,256]{4,3,2,1,0:T(8,128)(2,1)S(1)} %pad_maximum_fusion.3), channel_id=1, source_target_pairs={{0,2},{1,3},{2,0},{3,1},{4,6},{5,7},{6,4},{7,5},{8,10},{9,11},{10,... | collective-permute-start | bytes 294920 | tf_op jit(solution)/shard_map/ppermute | solution.py:420
  17.3 8.3 %copy-start = (f32[32,32]{1,0:T(8,128)S(1)}, f32[32,32]{1,0:T(8,128)}, u32[]{:S(2)}) copy-start(f32[32,32]{1,0:T(8,128)} %refs_4_.1) | copy-start | bytes 12292
  17.4 8.3 %copy-start.1 = (f32[32,32]{1,0:T(8,128)S(1)}, f32[32,32]{1,0:T(8,128)}, u32[]{:S(2)}) copy-start(f32[32,32]{1,0:T(8,128)} %refs_5_.1) | copy-start | bytes 12292
  17.4 6.4 %collective-permute-start.9 = (f32[8,2,16,256]{3,2,1,0:T(8,128)S(1)}, f32[8,2,16,256]{3,2,1,0:T(8,128)S(1)}, u32[]{:S(2)}, u32[]{:S(2)}) collective-permute-start(f32[8,2,16,256]{3,2,1,0:T(8,128)S(1)} %pad_maximum_fusion.refs_0_), channel_id=1, source_target_pairs={{0,2},{1,17},{2,0},{3,19},{4,6},{5,21},{6,4},{7,23},{8,10},{9,25},... | collective-permute-start | bytes 786440 | tf_op jit(solution)/shard_map/ppermute | solution.py:420
  19.2 5.7 %collective-permute-start.3 = (bf16[4,3,2,16,256]{4,3,2,1,0:T(8,128)(2,1)S(1)}, bf16[4,3,2,16,256]{4,3,2,1,0:T(8,128)(2,1)S(1)}, u32[]{:S(2)}, u32[]{:S(2)}) collective-permute-start(bf16[4,3,2,16,256]{4,3,2,1,0:T(8,128)(2,1)S(1)} %pad_maximum_fusion.1.refs_2_), channel_id=1, source_target_pairs={{0,4},{1,5},{2,6},{3,7},{4,0},{5,1},{6,2},{7,3},{8,12},{9,13},{10,... | collective-permute-start | bytes 589832 | tf_op jit(solution)/shard_map/ppermute | solution.py:420
  19.7 5.9 %collective-permute-start.7 = (f32[8,2,16,256]{3,2,1,0:T(8,128)S(1)}, f32[8,2,16,256]{3,2,1,0:T(8,128)S(1)}, u32[]{:S(2)}, u32[]{:S(2)}) collective-permute-start(f32[8,2,16,256]{3,2,1,0:T(8,128)S(1)} %pad_maximum_fusion.refs_0_), channel_id=1, source_target_pairs={{0,1},{1,0},{2,3},{3,2},{4,5},{5,4},{6,7},{7,6},{8,9},{9,8},{10,11... | collective-permute-start | bytes 786440 | tf_op jit(solution)/shard_map/ppermute | solution.py:420
  23.8 2.9 %collective-permute-start.10 = (f32[8,2,16,256]{3,2,1,0:T(8,128)S(1)}, f32[8,2,16,256]{3,2,1,0:T(8,128)S(1)}, u32[]{:S(2)}, u32[]{:S(2)}) collective-permute-start(f32[8,2,16,256]{3,2,1,0:T(8,128)S(1)} %collective-permute-done.9.refs_0_), channel_id=1, source_target_pairs={{0,1},{1,0},{2,3},{3,2},{4,5},{5,4},{6,7},{7,6},{8,9},{9,8},{10,11... | collective-permute-start | bytes 786440 | tf_op jit(solution)/shard_map/ppermute | solution.py:420
  23.8 1.8 %collective-permute-start.8 = (bf16[4,3,2,16,256]{4,3,2,1,0:T(8,128)(2,1)S(1)}, bf16[4,3,2,16,256]{4,3,2,1,0:T(8,128)(2,1)S(1)}, u32[]{:S(2)}, u32[]{:S(2)}) collective-permute-start(bf16[4,3,2,16,256]{4,3,2,1,0:T(8,128)(2,1)S(1)} %pad_maximum_fusion.1.refs_2_), channel_id=1, source_target_pairs={{0,1},{1,0},{2,3},{3,2},{4,5},{5,4},{6,7},{7,6},{8,9},{9,8},{10,11... | collective-permute-start | bytes 589832 | tf_op jit(solution)/shard_map/ppermute | solution.py:420
  24.9 2.9 %collective-permute-start.4 = (bf16[4,3,2,16,256]{4,3,2,1,0:T(8,128)(2,1)S(1)}, bf16[4,3,2,16,256]{4,3,2,1,0:T(8,128)(2,1)S(1)}, u32[]{:S(2)}, u32[]{:S(2)}) collective-permute-start(bf16[4,3,2,16,256]{4,3,2,1,0:T(8,128)(2,1)S(1)} %collective-permute-done.3.refs_7_), channel_id=1, source_target_pairs={{0,1},{1,0},{2,3},{3,2},{4,5},{5,4},{6,7},{7,6},{8,9},{9,8},{10,11... | collective-permute-start | bytes 589832 | tf_op jit(solution)/shard_map/ppermute | solution.py:420

commit v6 on v5

--- a/solution.py
+++ b/solution.py
@@ -222,8 +222,8 @@
 
 def take_first(sources, late, me, offsets, stripe, table, targets):
     count = len(offsets[0]) // 2
-    for flip in range(2):
-        values = [rows_of(sources[flip][:, part]) for part in range(2)]
+    for flip, source in sources:
+        values = [rows_of(source[:, part]) for part in range(2)]
         split = [halves(part) for part in values]
         base = started(values, [turned_by(table, high, low) for high, low in split])
         highs = [high for high, _ in split]
@@ -279,7 +279,7 @@
             jnp.concatenate([weights] * 2), lax.axis_index("ta") * (block_rows // NO)
         )
         table_out[...] = table
-        take_first(refs[:2], 0, me, offsets, stripe, table, refs[6:9])
+        take_first(enumerate(refs[:2]), 0, me, offsets, stripe, table, refs[6:9])
         take_second(enumerate(refs[2:4]), 0, me, second_offsets, tp_count, stripe, table, refs[9:12])
 
     shapes = kept_shapes(tp_count, stripe, block_rows)
@@ -298,19 +298,37 @@
     )
 
 
+def near_stage(masks, tp_count, stripe, block_rows, factor):
+    offsets = [offsets_of(each) for each in masks]
+
+    def kernel(*refs):
+        table = refs[1][...]
+        take_first([(0, refs[0])], 1, own_place(tp_count), offsets, stripe, table, refs[5:])
+
+    return pl.pallas_call(
+        kernel,
+        out_shape=kept_shapes(tp_count, stripe, block_rows),
+        in_specs=in_vmem(5),
+        out_specs=in_vmem(3),
+        input_output_aliases={2: 0, 3: 1, 4: 2},
+        compiler_params=pltpu.CompilerParams(vmem_limit_bytes=16 << 20),
+        name="near_stage",
+    )
+
+
 def first_stage(masks, second_masks, tp_count, stripe, block_rows, factor):
     offsets = [offsets_of(each) for each in masks]
     second_offsets = offsets_of(second_masks)
     scale = 0.5 * factor
 
     def kernel(*refs):
-        weights, table = refs[2], refs[3][...]
+        weights, table = refs[1], refs[2][...]
         me = own_place(tp_count)
-        targets, window, squares = refs[11:14], refs[17], refs[18]
+        targets, window, squares = refs[10:13], refs[16], refs[17]
         take_second(
-            [(0, refs[7])], 1, me, second_offsets, tp_count, stripe, table, refs[14:17]
-        )
-        take_first(refs[:2], 1, me, offsets, stripe, table, targets)
+            [(0, refs[6])], 1, me, second_offsets, tp_count, stripe, table, refs[13:16]
+        )
+        take_first([(1, refs[0])], 1, me, offsets, stripe, table, targets)
         values, highs, bases = targets
         high = whole(highs, 0)
         made = window_of(squares_of(whole(values, 0), weights[1]), mirrored(high))
@@ -327,9 +345,9 @@
         kernel,
         out_shape=kept_shapes(tp_count, stripe, block_rows) * 2
         + [square, jax.ShapeDtypeStruct((2, block_rows, block_rows), jnp.float32)],
-        in_specs=in_vmem(11),
+        in_specs=in_vmem(10),
         out_specs=in_vmem(8),
-        input_output_aliases={4: 0, 5: 1, 6: 2, 8: 3, 9: 4, 10: 5},
+        input_output_aliases={3: 0, 4: 1, 5: 2, 7: 3, 8: 4, 9: 5},
         compiler_params=pltpu.CompilerParams(vmem_limit_bytes=16 << 20),
         name="first_stage",
     )
@@ -444,8 +462,9 @@
     *kept, weights, last, table = early_stage(first_masks, second_masks, *sizes)(
         *first_parts[::2], *second_parts[::2], hamiltonian, interaction
     )
+    placed = near_stage(first_masks, *sizes)(first_parts[1], table, *kept[:3])
     known = first_stage(first_masks, second_masks, *sizes)(
-        *first_parts[1::2], weights, table, *kept[:3], second_parts[1], *kept[3:]
+        first_parts[3], weights, table, *placed, second_parts[1], *kept[3:]
     )
     result = second_stage(second_masks, *sizes)(
         second_parts[3], weights, last, table, *known[1:3], *known[6:], *known[3:6]

time: 30.6 us -> 30.8 us (level)
  transfers between devices with their start and end apart: 11 -> 11, of which waited for: 7 -> 7; matrix products, arithmetic and copies ran while one was open for 3% -> 3% of each run, Pallas kernels for 7% -> 8%
where the time goes in v6:
time: 30.8 us; the launch traced here: 30.6 us
  waiting for transfers between devices  13.1 us (43%)
  starting transfers between devices  11.6 us (38%)
  Pallas kernels  4.95 us (16%)
  local copies, waits for them, and re-layouts  0.82 us (3%)
    ppermute x11, waiting for transfers between devices, exchanged(): lax.ppermute(block, ('ta', 'tp'), [(i, i ^ masks[i % 2]) for i in range(c...  13.1 us
    ppermute x11, starting transfers between devices, exchanged(): lax.ppermute(block, ('ta', 'tp'), [(i, i ^ masks[i % 2]) for i in range(c...  11.6 us
    pallas_call x1, Pallas kernels, replicated(): second_stage(second_masks, *sizes)  2.65 us
    pallas_call x1, Pallas kernels, replicated(): early_stage(first_masks, second_masks, *sizes)  1.11 us
    pallas_call x1, Pallas kernels, replicated(): first_stage(first_masks, second_masks, *sizes)  0.91 us
    another operation x2, local copies, waits for them, and re-layouts, replicated(): first = jnp.stack([green[:, 0, 0], arriving[:, 0, 0]])  0.8 us
  transfers between devices with their start and end apart: 11, of which 7 were waited for; matrix products, arithmetic and copies ran while one was open for 3% of the time, Pallas kernels for 8%

profile of v6, /device:TPU:0, one launch (start us, length us, event | category | flops | bytes accessed | tf_op | source)
XLA Modules:
  0.0 30.6 jit_solution(9896381457129725482)
XLA Ops:
  0.0 4.1 %collective-permute-start = (f32[64,256]{1,0:T(8,128)}, f32[64,256]{1,0:T(8,128)S(1)}, u32[]{:S(2)}, u32[]{:S(2)}) collective-permute-start(f32[64,256]{1,0:T(8,128)} %bitcast.28), channel_id=1, source_target_pairs={{0,8},{1,9},{2,10},{3,11},{4,12},{5,13},{6,14},{7,15},{8,0},{9,1},... | collective-permute-start | bytes 196616 | tf_op jit(solution)/shard_map/ppermute | solution.py:438
  4.1 0.8 %slice_bitcast_fusion.2 = (f32[1,2,16,256]{3,2,1,0:T(8,128)S(1)}, f32[1,1,2,16,256]{4,3,2,1,0:T(8,128)S(1)}) fusion(f32[2,2,1,16,256]{4,3,2,1,0:T(8,128)} %param.3), kind=kLoop, calls=%fused_computation.11 | loop fusion | bytes 131072 | tf_op jit(solution)/shard_map/stack;squeeze | solution.py:441
  4.9 3.1 %collective-permute-done = f32[64,256]{1,0:T(8,128)S(1)} collective-permute-done((f32[64,256]{1,0:T(8,128)}, f32[64,256]{1,0:T(8,128)S(1)}, u32[]{:S(2)}, u32[]{:S(2)}) %collective-permute-start) | collective-permute-done | bytes 65568 | tf_op jit(solution)/shard_map/ppermute | solution.py:438
  7.9 1.8 %collective-permute-start.5 = (f32[2,2,16,256]{3,2,1,0:T(8,128)S(1)}, f32[2,2,16,256]{3,2,1,0:T(8,128)S(1)}, u32[]{:S(2)}, u32[]{:S(2)}) collective-permute-start(f32[2,2,16,256]{3,2,1,0:T(8,128)S(1)} %pad_maximum_fusion.5), channel_id=1, source_target_pairs={{0,16},{1,3},{2,18},{3,1},{4,20},{5,7},{6,22},{7,5},{8,24},{9,11},... | collective-permute-start | bytes 196616 | tf_op jit(solution)/shard_map/ppermute | solution.py:438
  9.7 0.4 %collective-permute-start.1 = (bf16[2,2,16,256]{3,2,1,0:T(8,128)(2,1)S(1)}, bf16[2,2,16,256]{3,2,1,0:T(8,128)(2,1)S(1)}, u32[]{:S(2)}, u32[]{:S(2)}) collective-permute-start(bf16[2,2,16,256]{3,2,1,0:T(8,128)(2,1)S(1)} %bitcast.25), channel_id=1, source_target_pairs={{0,16},{1,17},{2,18},{3,19},{4,20},{5,21},{6,22},{7,23},{8,24},{9,... | collective-permute-start | bytes 98312 | tf_op jit(solution)/shard_map/ppermute | solution.py:438
  10.1 2.2 %collective-permute-done.5 = f32[2,2,16,256]{3,2,1,0:T(8,128)S(1)} collective-permute-done((f32[2,2,16,256]{3,2,1,0:T(8,128)S(1)}, f32[2,2,16,256]{3,2,1,0:T(8,128)S(1)}, u32[]{:S(2)}, u32[]{:S(2)}) %collective-permute-start.5) | collective-permute-done | bytes 65568 | tf_op jit(solution)/shard_map/ppermute | solution.py:438
  12.3 1.0 %collective-permute-start.6 = (f32[4,2,16,256]{3,2,1,0:T(8,128)S(1)}, f32[4,2,16,256]{3,2,1,0:T(8,128)S(1)}, u32[]{:S(2)}, u32[]{:S(2)}) collective-permute-start(f32[4,2,16,256]{3,2,1,0:T(8,128)S(1)} %pad_maximum_fusion.2), channel_id=1, source_target_pairs={{0,4},{1,5},{2,6},{3,7},{4,0},{5,1},{6,2},{7,3},{8,12},{9,13},{10,... | collective-permute-start | bytes 393224 | tf_op jit(solution)/shard_map/ppermute | solution.py:438
  13.3 0.4 %collective-permute-done.1 = bf16[2,2,16,256]{3,2,1,0:T(8,128)(2,1)S(1)} collective-permute-done((bf16[2,2,16,256]{3,2,1,0:T(8,128)(2,1)S(1)}, bf16[2,2,16,256]{3,2,1,0:T(8,128)(2,1)S(1)}, u32[]{:S(2)}, u32[]{:S(2)}) %collective-permute-start.1) | collective-permute-done | bytes 32800 | tf_op jit(solution)/shard_map/ppermute | solution.py:438
  13.7 1.6 %collective-permute-start.2 = (bf16[2,3,2,16,256]{4,3,2,1,0:T(8,128)(2,1)S(1)}, bf16[2,3,2,16,256]{4,3,2,1,0:T(8,128)(2,1)S(1)}, u32[]{:S(2)}, u32[]{:S(2)}) collective-permute-start(bf16[2,3,2,16,256]{4,3,2,1,0:T(8,128)(2,1)S(1)} %pad_maximum_fusion.3), channel_id=1, source_target_pairs={{0,2},{1,3},{2,0},{3,1},{4,6},{5,7},{6,4},{7,5},{8,10},{9,11},{10,... | collective-permute-start | bytes 294920 | tf_op jit(solution)/shard_map/ppermute | solution.py:438
  15.3 2.0 %collective-permute-done.6 = f32[4,2,16,256]{3,2,1,0:T(8,128)S(1)} collective-permute-done((f32[4,2,16,256]{3,2,1,0:T(8,128)S(1)}, f32[4,2,16,256]{3,2,1,0:T(8,128)S(1)}, u32[]{:S(2)}, u32[]{:S(2)}) %collective-permute-start.6) | collective-permute-done | bytes 131104 | tf_op jit(solution)/shard_map/ppermute | solution.py:438
  17.3 0.0 copy-start
  17.4 0.0 copy-start.1
  17.4 1.8 %collective-permute-start.9 = (f32[8,2,16,256]{3,2,1,0:T(8,128)S(1)}, f32[8,2,16,256]{3,2,1,0:T(8,128)S(1)}, u32[]{:S(2)}, u32[]{:S(2)}) collective-permute-start(f32[8,2,16,256]{3,2,1,0:T(8,128)S(1)} %pad_maximum_fusion.refs_0_), channel_id=1, source_target_pairs={{0,2},{1,17},{2,0},{3,19},{4,6},{5,21},{6,4},{7,23},{8,10},{9,25},... | collective-permute-start | bytes 786440 | tf_op jit(solution)/shard_map/ppermute | solution.py:438
  19.2 0.0 collective-permute-done.2
  19.2 0.5 %collective-permute-start.3 = (bf16[4,3,2,16,256]{4,3,2,1,0:T(8,128)(2,1)S(1)}, bf16[4,3,2,16,256]{4,3,2,1,0:T(8,128)(2,1)S(1)}, u32[]{:S(2)}, u32[]{:S(2)}) collective-permute-start(bf16[4,3,2,16,256]{4,3,2,1,0:T(8,128)(2,1)S(1)} %pad_maximum_fusion.1.refs_2_), channel_id=1, source_target_pairs={{0,4},{1,5},{2,6},{3,7},{4,0},{5,1},{6,2},{7,3},{8,12},{9,13},{10,... | collective-permute-start | bytes 589832 | tf_op jit(solution)/shard_map/ppermute | solution.py:438
  19.7 0.0 collective-permute-start.7
  19.7 4.1 %collective-permute-done.9.refs_0_ = f32[8,2,16,256]{3,2,1,0:T(8,128)S(1)} collective-permute-done((f32[8,2,16,256]{3,2,1,0:T(8,128)S(1)}, f32[8,2,16,256]{3,2,1,0:T(8,128)S(1)}, u32[]{:S(2)}, u32[]{:S(2)}) %collective-permute-start.9) | collective-permute-done | bytes 262176 | tf_op jit(solution)/shard_map/ppermute | solution.py:438
  23.8 0.0 collective-permute-start.10
  23.8 0.5 %collective-permute-start.8 = (bf16[4,3,2,16,256]{4,3,2,1,0:T(8,128)(2,1)S(1)}, bf16[4,3,2,16,256]{4,3,2,1,0:T(8,128)(2,1)S(1)}, u32[]{:S(2)}, u32[]{:S(2)}) collective-permute-start(bf16[4,3,2,16,256]{4,3,2,1,0:T(8,128)(2,1)S(1)} %pad_maximum_fusion.1.refs_2_), channel_id=1, source_target_pairs={{0,1},{1,0},{2,3},{3,2},{4,5},{5,4},{6,7},{7,6},{8,9},{9,8},{10,11... | collective-permute-start | bytes 589832 | tf_op jit(solution)/shard_map/ppermute | solution.py:438
  24.3 0.6 %collective-permute-done.3.refs_6_ = bf16[4,3,2,16,256]{4,3,2,1,0:T(8,128)(2,1)S(1)} collective-permute-done((bf16[4,3,2,16,256]{4,3,2,1,0:T(8,128)(2,1)S(1)}, bf16[4,3,2,16,256]{4,3,2,1,0:T(8,128)(2,1)S(1)}, u32[]{:S(2)}, u32[]{:S(2)}) %collective-permute-start.3) | collective-permute-done | bytes 196640 | tf_op jit(solution)/shard_map/ppermute | solution.py:438
  24.9 0.0 collective-permute-start.4
  24.9 0.7 %collective-permute-done.8.refs_3_ = bf16[4,3,2,16,256]{4,3,2,1,0:T(8,128)(2,1)S(1)} collective-permute-done((bf16[4,3,2,16,256]{4,3,2,1,0:T(8,128)(2,1)S(1)}, bf16[4,3,2,16,256]{4,3,2,1,0:T(8,128)(2,1)S(1)}, u32[]{:S(2)}, u32[]{:S(2)}) %collective-permute-start.8) | collective-permute-done | bytes 196640 | tf_op jit(solution)/shard_map/ppermute | solution.py:438
  25.6 0.0 collective-permute-done.7.refs_1_
  25.6 0.0 copy-done
  25.6 0.0 copy-done.1
  25.6 1.1 %early_stage.1 = (f32[2,32,16,256]{3,2,1,0:T(8,128)S(1)}, bf16[2,32,16,256]{3,2,1,0:T(8,128)(2,1)S(1)}, f32[2,32,16,256]{3,2,1,0:T(8,128)S(1)}, f32[2,32,16,256]...) custom-call(f32[8,2,16,256]{3,2,1,0:T(8,128)S(1)} %pad_maximum_fusio, ...), custom_call_target="tpu_custom_call" | custom-call | tf_op jit(solution)/shard_map/early_stage/pallas_call | solution.py:462
  26.7 0.3 near_stage.1
  27.0 0.0 collective-permute-done.10.refs_0_
  27.0 0.9 %first_stage.1 = (f32[2,32,16,256]{3,2,1,0:T(8,128)S(1)}, bf16[2,32,16,256]{3,2,1,0:T(8,128)(2,1)S(1)}, f32[2,32,16,256]{3,2,1,0:T(8,128)S(1)}, f32[2,32,16,256]...) custom-call(f32[8,2,16,256]{3,2,1,0:T(8,128)S(1)} %collective-permut, ...), custom_call_target="tpu_custom_call", output_to_operand_aliasing={{0}: (3, {}), {1}: (4, {}), {2}: (5, {}), {3}: (7, {}), {4}... | custom-call | tf_op jit(solution)/shard_map/first_stage/pallas_call | solution.py:466
  28.0 0.0 collective-permute-done.4.refs_0_
  28.0 2.7 %second_stage.1 = (f32[2,2,16,256]{3,2,1,0:T(8,128)}, f32[2,32,16,256]{3,2,1,0:T(8,128)S(1)}, bf16[2,32,16,256]{3,2,1,0:T(8,128)(2,1)S(1)}, f32[2,32,16,256]{3,2,1,0:T(8,128)S(1)}) custom-call(bf16[4,3,2,16,256]{4,3,2,1,0:T(8,128)(2,1)S(1)} %collective-permute-done.4.refs_0_, ...), custom_call_target="tpu_custom_call", output_to_operand_aliasing={{1}: (8, {}), {2}: (9, {}), {3}: (10, {})} | custom-call | tf_op jit(solution)/shard_map/second_stage/pallas_call | solution.py:469
  (7 shorter events, 0.1 us)
Async XLA Ops:
  0.0 7.9 %collective-permute-start = (f32[64,256]{1,0:T(8,128)}, f32[64,256]{1,0:T(8,128)S(1)}, u32[]{:S(2)}, u32[]{:S(2)}) collective-permute-start(f32[64,256]{1,0:T(8,128)} %bitcast.28), channel_id=1, source_target_pairs={{0,8},{1,9},{2,10},{3,11},{4,12},{5,13},{6,14},{7,15},{8,0},{9,1},... | collective-permute-start | bytes 196616 | tf_op jit(solution)/shard_map/ppermute | solution.py:438
  7.9 4.3 %collective-permute-start.5 = (f32[2,2,16,256]{3,2,1,0:T(8,128)S(1)}, f32[2,2,16,256]{3,2,1,0:T(8,128)S(1)}, u32[]{:S(2)}, u32[]{:S(2)}) collective-permute-start(f32[2,2,16,256]{3,2,1,0:T(8,128)S(1)} %pad_maximum_fusion.5), channel_id=1, source_target_pairs={{0,16},{1,3},{2,18},{3,1},{4,20},{5,7},{6,22},{7,5},{8,24},{9,11},... | collective-permute-start | bytes 196616 | tf_op jit(solution)/shard_map/ppermute | solution.py:438
  9.7 4.0 %collective-permute-start.1 = (bf16[2,2,16,256]{3,2,1,0:T(8,128)(2,1)S(1)}, bf16[2,2,16,256]{3,2,1,0:T(8,128)(2,1)S(1)}, u32[]{:S(2)}, u32[]{:S(2)}) collective-permute-start(bf16[2,2,16,256]{3,2,1,0:T(8,128)(2,1)S(1)} %bitcast.25), channel_id=1, source_target_pairs={{0,16},{1,17},{2,18},{3,19},{4,20},{5,21},{6,22},{7,23},{8,24},{9,... | collective-permute-start | bytes 98312 | tf_op jit(solution)/shard_map/ppermute | solution.py:438
  12.3 5.0 %collective-permute-start.6 = (f32[4,2,16,256]{3,2,1,0:T(8,128)S(1)}, f32[4,2,16,256]{3,2,1,0:T(8,128)S(1)}, u32[]{:S(2)}, u32[]{:S(2)}) collective-permute-start(f32[4,2,16,256]{3,2,1,0:T(8,128)S(1)} %pad_maximum_fusion.2), channel_id=1, source_target_pairs={{0,4},{1,5},{2,6},{3,7},{4,0},{5,1},{6,2},{7,3},{8,12},{9,13},{10,... | collective-permute-start | bytes 393224 | tf_op jit(solution)/shard_map/ppermute | solution.py:438
  13.7 5.5 %collective-permute-start.2 = (bf16[2,3,2,16,256]{4,3,2,1,0:T(8,128)(2,1)S(1)}, bf16[2,3,2,16,256]{4,3,2,1,0:T(8,128)(2,1)S(1)}, u32[]{:S(2)}, u32[]{:S(2)}) collective-permute-start(bf16[2,3,2,16,256]{4,3,2,1,0:T(8,128)(2,1)S(1)} %pad_maximum_fusion.3), channel_id=1, source_target_pairs={{0,2},{1,3},{2,0},{3,1},{4,6},{5,7},{6,4},{7,5},{8,10},{9,11},{10,... | collective-permute-start | bytes 294920 | tf_op jit(solution)/shard_map/ppermute | solution.py:438
  17.3 8.3 %copy-start = (f32[32,32]{1,0:T(8,128)S(1)}, f32[32,32]{1,0:T(8,128)}, u32[]{:S(2)}) copy-start(f32[32,32]{1,0:T(8,128)} %refs_4_.1) | copy-start | bytes 12292
  17.4 8.3 %copy-start.1 = (f32[32,32]{1,0:T(8,128)S(1)}, f32[32,32]{1,0:T(8,128)}, u32[]{:S(2)}) copy-start(f32[32,32]{1,0:T(8,128)} %refs_5_.1) | copy-start | bytes 12292
  17.4 6.4 %collective-permute-start.9 = (f32[8,2,16,256]{3,2,1,0:T(8,128)S(1)}, f32[8,2,16,256]{3,2,1,0:T(8,128)S(1)}, u32[]{:S(2)}, u32[]{:S(2)}) collective-permute-start(f32[8,2,16,256]{3,2,1,0:T(8,128)S(1)} %pad_maximum_fusion.refs_0_), channel_id=1, source_target_pairs={{0,2},{1,17},{2,0},{3,19},{4,6},{5,21},{6,4},{7,23},{8,10},{9,25},... | collective-permute-start | bytes 786440 | tf_op jit(solution)/shard_map/ppermute | solution.py:438
  19.2 5.7 %collective-permute-start.3 = (bf16[4,3,2,16,256]{4,3,2,1,0:T(8,128)(2,1)S(1)}, bf16[4,3,2,16,256]{4,3,2,1,0:T(8,128)(2,1)S(1)}, u32[]{:S(2)}, u32[]{:S(2)}) collective-permute-start(bf16[4,3,2,16,256]{4,3,2,1,0:T(8,128)(2,1)S(1)} %pad_maximum_fusion.1.refs_2_), channel_id=1, source_target_pairs={{0,4},{1,5},{2,6},{3,7},{4,0},{5,1},{6,2},{7,3},{8,12},{9,13},{10,... | collective-permute-start | bytes 589832 | tf_op jit(solution)/shard_map/ppermute | solution.py:438
  19.7 5.9 %collective-permute-start.7 = (f32[8,2,16,256]{3,2,1,0:T(8,128)S(1)}, f32[8,2,16,256]{3,2,1,0:T(8,128)S(1)}, u32[]{:S(2)}, u32[]{:S(2)}) collective-permute-start(f32[8,2,16,256]{3,2,1,0:T(8,128)S(1)} %pad_maximum_fusion.refs_0_), channel_id=1, source_target_pairs={{0,1},{1,0},{2,3},{3,2},{4,5},{5,4},{6,7},{7,6},{8,9},{9,8},{10,11... | collective-permute-start | bytes 786440 | tf_op jit(solution)/shard_map/ppermute | solution.py:438
  23.8 3.2 %collective-permute-start.10 = (f32[8,2,16,256]{3,2,1,0:T(8,128)S(1)}, f32[8,2,16,256]{3,2,1,0:T(8,128)S(1)}, u32[]{:S(2)}, u32[]{:S(2)}) collective-permute-start(f32[8,2,16,256]{3,2,1,0:T(8,128)S(1)} %collective-permute-done.9.refs_0_), channel_id=1, source_target_pairs={{0,1},{1,0},{2,3},{3,2},{4,5},{5,4},{6,7},{7,6},{8,9},{9,8},{10,11... | collective-permute-start | bytes 786440 | tf_op jit(solution)/shard_map/ppermute | solution.py:438
  23.8 1.8 %collective-permute-start.8 = (bf16[4,3,2,16,256]{4,3,2,1,0:T(8,128)(2,1)S(1)}, bf16[4,3,2,16,256]{4,3,2,1,0:T(8,128)(2,1)S(1)}, u32[]{:S(2)}, u32[]{:S(2)}) collective-permute-start(bf16[4,3,2,16,256]{4,3,2,1,0:T(8,128)(2,1)S(1)} %pad_maximum_fusion.1.refs_2_), channel_id=1, source_target_pairs={{0,1},{1,0},{2,3},{3,2},{4,5},{5,4},{6,7},{7,6},{8,9},{9,8},{10,11... | collective-permute-start | bytes 589832 | tf_op jit(solution)/shard_map/ppermute | solution.py:438
  24.9 3.0 %collective-permute-start.4 = (bf16[4,3,2,16,256]{4,3,2,1,0:T(8,128)(2,1)S(1)}, bf16[4,3,2,16,256]{4,3,2,1,0:T(8,128)(2,1)S(1)}, u32[]{:S(2)}, u32[]{:S(2)}) collective-permute-start(bf16[4,3,2,16,256]{4,3,2,1,0:T(8,128)(2,1)S(1)} %collective-permute-done.3.refs_6_), channel_id=1, source_target_pairs={{0,1},{1,0},{2,3},{3,2},{4,5},{5,4},{6,7},{7,6},{8,9},{9,8},{10,11... | collective-permute-start | bytes 589832 | tf_op jit(solution)/shard_map/ppermute | solution.py:438
